TPU v7x, 256 devices: a whole 4x4x8 slice. The times are simulated.
256 devices in a mesh: node: 64 (over z, x, core), edge: 4 (over y).
Axes of the slice: x: 4, y: 4, z: 8, core: 2. Of those that a mesh axis runs over, the one named last changes fastest.
Arguments:
- teleport: float32 [131072, 128], P(('node', 'edge')), may hold values from -6 to 6
- cotangent: float32 [131072, 128], P(('node', 'edge')), may hold values from -6 to 6
- fetch_table: int32 [64, 128], replicated, may hold values from -1 to 7, as said below
- block_row: int32 [64, 192], P('node'), may hold values from 0 to 7
- block_slot: int32 [64, 192], P('node'), may hold values from 0 to 127, as said below
- values: bfloat16 [64, 192, 256, 256], P('node', None, 'edge'), may hold values from -0.078125 to 0.078125
Outputs:
- propagated: float32 [131072, 128], P(('node', 'edge'))
- teleport_grad: float32 [131072, 128], P(('node', 'edge'))
Inputs may be any that keep to these rules, and one draw needn't show every extreme that they name: `fetch_table`: entry n, o * 2 + k names a node block index j of owner group o that group n reads in slot k, or is -1 for an empty slot. Within the 2 slots of one owner the live ones come first and name distinct blocks. One owner group has all 2 slots live in every row. `block_slot`: every entry names a live slot of the group's row of fetch_table, and every live slot of that row is named by at least one adjacency block of the group.
All inputs are finite; a program needn't handle non-finite values.
Results may differ from a plain program's by a relative error of at most 0.004.
Values may be sent and summed in bfloat16 or wider, within the bound.
A program may use at most 128 MiB of HBM per device.

v0:
```python
import functools

import jax
import jax.numpy as jnp
from jax import lax
from jax.experimental import pallas as pl
from jax.experimental.pallas import tpu as pltpu
from jax.sharding import Mesh
from jax.sharding import PartitionSpec as P

MESH = pl.DeviceIdType.MESH

CAP = 2
STEPS = 2
Z_SIZE = 8
X_SIZE = 4
CORE_SIZE = 2
GROUP = 4


def fetch_all(members_ref, v_hbm, vbuf, sems):
    last = v_hbm.shape[0] - 1

    def issue(i, carry):
        b = jnp.minimum(members_ref[i], last)
        pltpu.make_async_copy(v_hbm.at[b], vbuf.at[i], sems.at[i]).start()
        return carry

    lax.fori_loop(0, vbuf.shape[0], issue, 0)


def wait_group(v_hbm, vbuf, sems, g):
    for m in range(GROUP):
        pltpu.make_async_copy(v_hbm.at[0], vbuf.at[g * GROUP + m], sems.at[g * GROUP + m]).wait()


def forward_kernel(rows_ref, members_ref, slots_ref, v_hbm, x_ref, out_ref, vbuf, sems):
    group_count = rows_ref.shape[0]
    block_count = v_hbm.shape[0]
    quarters, _, quarter, hidden = out_ref.shape
    fetch_all(members_ref, v_hbm, vbuf, sems)
    out_ref[...] = jnp.zeros_like(out_ref)

    def body(g, carry):
        wait_group(v_hbm, vbuf, sems, g)

        j = rows_ref[g]
        pieces = []
        for m in range(GROUP):
            valid = members_ref[g * GROUP + m] < block_count
            piece = x_ref[slots_ref[g * GROUP + m]]
            pieces.append(jnp.where(valid, piece, jnp.zeros_like(piece)))
        sources = jnp.concatenate(pieces, axis=0)
        weights = vbuf[pl.ds(g * GROUP, GROUP)].reshape(GROUP * quarter, vbuf.shape[-1])
        product = lax.dot_general(
            weights, sources, (((0,), (0,)), ((), ())), preferred_element_type=jnp.float32
        )
        out_ref[:, j] += product.reshape(quarters, quarter, hidden)
        return carry

    lax.fori_loop(0, group_count, body, 0)


def backward_kernel(rows_ref, members_ref, slots_ref, v_hbm, a_ref, out_ref, vbuf, sems):
    group_count = rows_ref.shape[0]
    block_count = v_hbm.shape[0]
    quarters, _, quarter, hidden = a_ref.shape
    fetch_all(members_ref, v_hbm, vbuf, sems)
    out_ref[...] = jnp.zeros_like(out_ref)

    def body(g, carry):
        wait_group(v_hbm, vbuf, sems, g)

        j = rows_ref[g]
        sources = a_ref[:, j].reshape(quarters * quarter, hidden)
        weights = vbuf[pl.ds(g * GROUP, GROUP)].reshape(GROUP * quarter, vbuf.shape[-1])
        product = jnp.dot(weights, sources, preferred_element_type=jnp.float32)
        for m in range(GROUP):
            s = slots_ref[g * GROUP + m]

            @pl.when(members_ref[g * GROUP + m] < block_count)
            def _():
                out_ref[s] += product[m * quarter:(m + 1) * quarter]

        return carry

    lax.fori_loop(0, group_count, body, 0)


def combine_kernel(want_ref, arrived_ref, out_ref):
    out_ref[...] = jnp.zeros_like(out_ref)
    lines = out_ref.shape[0]

    def body(q, carry):
        j = want_ref[q]

        @pl.when(j >= 0)
        def _():
            out_ref[q // CAP % lines, j] += arrived_ref[q]

        return carry

    lax.fori_loop(0, arrived_ref.shape[0], body, 0)


def edge_exchange_kernel(reduce, x_ref, out_ref, held, send_sem, recv_sem):
    count = held.shape[0]
    me = lax.axis_index("edge")
    barrier = pltpu.get_barrier_semaphore()
    for d in range(1, count):
        pl.semaphore_signal(
            barrier, inc=1, device_id={"edge": lax.rem(me + d, count)}, device_id_type=MESH
        )
    pl.semaphore_wait(barrier, count - 1)
    copies = []
    for d in range(1, count):
        peer = lax.rem(me + d, count)
        copy = pltpu.make_async_remote_copy(
            src_ref=x_ref.at[peer] if reduce else x_ref.at[0],
            dst_ref=held.at[me],
            send_sem=send_sem.at[d],
            recv_sem=recv_sem.at[d],
            device_id={"edge": peer},
            device_id_type=MESH,
        )
        copy.start()
        copies.append(copy)
    held[me] = x_ref[me] if reduce else x_ref[0]
    for copy in copies:
        copy.wait()
    if reduce:
        total = held[0]
        for q in range(1, count):
            total = total + held[q]
        out_ref[...] = total
    else:
        out_ref[...] = held[...]


def edge_exchange(chunks, count, reduce, collective_id):
    piece = chunks.shape[1:]
    out_shape = piece if reduce else (count,) + piece
    return pl.pallas_call(
        functools.partial(edge_exchange_kernel, reduce),
        out_shape=jax.ShapeDtypeStruct(out_shape, chunks.dtype),
        in_specs=[pl.BlockSpec(memory_space=pltpu.VMEM)],
        out_specs=pl.BlockSpec(memory_space=pltpu.VMEM),
        scratch_shapes=[
            pltpu.VMEM((count,) + piece, chunks.dtype),
            pltpu.SemaphoreType.DMA((count,)),
            pltpu.SemaphoreType.DMA((count,)),
        ],
        compiler_params=pltpu.CompilerParams(collective_id=collective_id, has_side_effects=True),
    )(chunks)


def block_apply(kernel, rows, members, slots, weights, dense, out_shape):
    block_count, quarter, width = weights.shape
    return pl.pallas_call(
        kernel,
        out_shape=jax.ShapeDtypeStruct(out_shape, jnp.float32),
        grid_spec=pltpu.PrefetchScalarGridSpec(
            num_scalar_prefetch=3,
            grid=(1,),
            in_specs=[
                pl.BlockSpec(memory_space=pl.ANY),
                pl.BlockSpec(dense.shape, lambda i, *_: (0,) * dense.ndim),
            ],
            out_specs=pl.BlockSpec(out_shape, lambda i, *_: (0,) * len(out_shape)),
            scratch_shapes=[
                pltpu.VMEM((members.shape[0], quarter, width), weights.dtype),
                pltpu.SemaphoreType.DMA((members.shape[0],)),
            ],
        ),
    )(rows, members, slots, weights, dense)


def combine_apply(wanted, arrived, blocks_dev):
    slot_total, quarter, hidden = arrived.shape
    lines = slot_total // (CAP * X_SIZE * CORE_SIZE)
    return pl.pallas_call(
        combine_kernel,
        out_shape=jax.ShapeDtypeStruct((lines, blocks_dev, quarter, hidden), jnp.float32),
        grid_spec=pltpu.PrefetchScalarGridSpec(
            num_scalar_prefetch=1,
            grid=(1,),
            in_specs=[pl.BlockSpec(arrived.shape, lambda i, w: (0, 0, 0))],
            out_specs=pl.BlockSpec(
                (lines, blocks_dev, quarter, hidden), lambda i, w: (0, 0, 0, 0)
            ),
        ),
    )(wanted, arrived)


def grouping(row_ids, blocks_dev):
    block_count = row_ids.shape[0]
    group_count = block_count // GROUP + blocks_dev
    hot = (row_ids[:, None] == jnp.arange(blocks_dev, dtype=jnp.int32)[None, :]).astype(jnp.float32)
    block_range = jnp.arange(block_count, dtype=jnp.int32)
    before = (block_range[None, :] < block_range[:, None]).astype(jnp.float32)
    rank = jnp.sum(
        jnp.dot(before, hot, precision=lax.Precision.HIGHEST) * hot, axis=1
    ).astype(jnp.int32)
    counts = jnp.sum(hot, axis=0).astype(jnp.int32)
    groups_per_row = (counts + GROUP - 1) // GROUP
    group_end = jnp.cumsum(groups_per_row)
    group_start = group_end - groups_per_row
    position = jnp.sum(hot * group_start[None, :].astype(jnp.float32), axis=1).astype(jnp.int32) * GROUP + rank
    member = jnp.full((group_count * GROUP,), block_count, jnp.int32).at[position].set(block_range)
    group_range = jnp.arange(group_count, dtype=jnp.int32)
    group_row = jnp.minimum(
        jnp.sum((group_range[:, None] >= group_end[None, :]).astype(jnp.int32), axis=1), blocks_dev - 1
    ).astype(jnp.int32)
    return member, group_row


def per_device(teleport, cotangent, fetch_table, block_row, block_slot, values):
    row_count, hidden = teleport.shape
    quarter = values.shape[2]
    blocks_dev = row_count // quarter
    slot_total = fetch_table.shape[1]
    quarters = lax.axis_size("edge")
    row_peers = X_SIZE * CORE_SIZE
    z_me = lax.axis_index("z")
    x_me = lax.axis_index("x")
    c_me = lax.axis_index("c")
    weights = values[0]
    row_ids = block_row[0]
    slot_ids = block_slot[0]

    owner = slot_ids // CAP
    placed_slots = (
        ((owner // CORE_SIZE % X_SIZE * CORE_SIZE + owner % CORE_SIZE) * Z_SIZE + owner // (CORE_SIZE * X_SIZE))
        * CAP
        + slot_ids % CAP
    ).astype(jnp.int32)

    peer_range = jnp.arange(row_peers, dtype=jnp.int32)
    z_range = jnp.arange(Z_SIZE, dtype=jnp.int32)
    peer_groups = (z_me * X_SIZE + peer_range // CORE_SIZE) * CORE_SIZE + peer_range % CORE_SIZE
    line_owners = (z_range * X_SIZE + x_me) * CORE_SIZE + c_me
    table_cols = line_owners[:, None] * CAP + jnp.arange(CAP, dtype=jnp.int32)[None, :]
    wanted = fetch_table[peer_groups[:, None, None], table_cols[None, :, :]]
    send_index = (z_range[None, :, None] * blocks_dev + jnp.maximum(wanted, 0)).reshape(-1)

    member, group_row = grouping(row_ids, blocks_dev)
    member_slot = jnp.take(placed_slots, member, axis=0, mode="clip")
    wanted_flat = wanted.reshape(-1)

    current = teleport
    for step_index in range(STEPS):
        rounded = current.astype(jnp.bfloat16).reshape(blocks_dev, quarter, hidden)
        line_blocks = lax.all_gather(rounded, "z", axis=0, tiled=True)
        outgoing = jnp.take(line_blocks, send_index, axis=0)
        received = lax.all_to_all(
            outgoing, ("x", "c"), split_axis=0, concat_axis=0, tiled=True
        )
        partial = block_apply(
            forward_kernel, group_row, member, member_slot, weights, received,
            (quarters, blocks_dev, quarter, hidden),
        )
        summed = edge_exchange(partial, quarters, True, 1)
        current = 0.9 * summed.reshape(row_count, hidden) + 0.1 * teleport

    adjoint = cotangent
    gradient = 0.1 * cotangent
    for step_index in range(STEPS):
        rounded = adjoint.astype(jnp.bfloat16).reshape(1, blocks_dev, quarter, hidden)
        whole_rows = edge_exchange(rounded, quarters, False, 2)
        slot_sums = block_apply(
            backward_kernel, group_row, member, member_slot, weights, whole_rows,
            (slot_total, quarter, hidden),
        )
        arrived = lax.all_to_all(
            slot_sums, ("x", "c"), split_axis=0, concat_axis=0, tiled=True
        )
        dense = combine_apply(wanted_flat, arrived, blocks_dev)
        owned = lax.psum_scatter(dense, "z", scatter_dimension=0, tiled=True)
        adjoint = 0.9 * owned.reshape(row_count, hidden)
        factor = 0.1 if step_index + 1 < STEPS else 1.0
        gradient = gradient + factor * adjoint
    return (current, gradient)


def solution(mesh):
    devices = mesh.devices.reshape(Z_SIZE, X_SIZE, CORE_SIZE, mesh.shape["edge"])
    fine = Mesh(devices, ("z", "x", "c", "edge"))
    node = ("z", "x", "c")
    placed = (
        P((*node, "edge"), None),
        P((*node, "edge"), None),
        P(),
        P(node, None),
        P(node, None),
        P(node, None, "edge", None),
    )
    return jax.shard_map(
        per_device,
        mesh=fine,
        in_specs=placed,
        out_specs=(P((*node, "edge"), None), P((*node, "edge"), None)),
        check_vma=False,
    )
```

profile of v0, /device:TPU:1, one launch (start us, length us, event | category | flops | bytes accessed | tf_op | source)
XLA Modules:
  0.0 346.2 jit_solution(6421224276595692705)
XLA Ops:
  7.2 0.0 copy-start
  7.2 0.8 convert_reduce_fusion
  8.0 0.9 fusion
  8.9 0.2 reduce-window.7
  9.1 0.8 select_reduce_fusion
  9.9 1.2 scatter_custom_fusion.members_ref
  11.1 0.0 copy-start.5
  11.2 0.7 fusion.7
  11.9 0.1 convert_reduce_fusion.1
  12.0 0.5 broadcast_minimum_fusion.rows_ref
  12.4 1.6 convert_element_type.73
  14.1 11.7 %shard_map.81.a_ref = bf16[4,8,64,128]{3,2,1,0:T(8,128)(2,1)} custom-call(bf16[1,8,64,128]{3,2,1,0:T(8,128)(2,1)} %bitcast.38), custom_call_target="tpu_custom_call" | custom-call | tf_op jit(solution)/shard_map/pallas_call | solution.py:143
  25.8 2.5 gather_fusion
  28.3 0.0 copy-done.5
  28.3 19.1 %shard_map.82 = f32[128,64,128]{2,1,0:T(8,128)} custom-call(s32[56]{0:T(128)} %broadcast_minimum_fusion.rows_ref, s32[224]{0:T(256)} %copy-done.5, s32[224]{0:T(256)} %gather_fusion, bf16[192,64,256]{2,1,0:T(8,128)(2,1)} %bitcast.34, bf16[4,8,64,128]{3,2,1,0:T(8,128)(2,1)} %shard_map.81.a_ref), custom_call_target="tpu_custom_call" | custom-call | tf_op jit(solution)/shard_map/pallas_call | solution.py:159
  47.3 0.0 copy-start.2
  47.3 6.6 %all-to-all-start.2 = ((f32[128,64,128]{2,1,0:T(8,128)}), f32[128,64,128]{2,1,0:T(8,128)}, u32[]{:S(2)}, u32[]{:S(2)}) async-start(f32[128,64,128]{2,1,0:T(8,128)} %shard_map.82), calls=%async_computation.2 | async-start | bytes 8388608 | tf_op jit(solution)/shard_map/all_to_all | solution.py:274
  54.0 0.0 all-gather.3.cloned.1.call-start
  54.0 0.7 convert_element_type.71
  54.7 0.0 all-gather.3.cloned.1.call-update
  54.7 0.0 reduce-scatter.3.cloned.1.call-start
  54.8 0.1 fusion.3
  54.9 0.1 broadcast_or_fusion
  54.9 0.1 reshape.235
  55.1 1.7 gather_fusion.1
  56.8 46.1 %all-to-all-done.2.arrived_ref = f32[128,64,128]{2,1,0:T(8,128)} async-done(((f32[128,64,128]{2,1,0:T(8,128)}), f32[128,64,128]{2,1,0:T(8,128)}, u32[]{:S(2)}, u32[]{:S(2)}) %all-to-all-start.2) | async-done | bytes 4194336 | tf_op jit(solution)/shard_map/all_to_all | solution.py:274
  102.9 7.2 %shard_map.83 = f32[8,8,64,128]{3,2,1,0:T(8,128)} custom-call(s32[128]{0:T(128)} %gather_fusion.1, f32[128,64,128]{2,1,0:T(8,128)} %all-to-all-done.2.arrived_ref), custom_call_target="tpu_custom_call" | custom-call | tf_op jit(solution)/shard_map/pallas_call | solution.py:181
  110.2 0.0 reduce-scatter.3.cloned.1.call-update
  110.2 0.1 add.205
  110.3 0.1 add.206
  110.4 0.3 copy-done.3
  110.7 0.0 all-gather.3.cloned.1.call-done
  110.8 2.2 gather_fusion.2
  113.0 1.6 broadcast_select_fusion
  114.5 4.3 %all-to-all-start = ((bf16[128,64,128]{2,1,0:T(8,128)(2,1)}), bf16[128,64,128]{2,1,0:T(8,128)(2,1)S(1)}, u32[]{:S(2)}, u32[]{:S(2)}) async-start(bf16[128,64,128]{2,1,0:T(8,128)(2,1)} %broadcast_select_fusion), calls=%async_computation | async-start | bytes 4194304 | tf_op jit(solution)/shard_map/all_to_all | solution.py:255
  118.8 29.3 %reduce-scatter.3.cloned.1.call-done = f32[1,8,64,128]{3,2,1,0:T(8,128)} async-done(((f32[8,8,64,128]{3,2,1,0:T(8,128)}), f32[1,8,64,128]{3,2,1,0:T(8,128)}) %reduce-scatter.3.cloned.1.call-update) | async-done | bytes 262160 | tf_op jit(solution)/shard_map/reduce_scatter | solution.py:278
  148.1 1.7 broadcast_multiply_fusion.1
  149.7 9.2 %shard_map.84.a_ref = bf16[4,8,64,128]{3,2,1,0:T(8,128)(2,1)} custom-call(bf16[1,8,64,128]{3,2,1,0:T(8,128)(2,1)} %get-tuple-element.6.x_ref), custom_call_target="tpu_custom_call" | custom-call | tf_op jit(solution)/shard_map/pallas_call | solution.py:143
  158.9 19.0 %shard_map.85 = f32[128,64,128]{2,1,0:T(8,128)} custom-call(s32[56]{0:T(128)} %broadcast_minimum_fusion.rows_ref, s32[224]{0:T(256)} %copy-done.5, s32[224]{0:T(256)} %gather_fusion, bf16[192,64,256]{2,1,0:T(8,128)(2,1)} %bitcast.35, bf16[4,8,64,128]{3,2,1,0:T(8,128)(2,1)} %shard_map.84.a_ref), custom_call_target="tpu_custom_call" | custom-call | tf_op jit(solution)/shard_map/pallas_call | solution.py:159
  178.0 0.0 all-to-all-done.x_ref
  178.0 1.3 copy-done.1
  179.3 10.4 %all-to-all-start.3 = ((f32[128,64,128]{2,1,0:T(8,128)}), f32[128,64,128]{2,1,0:T(8,128)}, u32[]{:S(2)}, u32[]{:S(2)}) async-start(f32[128,64,128]{2,1,0:T(8,128)} %shard_map.85), calls=%async_computation.4 | async-start | bytes 8388608 | tf_op jit(solution)/shard_map/all_to_all | solution.py:274
  189.8 0.0 all-gather.5.cloned.1.call-start
  189.8 19.8 %shard_map.77.x_ref = f32[4,8,64,128]{3,2,1,0:T(8,128)} custom-call(s32[56]{0:T(128)} %broadcast_minimum_fusion.rows_ref, s32[224]{0:T(256)} %copy-done.5, s32[224]{0:T(256)} %gather_fusion, bf16[192,64,256]{2,1,0:T(8,128)(2,1)} %bitcast.36, bf16[128,64,128]{2,1,0:T(8,128)(2,1)} %copy-done.1), custom_call_target="tpu_custom_call" | custom-call | tf_op jit(solution)/shard_map/pallas_call | solution.py:159
  209.6 17.1 %shard_map.78 = f32[8,64,128]{2,1,0:T(8,128)} custom-call(f32[4,8,64,128]{3,2,1,0:T(8,128)} %shard_map.77.x_ref), custom_call_target="tpu_custom_call" | custom-call | tf_op jit(solution)/shard_map/pallas_call | solution.py:143
  226.7 1.0 broadcast_multiply_fusion.3
  227.6 0.7 fusion.1
  228.3 0.0 all-gather.5.cloned.1.call-update
  228.4 0.0 reduce-scatter.5.cloned.1.call-start
  228.4 10.3 %all-to-all-done.3.arrived_ref = f32[128,64,128]{2,1,0:T(8,128)} async-done(((f32[128,64,128]{2,1,0:T(8,128)}), f32[128,64,128]{2,1,0:T(8,128)}, u32[]{:S(2)}, u32[]{:S(2)}) %all-to-all-start.3) | async-done | bytes 4194336 | tf_op jit(solution)/shard_map/all_to_all | solution.py:274
  238.7 7.2 %shard_map.86 = f32[8,8,64,128]{3,2,1,0:T(8,128)} custom-call(s32[128]{0:T(128)} %gather_fusion.1, f32[128,64,128]{2,1,0:T(8,128)} %all-to-all-done.3.arrived_ref), custom_call_target="tpu_custom_call" | custom-call | tf_op jit(solution)/shard_map/pallas_call | solution.py:181
  245.9 0.0 reduce-scatter.5.cloned.1.call-update
  246.0 14.8 %all-gather.5.cloned.1.call-done = bf16[64,64,128]{2,1,0:T(8,128)(2,1)} async-done(((bf16[8,64,128]{2,1,0:T(8,128)(2,1)}), bf16[64,64,128]{2,1,0:T(8,128)(2,1)}) %all-gather.5.cloned.1.call-update) | async-done | bytes 1048592 | tf_op jit(solution)/shard_map/all_gather | solution.py:253
  260.7 2.2 gather_fusion.3
  262.9 0.3 broadcast_select_fusion.1
  263.2 36.4 %all_to_all.20.x_ref = bf16[128,64,128]{2,1,0:T(8,128)(2,1)} all-to-all(bf16[128,64,128]{2,1,0:T(8,128)(2,1)S(1)} %broadcast_select_fusion.1), channel_id=1, replica_groups=mesh['z'=8,'x'=4,'c'=2,'edge'=4] {'x','c'}, dimensions={0} | all-to-all | bytes 4194304 | tf_op jit(solution)/shard_map/all_to_all | solution.py:255
  299.6 19.8 %shard_map.79.x_ref = f32[4,8,64,128]{3,2,1,0:T(8,128)} custom-call(s32[56]{0:T(128)} %broadcast_minimum_fusion.rows_ref, s32[224]{0:T(256)} %copy-done.5, s32[224]{0:T(256)} %gather_fusion, bf16[192,64,256]{2,1,0:T(8,128)(2,1)} %bitcast.37, bf16[128,64,128]{2,1,0:T(8,128)(2,1)} %all_to_all.20.x_ref), custom_call_target="tpu_custom_call" | custom-call | tf_op jit(solution)/shard_map/pallas_call | solution.py:159
  319.4 0.0 copy-start.4
  319.4 16.8 %shard_map.80 = f32[8,64,128]{2,1,0:T(8,128)} custom-call(f32[4,8,64,128]{3,2,1,0:T(8,128)} %shard_map.79.x_ref), custom_call_target="tpu_custom_call" | custom-call | tf_op jit(solution)/shard_map/pallas_call | solution.py:143
  336.2 1.0 broadcast_multiply_fusion.2
  337.2 0.7 bitcast_add_fusion.2
  337.9 1.0 broadcast_multiply_fusion
  338.9 0.0 copy-done.4
  338.9 0.7 bitcast_add_fusion
  (16 shorter events, 0.1 us)
Async XLA Ops:
  7.2 47.9 %copy-start = (s32[64,128]{1,0:T(8,128)S(1)}, s32[64,128]{1,0:T(8,128)}, u32[]{:S(2)}) copy-start(s32[64,128]{1,0:T(8,128)} %param.10) | copy-start | bytes 98308
  11.1 17.1 %copy-start.5 = (s32[224]{0:T(256)}, s32[224]{0:T(256)S(1)}, u32[]{:S(2)}) copy-start(s32[224]{0:T(256)S(1)} %scatter_custom_fusion.members_ref) | copy-start | bytes 2692
  47.3 6.7 %copy-start.2 = (f32[512,128]{1,0:T(8,128)S(1)}, f32[512,128]{1,0:T(8,128)}, u32[]{:S(2)}) copy-start(f32[512,128]{1,0:T(8,128)} %param.8) | copy-start | bytes 786436
  47.3 55.6 %all-to-all-start.2 = ((f32[128,64,128]{2,1,0:T(8,128)}), f32[128,64,128]{2,1,0:T(8,128)}, u32[]{:S(2)}, u32[]{:S(2)}) async-start(f32[128,64,128]{2,1,0:T(8,128)} %shard_map.82), calls=%async_computation.2 | async-start | bytes 8388608 | tf_op jit(solution)/shard_map/all_to_all | solution.py:274
  54.0 56.8 %all-gather.3.cloned.1.call-start = ((), (), s32[]{:S(2)}) async-start(), calls=%async_computation.6 | async-start | bytes 1179648 | tf_op jit(solution)/shard_map/all_gather | solution.py:253
  54.7 93.4 %reduce-scatter.3.cloned.1.call-start = ((), (), s32[]{:S(2)}) async-start(), calls=%async_computation.8 | async-start | bytes 2359296 | tf_op jit(solution)/shard_map/reduce_scatter | solution.py:278
  110.1 0.6 copy-start.3
  114.5 63.4 %all-to-all-start = ((bf16[128,64,128]{2,1,0:T(8,128)(2,1)}), bf16[128,64,128]{2,1,0:T(8,128)(2,1)S(1)}, u32[]{:S(2)}, u32[]{:S(2)}) async-start(bf16[128,64,128]{2,1,0:T(8,128)(2,1)} %broadcast_select_fusion), calls=%async_computation | async-start | bytes 4194304 | tf_op jit(solution)/shard_map/all_to_all | solution.py:255
  178.0 1.4 copy-start.1
  179.3 59.4 %all-to-all-start.3 = ((f32[128,64,128]{2,1,0:T(8,128)}), f32[128,64,128]{2,1,0:T(8,128)}, u32[]{:S(2)}, u32[]{:S(2)}) async-start(f32[128,64,128]{2,1,0:T(8,128)} %shard_map.85), calls=%async_computation.4 | async-start | bytes 8388608 | tf_op jit(solution)/shard_map/all_to_all | solution.py:274
  189.8 71.0 %all-gather.5.cloned.1.call-start = ((), (), s32[]{:S(2)}) async-start(), calls=%async_computation.7 | async-start | bytes 1179648 | tf_op jit(solution)/shard_map/all_gather | solution.py:253
  228.4 109.6 %reduce-scatter.5.cloned.1.call-start = ((), (), s32[]{:S(2)}) async-start(), calls=%async_computation.9 | async-start | bytes 2359296 | tf_op jit(solution)/shard_map/reduce_scatter | solution.py:278
  319.4 19.5 %copy-start.4 = (f32[512,128]{1,0:T(8,128)S(1)}, f32[512,128]{1,0:T(8,128)}, u32[]{:S(2)}) copy-start(f32[512,128]{1,0:T(8,128)} %param.9) | copy-start | bytes 786436
Sparse Core Ops, SparseCore 0:
  57.2 36.7 all-gather.2
  110.3 37.7 reduce-scatter.2
  228.5 32.2 all-gather.4
  263.1 41.7 reduce-scatter.4
where the time goes:
time: 347 us; the launch traced here: 346 us
  Pallas kernels  147 us (42%)
  waiting for transfers between devices  101 us (29%)
  blocking collectives  36.4 us (10%)
  starting transfers between devices  21.4 us (6%)
  other arithmetic  14.2 us (4%)
  between operations  14 us (4%)
  local copies, waits for them, and re-layouts  11.8 us (3%)
    pallas_call x4, Pallas kernels, block_apply(): pl.pallas_call(kernel, out_shape=jax.ShapeDtypeStruct(out_shape, jnp.floa...  77.7 us
    all_to_all x2, waiting for transfers between devices, per_device(): lax.all_to_all(slot_sums, ('x', 'c'), split_axis=0, concat_axis=0, tiled=...  56.4 us
    pallas_call x4, Pallas kernels, edge_exchange(): pl.pallas_call(functools.partial(edge_exchange_kernel, reduce), out_shape...  54.7 us
    all_to_all x1, blocking collectives, per_device(): lax.all_to_all(outgoing, ('x', 'c'), split_axis=0, concat_axis=0, tiled=T...  36.4 us
    reduce_scatter x2, waiting for transfers between devices, per_device(): owned = lax.psum_scatter(dense, 'z', scatter_dimension=0, tiled=True)  29.3 us
    all_to_all x2, starting transfers between devices, per_device(): lax.all_to_all(slot_sums, ('x', 'c'), split_axis=0, concat_axis=0, tiled=...  17.1 us
    all_gather x2, waiting for transfers between devices, per_device(): line_blocks = lax.all_gather(rounded, 'z', axis=0, tiled=True)  14.8 us
    pallas_call x2, Pallas kernels, combine_apply(): pl.pallas_call(combine_kernel, out_shape=jax.ShapeDtypeStruct((lines, blo...  14.5 us
  transfers between devices with their start and end apart: 7, of which 4 were waited for; matrix products, arithmetic and copies ran while one was open for 4% of the time, Pallas kernels for 34%

commit v1 on v0

--- a/solution.py
+++ b/solution.py
@@ -241,22 +241,24 @@
     line_owners = (z_range * X_SIZE + x_me) * CORE_SIZE + c_me
     table_cols = line_owners[:, None] * CAP + jnp.arange(CAP, dtype=jnp.int32)[None, :]
     wanted = fetch_table[peer_groups[:, None, None], table_cols[None, :, :]]
-    send_index = (z_range[None, :, None] * blocks_dev + jnp.maximum(wanted, 0)).reshape(-1)
+    me = (z_me * X_SIZE + x_me) * CORE_SIZE + c_me
+    own_requests = lax.dynamic_slice_in_dim(fetch_table, me * CAP, CAP, 1).reshape(-1)
+    send_index = jnp.maximum(own_requests, 0)
 
     member, group_row = grouping(row_ids, blocks_dev)
     member_slot = jnp.take(placed_slots, member, axis=0, mode="clip")
+    reader_slot = jnp.take(slot_ids, member, axis=0, mode="clip")
     wanted_flat = wanted.reshape(-1)
 
     current = teleport
     for step_index in range(STEPS):
         rounded = current.astype(jnp.bfloat16).reshape(blocks_dev, quarter, hidden)
-        line_blocks = lax.all_gather(rounded, "z", axis=0, tiled=True)
-        outgoing = jnp.take(line_blocks, send_index, axis=0)
+        outgoing = jnp.take(rounded, send_index, axis=0)
         received = lax.all_to_all(
-            outgoing, ("x", "c"), split_axis=0, concat_axis=0, tiled=True
+            outgoing, ("z", "x", "c"), split_axis=0, concat_axis=0, tiled=True
         )
         partial = block_apply(
-            forward_kernel, group_row, member, member_slot, weights, received,
+            forward_kernel, group_row, member, reader_slot, weights, received,
             (quarters, blocks_dev, quarter, hidden),
         )
         summed = edge_exchange(partial, quarters, True, 1)

time: 347 us -> 398 us (1.15); the launches traced: 346 us -> 393 us
  waiting for transfers between devices: 101 us -> 171 us
  blocking collectives: 36.4 us -> 0 us
  starting transfers between devices: 21.4 us -> 31.1 us
    all_to_all x1 -> x2, waiting for transfers between devices: 0.01 us -> 53.8 us  [per_device(): lax.all_to_all(outgoing, ('z', 'x', 'c'), split_axis=0, concat_axis=0, ti...]
    reduce_scatter x2, waiting for transfers between devices: 29.3 us -> 66.1 us  [per_device(): owned = lax.psum_scatter(dense, 'z', scatter_dimension=0, tiled=True)]
    all_to_all x1 -> x0, blocking collectives: 36.4 us -> none  [per_device(): lax.all_to_all(outgoing, ('x', 'c'), split_axis=0, concat_axis=0, tiled=T...]
    all_gather x2 -> x0, waiting for transfers between devices: 14.8 us -> none  [per_device(): line_blocks = lax.all_gather(rounded, 'z', axis=0, tiled=True)]
    all_to_all x1 -> x2, starting transfers between devices: 4.27 us -> 18.9 us  [per_device(): lax.all_to_all(outgoing, ('z', 'x', 'c'), split_axis=0, concat_axis=0, ti...]
    all_to_all x2, waiting for transfers between devices: 56.4 us -> 50.9 us  [per_device(): lax.all_to_all(slot_sums, ('x', 'c'), split_axis=0, concat_axis=0, tiled=...]
    all_to_all x2, starting transfers between devices: 17.1 us -> 12.2 us  [per_device(): lax.all_to_all(slot_sums, ('x', 'c'), split_axis=0, concat_axis=0, tiled=...]
  transfers between devices with their start and end apart: 7 -> 6, of which waited for: 4 -> 4; matrix products, arithmetic and copies ran while one was open for 4% -> 4% of each run, Pallas kernels for 34% -> 28%
where the time goes in v1:
time: 398 us; the launch traced here: 393 us
  waiting for transfers between devices  171 us (43%)
  Pallas kernels  148 us (37%)
  starting transfers between devices  31.1 us (8%)
  other arithmetic  14.4 us (4%)
  between operations  14.3 us (4%)
  local copies, waits for them, and re-layouts  13.3 us (3%)
    pallas_call x4, Pallas kernels, block_apply(): pl.pallas_call(kernel, out_shape=jax.ShapeDtypeStruct(out_shape, jnp.floa...  77.7 us
    reduce_scatter x2, waiting for transfers between devices, per_device(): owned = lax.psum_scatter(dense, 'z', scatter_dimension=0, tiled=True)  66.1 us
    pallas_call x4, Pallas kernels, edge_exchange(): pl.pallas_call(functools.partial(edge_exchange_kernel, reduce), out_shape...  56.6 us
    all_to_all x2, waiting for transfers between devices, per_device(): lax.all_to_all(outgoing, ('z', 'x', 'c'), split_axis=0, concat_axis=0, ti...  53.8 us
    all_to_all x2, waiting for transfers between devices, per_device(): lax.all_to_all(slot_sums, ('x', 'c'), split_axis=0, concat_axis=0, tiled=...  50.9 us
    all_to_all x2, starting transfers between devices, per_device(): lax.all_to_all(outgoing, ('z', 'x', 'c'), split_axis=0, concat_axis=0, ti...  18.9 us
    pallas_call x2, Pallas kernels, combine_apply(): pl.pallas_call(combine_kernel, out_shape=jax.ShapeDtypeStruct((lines, blo...  13.9 us
    all_to_all x2, starting transfers between devices, per_device(): lax.all_to_all(slot_sums, ('x', 'c'), split_axis=0, concat_axis=0, tiled=...  12.2 us
  transfers between devices with their start and end apart: 6, of which 4 were waited for; matrix products, arithmetic and copies ran while one was open for 4% of the time, Pallas kernels for 28%

profile of v1, /device:TPU:1, one launch (start us, length us, event | category | flops | bytes accessed | tf_op | source)
XLA Modules:
  0.0 393.0 jit_solution(10642849290256893644)
XLA Ops:
  7.2 0.8 convert_reduce_fusion
  8.0 0.9 fusion
  8.9 0.2 reduce-window.7
  9.1 0.8 select_reduce_fusion
  9.9 1.2 scatter_custom_fusion.members_ref
  11.1 0.0 copy-start.6
  11.1 0.7 fusion.7
  11.9 0.1 convert_reduce_fusion.1
  11.9 0.5 broadcast_minimum_fusion.rows_ref
  12.5 1.6 convert_element_type.73
  14.1 11.7 %shard_map.81.a_ref = bf16[4,8,64,128]{3,2,1,0:T(8,128)(2,1)} custom-call(bf16[1,8,64,128]{3,2,1,0:T(8,128)(2,1)} %bitcast.42), custom_call_target="tpu_custom_call" | custom-call | tf_op jit(solution)/shard_map/pallas_call | solution.py:143
  25.8 2.5 gather_fusion.2
  28.3 0.0 copy-done.6
  28.3 19.1 %shard_map.82 = f32[128,64,128]{2,1,0:T(8,128)} custom-call(s32[56]{0:T(128)} %broadcast_minimum_fusion.rows_ref, s32[224]{0:T(256)} %copy-done.6, s32[224]{0:T(256)} %gather_fusion.2, bf16[192,64,256]{2,1,0:T(8,128)(2,1)} %bitcast.36, bf16[4,8,64,128]{3,2,1,0:T(8,128)(2,1)} %shard_map.81.a_ref), custom_call_target="tpu_custom_call" | custom-call | tf_op jit(solution)/shard_map/pallas_call | solution.py:159
  47.4 6.5 %all-to-all-start.2 = ((f32[128,64,128]{2,1,0:T(8,128)}), f32[128,64,128]{2,1,0:T(8,128)}, u32[]{:S(2)}, u32[]{:S(2)}) async-start(f32[128,64,128]{2,1,0:T(8,128)} %shard_map.82), calls=%async_computation.2 | async-start | bytes 8388608 | tf_op jit(solution)/shard_map/all_to_all | solution.py:276
  53.9 0.0 copy-start
  53.9 0.0 reduce-scatter.3.cloned.1.call-start
  53.9 0.1 fusion.3
  54.0 0.1 broadcast_or_fusion
  54.1 0.1 reshape.233
  54.2 0.4 copy-done
  54.6 0.0 copy-start.4
  54.6 1.8 gather_fusion.1
  56.5 0.1 dynamic-slice_maximum_fusion
  56.5 0.1 max.11
  56.7 0.0 copy-done.4
  56.7 1.0 gather_fusion.3
  57.7 45.1 %all-to-all-done.2.arrived_ref = f32[128,64,128]{2,1,0:T(8,128)} async-done(((f32[128,64,128]{2,1,0:T(8,128)}), f32[128,64,128]{2,1,0:T(8,128)}, u32[]{:S(2)}, u32[]{:S(2)}) %all-to-all-start.2) | async-done | bytes 4194336 | tf_op jit(solution)/shard_map/all_to_all | solution.py:276
  102.8 6.9 %shard_map.83 = f32[8,8,64,128]{3,2,1,0:T(8,128)} custom-call(s32[128]{0:T(128)} %gather_fusion.1, f32[128,64,128]{2,1,0:T(8,128)} %all-to-all-done.2.arrived_ref), custom_call_target="tpu_custom_call" | custom-call | tf_op jit(solution)/shard_map/pallas_call | solution.py:181
  109.7 0.0 reduce-scatter.3.cloned.1.call-update
  109.8 1.6 broadcast_select_fusion
  111.4 10.6 %all-to-all-start = ((bf16[128,64,128]{2,1,0:T(8,128)(2,1)}), bf16[128,64,128]{2,1,0:T(8,128)(2,1)S(1)}, u32[]{:S(2)}, u32[]{:S(2)}) async-start(bf16[128,64,128]{2,1,0:T(8,128)(2,1)} %broadcast_select_fusion), calls=%async_computation | async-start | bytes 4194304 | tf_op jit(solution)/shard_map/all_to_all | solution.py:257
  122.0 66.1 %reduce-scatter.3.cloned.1.call-done = f32[1,8,64,128]{3,2,1,0:T(8,128)} async-done(((f32[8,8,64,128]{3,2,1,0:T(8,128)}), f32[1,8,64,128]{3,2,1,0:T(8,128)}) %reduce-scatter.3.cloned.1.call-update) | async-done | bytes 262160 | tf_op jit(solution)/shard_map/reduce_scatter | solution.py:280
  188.1 1.7 broadcast_multiply_fusion.1
  189.8 12.4 %shard_map.84.a_ref = bf16[4,8,64,128]{3,2,1,0:T(8,128)(2,1)} custom-call(bf16[1,8,64,128]{3,2,1,0:T(8,128)(2,1)} %get-tuple-element.4.x_ref), custom_call_target="tpu_custom_call" | custom-call | tf_op jit(solution)/shard_map/pallas_call | solution.py:143
  202.1 19.0 %shard_map.85 = f32[128,64,128]{2,1,0:T(8,128)} custom-call(s32[56]{0:T(128)} %broadcast_minimum_fusion.rows_ref, s32[224]{0:T(256)} %copy-done.6, s32[224]{0:T(256)} %gather_fusion.2, bf16[192,64,256]{2,1,0:T(8,128)(2,1)} %bitcast.37, bf16[4,8,64,128]{3,2,1,0:T(8,128)(2,1)} %shard_map.84.a_ref), custom_call_target="tpu_custom_call" | custom-call | tf_op jit(solution)/shard_map/pallas_call | solution.py:159
  221.2 0.0 copy-start.1
  221.2 0.0 all-to-all-done.x_ref
  221.2 0.0 copy-start.2
  221.2 1.4 copy-done.2
  222.6 5.7 %all-to-all-start.3 = ((f32[128,64,128]{2,1,0:T(8,128)}), f32[128,64,128]{2,1,0:T(8,128)}, u32[]{:S(2)}, u32[]{:S(2)}) async-start(f32[128,64,128]{2,1,0:T(8,128)} %shard_map.85), calls=%async_computation.4 | async-start | bytes 8388608 | tf_op jit(solution)/shard_map/all_to_all | solution.py:276
  228.3 0.0 copy-done.1
  228.3 2.5 gather_fusion
  230.8 19.8 %shard_map.77.x_ref = f32[4,8,64,128]{3,2,1,0:T(8,128)} custom-call(s32[56]{0:T(128)} %broadcast_minimum_fusion.rows_ref, s32[224]{0:T(256)} %copy-done.6, s32[224]{0:T(256)} %gather_fusion, bf16[192,64,256]{2,1,0:T(8,128)(2,1)} %bitcast.38, bf16[128,64,128]{2,1,0:T(8,128)(2,1)} %copy-done.2), custom_call_target="tpu_custom_call" | custom-call | tf_op jit(solution)/shard_map/pallas_call | solution.py:159
  250.6 17.2 %shard_map.78 = f32[8,64,128]{2,1,0:T(8,128)} custom-call(f32[4,8,64,128]{3,2,1,0:T(8,128)} %shard_map.77.x_ref), custom_call_target="tpu_custom_call" | custom-call | tf_op jit(solution)/shard_map/pallas_call | solution.py:143
  267.8 1.0 broadcast_multiply_fusion.3
  268.8 1.0 gather_fusion.4
  269.8 1.7 broadcast_select_fusion.1
  271.4 5.8 %all-to-all-done.3.arrived_ref = f32[128,64,128]{2,1,0:T(8,128)} async-done(((f32[128,64,128]{2,1,0:T(8,128)}), f32[128,64,128]{2,1,0:T(8,128)}, u32[]{:S(2)}, u32[]{:S(2)}) %all-to-all-start.3) | async-done | bytes 4194336 | tf_op jit(solution)/shard_map/all_to_all | solution.py:276
  277.2 8.3 %all-to-all-start.1 = ((bf16[128,64,128]{2,1,0:T(8,128)(2,1)}), bf16[128,64,128]{2,1,0:T(8,128)(2,1)S(1)}, u32[]{:S(2)}, u32[]{:S(2)}) async-start(bf16[128,64,128]{2,1,0:T(8,128)(2,1)} %broadcast_select_fusion.1), calls=%async_computation.1 | async-start | bytes 4194304 | tf_op jit(solution)/shard_map/all_to_all | solution.py:257
  285.5 0.0 reduce-scatter.5.cloned.1.call-start
  285.5 6.9 %shard_map.86 = f32[8,8,64,128]{3,2,1,0:T(8,128)} custom-call(s32[128]{0:T(128)} %gather_fusion.1, f32[128,64,128]{2,1,0:T(8,128)} %all-to-all-done.3.arrived_ref), custom_call_target="tpu_custom_call" | custom-call | tf_op jit(solution)/shard_map/pallas_call | solution.py:181
  292.4 0.0 reduce-scatter.5.cloned.1.call-update
  292.5 53.8 %all-to-all-done.1.x_ref = bf16[128,64,128]{2,1,0:T(8,128)(2,1)S(1)} async-done(((bf16[128,64,128]{2,1,0:T(8,128)(2,1)}), bf16[128,64,128]{2,1,0:T(8,128)(2,1)S(1)}, u32[]{:S(2)}, u32[]{:S(2)}) %all-to-all-start.1) | async-done | bytes 2097184 | tf_op jit(solution)/shard_map/all_to_all | solution.py:257
  346.2 0.0 copy-start.3
  346.2 1.3 copy-done.3
  347.5 19.8 %shard_map.79.x_ref = f32[4,8,64,128]{3,2,1,0:T(8,128)} custom-call(s32[56]{0:T(128)} %broadcast_minimum_fusion.rows_ref, s32[224]{0:T(256)} %copy-done.6, s32[224]{0:T(256)} %gather_fusion, bf16[192,64,256]{2,1,0:T(8,128)(2,1)} %bitcast.39, bf16[128,64,128]{2,1,0:T(8,128)(2,1)} %copy-done.3), custom_call_target="tpu_custom_call" | custom-call | tf_op jit(solution)/shard_map/pallas_call | solution.py:159
  367.4 0.0 copy-start.5
  367.4 15.3 %shard_map.80 = f32[8,64,128]{2,1,0:T(8,128)} custom-call(f32[4,8,64,128]{3,2,1,0:T(8,128)} %shard_map.79.x_ref), custom_call_target="tpu_custom_call" | custom-call | tf_op jit(solution)/shard_map/pallas_call | solution.py:143
  382.8 1.0 broadcast_multiply_fusion.2
  383.7 0.7 bitcast_add_fusion.2
  384.5 1.0 broadcast_multiply_fusion
  385.5 0.0 copy-done.5
  385.5 0.7 bitcast_add_fusion
  (14 shorter events, 0.2 us)
Async XLA Ops:
  11.1 17.2 %copy-start.6 = (s32[224]{0:T(256)}, s32[224]{0:T(256)S(1)}, u32[]{:S(2)}) copy-start(s32[224]{0:T(256)S(1)} %scatter_custom_fusion.members_ref) | copy-start | bytes 2692
  47.4 55.4 %all-to-all-start.2 = ((f32[128,64,128]{2,1,0:T(8,128)}), f32[128,64,128]{2,1,0:T(8,128)}, u32[]{:S(2)}, u32[]{:S(2)}) async-start(f32[128,64,128]{2,1,0:T(8,128)} %shard_map.82), calls=%async_computation.2 | async-start | bytes 8388608 | tf_op jit(solution)/shard_map/all_to_all | solution.py:276
  53.9 0.8 copy-start
  53.9 134.2 %reduce-scatter.3.cloned.1.call-start = ((), (), s32[]{:S(2)}) async-start(), calls=%async_computation.6 | async-start | bytes 2359296 | tf_op jit(solution)/shard_map/reduce_scatter | solution.py:280
  54.6 2.0 copy-start.4
  111.4 109.8 %all-to-all-start = ((bf16[128,64,128]{2,1,0:T(8,128)(2,1)}), bf16[128,64,128]{2,1,0:T(8,128)(2,1)S(1)}, u32[]{:S(2)}, u32[]{:S(2)}) async-start(bf16[128,64,128]{2,1,0:T(8,128)(2,1)} %broadcast_select_fusion), calls=%async_computation | async-start | bytes 4194304 | tf_op jit(solution)/shard_map/all_to_all | solution.py:257
  221.2 7.1 %copy-start.1 = (s32[1,192]{1,0:T(1,128)S(1)}, s32[1,192]{1,0:T(1,128)}, u32[]{:S(2)}) copy-start(s32[1,192]{1,0:T(1,128)} %param.12) | copy-start | bytes 2308
  221.2 1.4 copy-start.2
  222.6 54.6 %all-to-all-start.3 = ((f32[128,64,128]{2,1,0:T(8,128)}), f32[128,64,128]{2,1,0:T(8,128)}, u32[]{:S(2)}, u32[]{:S(2)}) async-start(f32[128,64,128]{2,1,0:T(8,128)} %shard_map.85), calls=%async_computation.4 | async-start | bytes 8388608 | tf_op jit(solution)/shard_map/all_to_all | solution.py:276
  277.2 69.1 %all-to-all-start.1 = ((bf16[128,64,128]{2,1,0:T(8,128)(2,1)}), bf16[128,64,128]{2,1,0:T(8,128)(2,1)S(1)}, u32[]{:S(2)}, u32[]{:S(2)}) async-start(bf16[128,64,128]{2,1,0:T(8,128)(2,1)} %broadcast_select_fusion.1), calls=%async_computation.1 | async-start | bytes 4194304 | tf_op jit(solution)/shard_map/all_to_all | solution.py:257
  285.5 99.0 %reduce-scatter.5.cloned.1.call-start = ((), (), s32[]{:S(2)}) async-start(), calls=%async_computation.7 | async-start | bytes 2359296 | tf_op jit(solution)/shard_map/reduce_scatter | solution.py:280
  346.2 1.3 copy-start.3
  367.4 18.1 %copy-start.5 = (f32[512,128]{1,0:T(8,128)S(1)}, f32[512,128]{1,0:T(8,128)}, u32[]{:S(2)}) copy-start(f32[512,128]{1,0:T(8,128)} %param.9) | copy-start | bytes 786436
Sparse Core Ops, SparseCore 0:
  109.9 78.1 reduce-scatter.2
  292.6 62.6 reduce-scatter.4

commit v2 on v0

--- a/solution.py
+++ b/solution.py
@@ -26,7 +26,7 @@
         pltpu.make_async_copy(v_hbm.at[b], vbuf.at[i], sems.at[i]).start()
         return carry
 
-    lax.fori_loop(0, vbuf.shape[0], issue, 0)
+    lax.fori_loop(0, vbuf.shape[0], issue, 0, unroll=8)
 
 
 def wait_group(v_hbm, vbuf, sems, g):
@@ -58,7 +58,7 @@
         out_ref[:, j] += product.reshape(quarters, quarter, hidden)
         return carry
 
-    lax.fori_loop(0, group_count, body, 0)
+    lax.fori_loop(0, group_count, body, 0, unroll=4)
 
 
 def backward_kernel(rows_ref, members_ref, slots_ref, v_hbm, a_ref, out_ref, vbuf, sems):
@@ -84,7 +84,7 @@
 
         return carry
 
-    lax.fori_loop(0, group_count, body, 0)
+    lax.fori_loop(0, group_count, body, 0, unroll=4)
 
 
 def combine_kernel(want_ref, arrived_ref, out_ref):
@@ -100,7 +100,7 @@
 
         return carry
 
-    lax.fori_loop(0, arrived_ref.shape[0], body, 0)
+    lax.fori_loop(0, arrived_ref.shape[0], body, 0, unroll=8)
 
 
 def edge_exchange_kernel(reduce, x_ref, out_ref, held, send_sem, recv_sem):

time: 347 us -> 348 us (level)
  transfers between devices with their start and end apart: 7 -> 7, of which waited for: 4 -> 4; matrix products, arithmetic and copies ran while one was open for 4% -> 4% of each run, Pallas kernels for 34% -> 33%
where the time goes in v2:
time: 348 us; the launch traced here: 347 us
  Pallas kernels  147 us (42%)
  waiting for transfers between devices  101 us (29%)
  blocking collectives  36.4 us (10%)
  starting transfers between devices  21.1 us (6%)
  other arithmetic  14.2 us (4%)
  between operations  14 us (4%)
  local copies, waits for them, and re-layouts  11.8 us (3%)
    pallas_call x4, Pallas kernels, block_apply(): pl.pallas_call(kernel, out_shape=jax.ShapeDtypeStruct(out_shape, jnp.floa...  78.6 us
    all_to_all x2, waiting for transfers between devices, per_device(): lax.all_to_all(slot_sums, ('x', 'c'), split_axis=0, concat_axis=0, tiled=...  56.4 us
    pallas_call x4, Pallas kernels, edge_exchange(): pl.pallas_call(functools.partial(edge_exchange_kernel, reduce), out_shape...  55.2 us
    all_to_all x1, blocking collectives, per_device(): lax.all_to_all(outgoing, ('x', 'c'), split_axis=0, concat_axis=0, tiled=T...  36.4 us
    reduce_scatter x2, waiting for transfers between devices, per_device(): owned = lax.psum_scatter(dense, 'z', scatter_dimension=0, tiled=True)  29.4 us
    all_to_all x2, starting transfers between devices, per_device(): lax.all_to_all(slot_sums, ('x', 'c'), split_axis=0, concat_axis=0, tiled=...  16.6 us
    all_gather x2, waiting for transfers between devices, per_device(): line_blocks = lax.all_gather(rounded, 'z', axis=0, tiled=True)  15.4 us
    pallas_call x2, Pallas kernels, combine_apply(): pl.pallas_call(combine_kernel, out_shape=jax.ShapeDtypeStruct((lines, blo...  13.5 us
  transfers between devices with their start and end apart: 7, of which 4 were waited for; matrix products, arithmetic and copies ran while one was open for 4% of the time, Pallas kernels for 33%

profile of v2, /device:TPU:1, one launch (start us, length us, event | category | flops | bytes accessed | tf_op | source)
XLA Modules:
  0.0 347.1 jit_solution(12185991169772979534)
XLA Ops:
  7.2 0.0 copy-start
  7.2 0.8 convert_reduce_fusion
  8.0 0.9 fusion
  8.9 0.2 reduce-window.7
  9.1 0.8 select_reduce_fusion
  9.9 1.2 scatter_custom_fusion.members_ref
  11.1 0.0 copy-start.5
  11.2 0.7 fusion.7
  11.9 0.1 convert_reduce_fusion.1
  12.0 0.5 broadcast_minimum_fusion.rows_ref
  12.4 1.6 convert_element_type.73
  14.1 11.7 %shard_map.81.a_ref = bf16[4,8,64,128]{3,2,1,0:T(8,128)(2,1)} custom-call(bf16[1,8,64,128]{3,2,1,0:T(8,128)(2,1)} %bitcast.38), custom_call_target="tpu_custom_call" | custom-call | tf_op jit(solution)/shard_map/pallas_call | solution.py:143
  25.8 2.5 gather_fusion
  28.3 0.0 copy-done.5
  28.3 19.5 %shard_map.82 = f32[128,64,128]{2,1,0:T(8,128)} custom-call(s32[56]{0:T(128)} %broadcast_minimum_fusion.rows_ref, s32[224]{0:T(256)} %copy-done.5, s32[224]{0:T(256)} %gather_fusion, bf16[192,64,256]{2,1,0:T(8,128)(2,1)} %bitcast.34, bf16[4,8,64,128]{3,2,1,0:T(8,128)(2,1)} %shard_map.81.a_ref), custom_call_target="tpu_custom_call" | custom-call | tf_op jit(solution)/shard_map/pallas_call | solution.py:159
  47.8 0.0 copy-start.2
  47.8 6.6 %all-to-all-start.2 = ((f32[128,64,128]{2,1,0:T(8,128)}), f32[128,64,128]{2,1,0:T(8,128)}, u32[]{:S(2)}, u32[]{:S(2)}) async-start(f32[128,64,128]{2,1,0:T(8,128)} %shard_map.82), calls=%async_computation.2 | async-start | bytes 8388608 | tf_op jit(solution)/shard_map/all_to_all | solution.py:274
  54.4 0.0 all-gather.3.cloned.1.call-start
  54.5 0.7 convert_element_type.71
  55.1 0.0 all-gather.3.cloned.1.call-update
  55.2 0.0 reduce-scatter.3.cloned.1.call-start
  55.3 0.1 fusion.3
  55.3 0.1 broadcast_or_fusion
  55.4 0.1 reshape.235
  55.6 1.7 gather_fusion.1
  57.3 46.1 %all-to-all-done.2.arrived_ref = f32[128,64,128]{2,1,0:T(8,128)} async-done(((f32[128,64,128]{2,1,0:T(8,128)}), f32[128,64,128]{2,1,0:T(8,128)}, u32[]{:S(2)}, u32[]{:S(2)}) %all-to-all-start.2) | async-done | bytes 4194336 | tf_op jit(solution)/shard_map/all_to_all | solution.py:274
  103.4 6.8 %shard_map.83 = f32[8,8,64,128]{3,2,1,0:T(8,128)} custom-call(s32[128]{0:T(128)} %gather_fusion.1, f32[128,64,128]{2,1,0:T(8,128)} %all-to-all-done.2.arrived_ref), custom_call_target="tpu_custom_call" | custom-call | tf_op jit(solution)/shard_map/pallas_call | solution.py:181
  110.1 0.0 reduce-scatter.3.cloned.1.call-update
  110.2 0.1 add.205
  110.2 0.1 add.206
  110.4 0.3 copy-done.3
  110.7 0.0 all-gather.3.cloned.1.call-done
  110.8 2.2 gather_fusion.2
  112.9 1.6 broadcast_select_fusion
  114.5 4.3 %all-to-all-start = ((bf16[128,64,128]{2,1,0:T(8,128)(2,1)}), bf16[128,64,128]{2,1,0:T(8,128)(2,1)S(1)}, u32[]{:S(2)}, u32[]{:S(2)}) async-start(bf16[128,64,128]{2,1,0:T(8,128)(2,1)} %broadcast_select_fusion), calls=%async_computation | async-start | bytes 4194304 | tf_op jit(solution)/shard_map/all_to_all | solution.py:255
  118.9 29.4 %reduce-scatter.3.cloned.1.call-done = f32[1,8,64,128]{3,2,1,0:T(8,128)} async-done(((f32[8,8,64,128]{3,2,1,0:T(8,128)}), f32[1,8,64,128]{3,2,1,0:T(8,128)}) %reduce-scatter.3.cloned.1.call-update) | async-done | bytes 262160 | tf_op jit(solution)/shard_map/reduce_scatter | solution.py:278
  148.3 1.7 broadcast_multiply_fusion.1
  150.0 9.7 %shard_map.84.a_ref = bf16[4,8,64,128]{3,2,1,0:T(8,128)(2,1)} custom-call(bf16[1,8,64,128]{3,2,1,0:T(8,128)(2,1)} %get-tuple-element.6.x_ref), custom_call_target="tpu_custom_call" | custom-call | tf_op jit(solution)/shard_map/pallas_call | solution.py:143
  159.7 19.5 %shard_map.85 = f32[128,64,128]{2,1,0:T(8,128)} custom-call(s32[56]{0:T(128)} %broadcast_minimum_fusion.rows_ref, s32[224]{0:T(256)} %copy-done.5, s32[224]{0:T(256)} %gather_fusion, bf16[192,64,256]{2,1,0:T(8,128)(2,1)} %bitcast.35, bf16[4,8,64,128]{3,2,1,0:T(8,128)(2,1)} %shard_map.84.a_ref), custom_call_target="tpu_custom_call" | custom-call | tf_op jit(solution)/shard_map/pallas_call | solution.py:159
  179.2 0.0 all-to-all-done.x_ref
  179.2 1.3 copy-done.1
  180.5 10.0 %all-to-all-start.3 = ((f32[128,64,128]{2,1,0:T(8,128)}), f32[128,64,128]{2,1,0:T(8,128)}, u32[]{:S(2)}, u32[]{:S(2)}) async-start(f32[128,64,128]{2,1,0:T(8,128)} %shard_map.85), calls=%async_computation.4 | async-start | bytes 8388608 | tf_op jit(solution)/shard_map/all_to_all | solution.py:274
  190.5 0.0 all-gather.5.cloned.1.call-start
  190.6 19.8 %shard_map.77.x_ref = f32[4,8,64,128]{3,2,1,0:T(8,128)} custom-call(s32[56]{0:T(128)} %broadcast_minimum_fusion.rows_ref, s32[224]{0:T(256)} %copy-done.5, s32[224]{0:T(256)} %gather_fusion, bf16[192,64,256]{2,1,0:T(8,128)(2,1)} %bitcast.36, bf16[128,64,128]{2,1,0:T(8,128)(2,1)} %copy-done.1), custom_call_target="tpu_custom_call" | custom-call | tf_op jit(solution)/shard_map/pallas_call | solution.py:159
  210.3 17.1 %shard_map.78 = f32[8,64,128]{2,1,0:T(8,128)} custom-call(f32[4,8,64,128]{3,2,1,0:T(8,128)} %shard_map.77.x_ref), custom_call_target="tpu_custom_call" | custom-call | tf_op jit(solution)/shard_map/pallas_call | solution.py:143
  227.4 1.0 broadcast_multiply_fusion.3
  228.4 0.7 fusion.1
  229.1 0.0 all-gather.5.cloned.1.call-update
  229.1 0.0 reduce-scatter.5.cloned.1.call-start
  229.2 10.3 %all-to-all-done.3.arrived_ref = f32[128,64,128]{2,1,0:T(8,128)} async-done(((f32[128,64,128]{2,1,0:T(8,128)}), f32[128,64,128]{2,1,0:T(8,128)}, u32[]{:S(2)}, u32[]{:S(2)}) %all-to-all-start.3) | async-done | bytes 4194336 | tf_op jit(solution)/shard_map/all_to_all | solution.py:274
  239.5 6.7 %shard_map.86 = f32[8,8,64,128]{3,2,1,0:T(8,128)} custom-call(s32[128]{0:T(128)} %gather_fusion.1, f32[128,64,128]{2,1,0:T(8,128)} %all-to-all-done.3.arrived_ref), custom_call_target="tpu_custom_call" | custom-call | tf_op jit(solution)/shard_map/pallas_call | solution.py:181
  246.2 0.0 reduce-scatter.5.cloned.1.call-update
  246.3 15.4 %all-gather.5.cloned.1.call-done = bf16[64,64,128]{2,1,0:T(8,128)(2,1)} async-done(((bf16[8,64,128]{2,1,0:T(8,128)(2,1)}), bf16[64,64,128]{2,1,0:T(8,128)(2,1)}) %all-gather.5.cloned.1.call-update) | async-done | bytes 1048592 | tf_op jit(solution)/shard_map/all_gather | solution.py:253
  261.6 2.2 gather_fusion.3
  263.8 0.3 broadcast_select_fusion.1
  264.1 36.4 %all_to_all.20.x_ref = bf16[128,64,128]{2,1,0:T(8,128)(2,1)} all-to-all(bf16[128,64,128]{2,1,0:T(8,128)(2,1)S(1)} %broadcast_select_fusion.1), channel_id=1, replica_groups=mesh['z'=8,'x'=4,'c'=2,'edge'=4] {'x','c'}, dimensions={0} | all-to-all | bytes 4194304 | tf_op jit(solution)/shard_map/all_to_all | solution.py:255
  300.5 19.8 %shard_map.79.x_ref = f32[4,8,64,128]{3,2,1,0:T(8,128)} custom-call(s32[56]{0:T(128)} %broadcast_minimum_fusion.rows_ref, s32[224]{0:T(256)} %copy-done.5, s32[224]{0:T(256)} %gather_fusion, bf16[192,64,256]{2,1,0:T(8,128)(2,1)} %bitcast.37, bf16[128,64,128]{2,1,0:T(8,128)(2,1)} %all_to_all.20.x_ref), custom_call_target="tpu_custom_call" | custom-call | tf_op jit(solution)/shard_map/pallas_call | solution.py:159
  320.3 0.0 copy-start.4
  320.3 16.8 %shard_map.80 = f32[8,64,128]{2,1,0:T(8,128)} custom-call(f32[4,8,64,128]{3,2,1,0:T(8,128)} %shard_map.79.x_ref), custom_call_target="tpu_custom_call" | custom-call | tf_op jit(solution)/shard_map/pallas_call | solution.py:143
  337.1 1.0 broadcast_multiply_fusion.2
  338.1 0.7 bitcast_add_fusion.2
  338.8 1.0 broadcast_multiply_fusion
  339.8 0.0 copy-done.4
  339.8 0.7 bitcast_add_fusion
  (16 shorter events, 0.1 us)
Async XLA Ops:
  7.2 48.4 %copy-start = (s32[64,128]{1,0:T(8,128)S(1)}, s32[64,128]{1,0:T(8,128)}, u32[]{:S(2)}) copy-start(s32[64,128]{1,0:T(8,128)} %param.10) | copy-start | bytes 98308
  11.1 17.1 %copy-start.5 = (s32[224]{0:T(256)}, s32[224]{0:T(256)S(1)}, u32[]{:S(2)}) copy-start(s32[224]{0:T(256)S(1)} %scatter_custom_fusion.members_ref) | copy-start | bytes 2692
  47.8 6.7 %copy-start.2 = (f32[512,128]{1,0:T(8,128)S(1)}, f32[512,128]{1,0:T(8,128)}, u32[]{:S(2)}) copy-start(f32[512,128]{1,0:T(8,128)} %param.8) | copy-start | bytes 786436
  47.8 55.6 %all-to-all-start.2 = ((f32[128,64,128]{2,1,0:T(8,128)}), f32[128,64,128]{2,1,0:T(8,128)}, u32[]{:S(2)}, u32[]{:S(2)}) async-start(f32[128,64,128]{2,1,0:T(8,128)} %shard_map.82), calls=%async_computation.2 | async-start | bytes 8388608 | tf_op jit(solution)/shard_map/all_to_all | solution.py:274
  54.4 56.3 %all-gather.3.cloned.1.call-start = ((), (), s32[]{:S(2)}) async-start(), calls=%async_computation.6 | async-start | bytes 1179648 | tf_op jit(solution)/shard_map/all_gather | solution.py:253
  55.2 93.1 %reduce-scatter.3.cloned.1.call-start = ((), (), s32[]{:S(2)}) async-start(), calls=%async_computation.8 | async-start | bytes 2359296 | tf_op jit(solution)/shard_map/reduce_scatter | solution.py:278
  110.1 0.6 copy-start.3
  114.5 64.7 %all-to-all-start = ((bf16[128,64,128]{2,1,0:T(8,128)(2,1)}), bf16[128,64,128]{2,1,0:T(8,128)(2,1)S(1)}, u32[]{:S(2)}, u32[]{:S(2)}) async-start(bf16[128,64,128]{2,1,0:T(8,128)(2,1)} %broadcast_select_fusion), calls=%async_computation | async-start | bytes 4194304 | tf_op jit(solution)/shard_map/all_to_all | solution.py:255
  179.2 1.4 copy-start.1
  180.5 58.9 %all-to-all-start.3 = ((f32[128,64,128]{2,1,0:T(8,128)}), f32[128,64,128]{2,1,0:T(8,128)}, u32[]{:S(2)}, u32[]{:S(2)}) async-start(f32[128,64,128]{2,1,0:T(8,128)} %shard_map.85), calls=%async_computation.4 | async-start | bytes 8388608 | tf_op jit(solution)/shard_map/all_to_all | solution.py:274
  190.5 71.1 %all-gather.5.cloned.1.call-start = ((), (), s32[]{:S(2)}) async-start(), calls=%async_computation.7 | async-start | bytes 1179648 | tf_op jit(solution)/shard_map/all_gather | solution.py:253
  229.1 109.7 %reduce-scatter.5.cloned.1.call-start = ((), (), s32[]{:S(2)}) async-start(), calls=%async_computation.9 | async-start | bytes 2359296 | tf_op jit(solution)/shard_map/reduce_scatter | solution.py:278
  320.3 19.5 %copy-start.4 = (f32[512,128]{1,0:T(8,128)S(1)}, f32[512,128]{1,0:T(8,128)}, u32[]{:S(2)}) copy-start(f32[512,128]{1,0:T(8,128)} %param.9) | copy-start | bytes 786436
Sparse Core Ops, SparseCore 0:
  57.6 36.7 all-gather.2
  110.3 37.9 reduce-scatter.2
  229.2 32.3 all-gather.4
  264.0 41.7 reduce-scatter.4

commit v3 on v2

--- a/solution.py
+++ b/solution.py
@@ -248,6 +248,8 @@
     wanted_flat = wanted.reshape(-1)
 
     current = teleport
+    adjoint = cotangent
+    gradient = 0.1 * cotangent
     for step_index in range(STEPS):
         rounded = current.astype(jnp.bfloat16).reshape(blocks_dev, quarter, hidden)
         line_blocks = lax.all_gather(rounded, "z", axis=0, tiled=True)
@@ -262,9 +264,6 @@
         summed = edge_exchange(partial, quarters, True, 1)
         current = 0.9 * summed.reshape(row_count, hidden) + 0.1 * teleport
 
-    adjoint = cotangent
-    gradient = 0.1 * cotangent
-    for step_index in range(STEPS):
         rounded = adjoint.astype(jnp.bfloat16).reshape(1, blocks_dev, quarter, hidden)
         whole_rows = edge_exchange(rounded, quarters, False, 2)
         slot_sums = block_apply(
@@ -279,6 +278,8 @@
         adjoint = 0.9 * owned.reshape(row_count, hidden)
         factor = 0.1 if step_index + 1 < STEPS else 1.0
         gradient = gradient + factor * adjoint
+        if step_index + 1 < STEPS:
+            current, adjoint = lax.optimization_barrier((current, adjoint))
     return (current, gradient)
 
 

time: 348 us -> 359 us (1.032)
  waiting for transfers between devices: 101 us -> 121 us
  blocking collectives: 36.4 us -> 30.2 us
  starting transfers between devices: 21.1 us -> 16.8 us
    all_to_all x2, waiting for transfers between devices: 56.4 us -> 94.2 us  [per_device(): lax.all_to_all(slot_sums, ('x', 'c'), split_axis=0, concat_axis=0, tiled=...]
    reduce_scatter x2, waiting for transfers between devices: 29.4 us -> 0.01 us  [per_device(): owned = lax.psum_scatter(dense, 'z', scatter_dimension=0, tiled=True)]
    all_to_all x1, waiting for transfers between devices: 0.01 us -> 26.3 us  [per_device(): lax.all_to_all(outgoing, ('x', 'c'), split_axis=0, concat_axis=0, tiled=T...]
    all_gather x2, waiting for transfers between devices: 15.4 us -> 0.04 us  [per_device(): line_blocks = lax.all_gather(rounded, 'z', axis=0, tiled=True)]
    all_to_all x1, blocking collectives: 36.4 us -> 30.2 us  [per_device(): lax.all_to_all(outgoing, ('x', 'c'), split_axis=0, concat_axis=0, tiled=T...]
    all_to_all x2, starting transfers between devices: 16.6 us -> 12.5 us  [per_device(): lax.all_to_all(slot_sums, ('x', 'c'), split_axis=0, concat_axis=0, tiled=...]
  transfers between devices with their start and end apart: 7 -> 7, of which waited for: 4 -> 3; matrix products, arithmetic and copies ran while one was open for 4% -> 4% of each run, Pallas kernels for 33% -> 24%
where the time goes in v3:
time: 359 us; the launch traced here: 357 us
  Pallas kernels  147 us (41%)
  waiting for transfers between devices  121 us (34%)
  blocking collectives  30.2 us (8%)
  starting transfers between devices  16.8 us (5%)
  other arithmetic  14.3 us (4%)
  between operations  14 us (4%)
  local copies, waits for them, and re-layouts  11.9 us (3%)
    all_to_all x2, waiting for transfers between devices, per_device(): lax.all_to_all(slot_sums, ('x', 'c'), split_axis=0, concat_axis=0, tiled=...  94.2 us
    pallas_call x4, Pallas kernels, block_apply(): pl.pallas_call(kernel, out_shape=jax.ShapeDtypeStruct(out_shape, jnp.floa...  78.7 us
    pallas_call x4, Pallas kernels, edge_exchange(): pl.pallas_call(functools.partial(edge_exchange_kernel, reduce), out_shape...  55.9 us
    all_to_all x1, blocking collectives, per_device(): lax.all_to_all(outgoing, ('x', 'c'), split_axis=0, concat_axis=0, tiled=T...  30.2 us
    all_to_all x1, waiting for transfers between devices, per_device(): lax.all_to_all(outgoing, ('x', 'c'), split_axis=0, concat_axis=0, tiled=T...  26.3 us
    pallas_call x2, Pallas kernels, combine_apply(): pl.pallas_call(combine_kernel, out_shape=jax.ShapeDtypeStruct((lines, blo...  12.8 us
    all_to_all x2, starting transfers between devices, per_device(): lax.all_to_all(slot_sums, ('x', 'c'), split_axis=0, concat_axis=0, tiled=...  12.5 us
  transfers between devices with their start and end apart: 7, of which 3 were waited for; matrix products, arithmetic and copies ran while one was open for 4% of the time, Pallas kernels for 24%

profile of v3, /device:TPU:1, one launch (start us, length us, event | category | flops | bytes accessed | tf_op | source)
XLA Modules:
  0.0 356.9 jit_solution(8587792372031553542)
XLA Ops:
  7.2 0.0 copy-start
  7.2 0.8 convert_reduce_fusion
  8.0 0.9 fusion
  8.9 0.2 reduce-window.7
  9.1 0.8 select_reduce_fusion
  9.9 1.2 scatter_custom_fusion.members_ref
  11.1 0.0 copy-start.6
  11.2 0.7 fusion.6
  11.9 0.1 convert_reduce_fusion.1
  12.0 0.5 broadcast_minimum_fusion.rows_ref
  12.5 1.6 convert_element_type.71
  14.1 11.7 %shard_map.79.a_ref = bf16[4,8,64,128]{3,2,1,0:T(8,128)(2,1)} custom-call(bf16[1,8,64,128]{3,2,1,0:T(8,128)(2,1)} %bitcast.38), custom_call_target="tpu_custom_call" | custom-call | tf_op jit(solution)/shard_map/pallas_call | solution.py:143
  25.9 2.5 gather_fusion
  28.4 0.0 copy-done.6
  28.4 19.5 %shard_map.80 = f32[128,64,128]{2,1,0:T(8,128)} custom-call(s32[56]{0:T(128)} %broadcast_minimum_fusion.rows_ref, s32[224]{0:T(256)} %copy-done.6, s32[224]{0:T(256)} %gather_fusion, bf16[192,64,256]{2,1,0:T(8,128)(2,1)} %bitcast.34, bf16[4,8,64,128]{3,2,1,0:T(8,128)(2,1)} %shard_map.79.a_ref), custom_call_target="tpu_custom_call" | custom-call | tf_op jit(solution)/shard_map/pallas_call | solution.py:159
  47.9 0.0 copy-start.2
  47.9 6.6 %all-to-all-start.1 = ((f32[128,64,128]{2,1,0:T(8,128)}), f32[128,64,128]{2,1,0:T(8,128)}, u32[]{:S(2)}, u32[]{:S(2)}) async-start(f32[128,64,128]{2,1,0:T(8,128)} %shard_map.80), calls=%async_computation.1 | async-start | bytes 8388608 | tf_op jit(solution)/shard_map/all_to_all | solution.py:273
  54.6 0.0 all-gather.3.cloned.1.call-start
  54.6 0.0 copy-done.2
  54.6 0.7 convert_element_type.70
  55.2 0.0 all-gather.3.cloned.1.call-update
  55.3 0.0 reduce-scatter.3.cloned.1.call-start
  55.4 0.1 fusion.2
  55.5 0.1 broadcast_or_fusion
  55.5 0.1 reshape.240
  55.7 0.0 copy-done
  55.7 1.8 gather_fusion.1
  57.5 46.0 %all-to-all-done.1.arrived_ref = f32[128,64,128]{2,1,0:T(8,128)} async-done(((f32[128,64,128]{2,1,0:T(8,128)}), f32[128,64,128]{2,1,0:T(8,128)}, u32[]{:S(2)}, u32[]{:S(2)}) %all-to-all-start.1) | async-done | bytes 4194336 | tf_op jit(solution)/shard_map/all_to_all | solution.py:273
  103.5 6.4 %shard_map.81 = f32[8,8,64,128]{3,2,1,0:T(8,128)} custom-call(s32[128]{0:T(128)} %gather_fusion.1, f32[128,64,128]{2,1,0:T(8,128)} %all-to-all-done.1.arrived_ref), custom_call_target="tpu_custom_call" | custom-call | tf_op jit(solution)/shard_map/pallas_call | solution.py:181
  109.9 0.0 reduce-scatter.3.cloned.1.call-update
  110.0 0.1 add.205
  110.0 0.1 add.206
  110.2 0.4 copy-done.3
  110.5 0.0 all-gather.3.cloned.1.call-done
  110.6 2.2 gather_fusion.2
  112.7 0.3 broadcast_select_fusion
  113.0 30.2 %all_to_all.20.x_ref = bf16[128,64,128]{2,1,0:T(8,128)(2,1)} all-to-all(bf16[128,64,128]{2,1,0:T(8,128)(2,1)S(1)} %broadcast_select_fusion), channel_id=1, replica_groups=mesh['z'=8,'x'=4,'c'=2,'edge'=4] {'x','c'}, dimensions={0} | all-to-all | bytes 4194304 | tf_op jit(solution)/shard_map/all_to_all | solution.py:257
  143.2 19.8 %shard_map.77.x_ref = f32[4,8,64,128]{3,2,1,0:T(8,128)} custom-call(s32[56]{0:T(128)} %broadcast_minimum_fusion.rows_ref, s32[224]{0:T(256)} %copy-done.6, s32[224]{0:T(256)} %gather_fusion, bf16[192,64,256]{2,1,0:T(8,128)(2,1)} %bitcast.35, bf16[128,64,128]{2,1,0:T(8,128)(2,1)} %all_to_all.20.x_ref), custom_call_target="tpu_custom_call" | custom-call | tf_op jit(solution)/shard_map/pallas_call | solution.py:159
  163.0 16.0 %shard_map.78 = f32[8,64,128]{2,1,0:T(8,128)} custom-call(f32[4,8,64,128]{3,2,1,0:T(8,128)} %shard_map.77.x_ref), custom_call_target="tpu_custom_call" | custom-call | tf_op jit(solution)/shard_map/pallas_call | solution.py:143
  179.1 1.0 broadcast_multiply_fusion.4
  180.1 0.7 bitcast_add_fusion.3
  180.8 1.6 broadcast_multiply_fusion.2
  182.4 11.9 %shard_map.84.a_ref = bf16[4,8,64,128]{3,2,1,0:T(8,128)(2,1)} custom-call(bf16[1,8,64,128]{3,2,1,0:T(8,128)(2,1)} %broadcast_multiply_fusion.2), custom_call_target="tpu_custom_call" | custom-call | tf_op jit(solution)/shard_map/pallas_call | solution.py:143
  194.3 19.5 %shard_map.85 = f32[128,64,128]{2,1,0:T(8,128)} custom-call(s32[56]{0:T(128)} %broadcast_minimum_fusion.rows_ref, s32[224]{0:T(256)} %copy-done.6, s32[224]{0:T(256)} %gather_fusion, bf16[192,64,256]{2,1,0:T(8,128)(2,1)} %bitcast.36, bf16[4,8,64,128]{3,2,1,0:T(8,128)(2,1)} %shard_map.84.a_ref), custom_call_target="tpu_custom_call" | custom-call | tf_op jit(solution)/shard_map/pallas_call | solution.py:159
  213.8 5.9 %all-to-all-start.3 = ((f32[128,64,128]{2,1,0:T(8,128)}), f32[128,64,128]{2,1,0:T(8,128)}, u32[]{:S(2)}, u32[]{:S(2)}) async-start(f32[128,64,128]{2,1,0:T(8,128)} %shard_map.85), calls=%async_computation.4 | async-start | bytes 8388608 | tf_op jit(solution)/shard_map/all_to_all | solution.py:273
  219.8 0.0 all-gather.5.cloned.1.call-start
  219.8 0.7 all-gather.5.cloned.1.call-update
  220.5 0.0 reduce-scatter.5.cloned.1.call-start
  220.5 48.2 %all-to-all-done.3.arrived_ref = f32[128,64,128]{2,1,0:T(8,128)} async-done(((f32[128,64,128]{2,1,0:T(8,128)}), f32[128,64,128]{2,1,0:T(8,128)}, u32[]{:S(2)}, u32[]{:S(2)}) %all-to-all-start.3) | async-done | bytes 4194336 | tf_op jit(solution)/shard_map/all_to_all | solution.py:273
  268.7 6.4 %shard_map.86 = f32[8,8,64,128]{3,2,1,0:T(8,128)} custom-call(s32[128]{0:T(128)} %gather_fusion.1, f32[128,64,128]{2,1,0:T(8,128)} %all-to-all-done.3.arrived_ref), custom_call_target="tpu_custom_call" | custom-call | tf_op jit(solution)/shard_map/pallas_call | solution.py:181
  275.1 0.0 reduce-scatter.5.cloned.1.call-update
  275.1 0.0 all-gather.5.cloned.1.call-done
  275.2 2.2 gather_fusion.3
  277.3 1.6 broadcast_select_fusion.1
  278.9 4.2 %all-to-all-start.2 = ((bf16[128,64,128]{2,1,0:T(8,128)(2,1)}), bf16[128,64,128]{2,1,0:T(8,128)(2,1)S(1)}, u32[]{:S(2)}, u32[]{:S(2)}) async-start(bf16[128,64,128]{2,1,0:T(8,128)(2,1)} %broadcast_select_fusion.1), calls=%async_computation.3 | async-start | bytes 4194304 | tf_op jit(solution)/shard_map/all_to_all | solution.py:257
  283.2 26.3 %all-to-all-done.2.x_ref = bf16[128,64,128]{2,1,0:T(8,128)(2,1)S(1)} async-done(((bf16[128,64,128]{2,1,0:T(8,128)(2,1)}), bf16[128,64,128]{2,1,0:T(8,128)(2,1)S(1)}, u32[]{:S(2)}, u32[]{:S(2)}) %all-to-all-start.2) | async-done | bytes 2097184 | tf_op jit(solution)/shard_map/all_to_all | solution.py:257
  309.5 1.3 copy-done.1
  310.8 19.8 %shard_map.82.x_ref = f32[4,8,64,128]{3,2,1,0:T(8,128)} custom-call(s32[56]{0:T(128)} %broadcast_minimum_fusion.rows_ref, s32[224]{0:T(256)} %copy-done.6, s32[224]{0:T(256)} %gather_fusion, bf16[192,64,256]{2,1,0:T(8,128)(2,1)} %bitcast.37, bf16[128,64,128]{2,1,0:T(8,128)(2,1)} %copy-done.1), custom_call_target="tpu_custom_call" | custom-call | tf_op jit(solution)/shard_map/pallas_call | solution.py:159
  330.7 0.0 copy-start.5
  330.7 16.2 %shard_map.83 = f32[8,64,128]{2,1,0:T(8,128)} custom-call(f32[4,8,64,128]{3,2,1,0:T(8,128)} %shard_map.82.x_ref), custom_call_target="tpu_custom_call" | custom-call | tf_op jit(solution)/shard_map/pallas_call | solution.py:143
  346.9 1.0 broadcast_multiply_fusion.3
  347.9 0.7 bitcast_add_fusion.2
  348.6 1.0 broadcast_multiply_fusion.1
  349.6 0.7 bitcast_add_fusion
  (19 shorter events, 0.1 us)
Async XLA Ops:
  7.2 48.5 %copy-start = (s32[64,128]{1,0:T(8,128)S(1)}, s32[64,128]{1,0:T(8,128)}, u32[]{:S(2)}) copy-start(s32[64,128]{1,0:T(8,128)} %param.10) | copy-start | bytes 98308
  11.1 17.3 %copy-start.6 = (s32[224]{0:T(256)}, s32[224]{0:T(256)S(1)}, u32[]{:S(2)}) copy-start(s32[224]{0:T(256)S(1)} %scatter_custom_fusion.members_ref) | copy-start | bytes 2692
  47.9 6.6 %copy-start.2 = (f32[512,128]{1,0:T(8,128)S(1)}, f32[512,128]{1,0:T(8,128)}, u32[]{:S(2)}) copy-start(f32[512,128]{1,0:T(8,128)} %param.8) | copy-start | bytes 786436
  47.9 55.6 %all-to-all-start.1 = ((f32[128,64,128]{2,1,0:T(8,128)}), f32[128,64,128]{2,1,0:T(8,128)}, u32[]{:S(2)}, u32[]{:S(2)}) async-start(f32[128,64,128]{2,1,0:T(8,128)} %shard_map.80), calls=%async_computation.1 | async-start | bytes 8388608 | tf_op jit(solution)/shard_map/all_to_all | solution.py:273
  54.6 56.0 %all-gather.3.cloned.1.call-start = ((), (), s32[]{:S(2)}) async-start(), calls=%async_computation.6 | async-start | bytes 1179648 | tf_op jit(solution)/shard_map/all_gather | solution.py:255
  55.3 125.5 %reduce-scatter.3.cloned.1.call-start = ((), (), s32[]{:S(2)}) async-start(), calls=%async_computation.7 | async-start | bytes 2359296 | tf_op jit(solution)/shard_map/reduce_scatter | solution.py:277
  109.9 0.6 copy-start.3
  213.8 54.8 %all-to-all-start.3 = ((f32[128,64,128]{2,1,0:T(8,128)}), f32[128,64,128]{2,1,0:T(8,128)}, u32[]{:S(2)}, u32[]{:S(2)}) async-start(f32[128,64,128]{2,1,0:T(8,128)} %shard_map.85), calls=%async_computation.4 | async-start | bytes 8388608 | tf_op jit(solution)/shard_map/all_to_all | solution.py:273
  219.8 55.4 %all-gather.5.cloned.1.call-start = ((), (), s32[]{:S(2)}) async-start(), calls=%async_computation.8 | async-start | bytes 1179648 | tf_op jit(solution)/shard_map/all_gather | solution.py:255
  220.5 128.2 %reduce-scatter.5.cloned.1.call-start = ((), (), s32[]{:S(2)}) async-start(), calls=%async_computation.9 | async-start | bytes 2359296 | tf_op jit(solution)/shard_map/reduce_scatter | solution.py:277
  278.9 4.2 %copy-start.4 = (f32[1,8,64,128]{3,2,1,0:T(8,128)S(1)}, f32[1,8,64,128]{3,2,1,0:T(8,128)}, u32[]{:S(2)}) copy-start(f32[1,8,64,128]{3,2,1,0:T(8,128)} %reduce-scatter.3.cloned.1.call-done) | copy-start | bytes 786436
  278.9 30.6 %all-to-all-start.2 = ((bf16[128,64,128]{2,1,0:T(8,128)(2,1)}), bf16[128,64,128]{2,1,0:T(8,128)(2,1)S(1)}, u32[]{:S(2)}, u32[]{:S(2)}) async-start(bf16[128,64,128]{2,1,0:T(8,128)(2,1)} %broadcast_select_fusion.1), calls=%async_computation.3 | async-start | bytes 4194304 | tf_op jit(solution)/shard_map/all_to_all | solution.py:257
  309.5 1.3 copy-start.1
  330.7 19.0 %copy-start.5 = (f32[512,128]{1,0:T(8,128)S(1)}, f32[512,128]{1,0:T(8,128)}, u32[]{:S(2)}) copy-start(f32[512,128]{1,0:T(8,128)} %param.9) | copy-start | bytes 786436
Sparse Core Ops, SparseCore 0:
  57.8 36.7 all-gather.2
  110.1 38.5 reduce-scatter.2
  223.0 36.6 all-gather.4
  275.3 37.7 reduce-scatter.4

commit v4 on v2

--- a/solution.py
+++ b/solution.py
@@ -16,33 +16,21 @@
 X_SIZE = 4
 CORE_SIZE = 2
 GROUP = 4
-
-
-def fetch_all(members_ref, v_hbm, vbuf, sems):
-    last = v_hbm.shape[0] - 1
-
-    def issue(i, carry):
-        b = jnp.minimum(members_ref[i], last)
-        pltpu.make_async_copy(v_hbm.at[b], vbuf.at[i], sems.at[i]).start()
-        return carry
-
-    lax.fori_loop(0, vbuf.shape[0], issue, 0, unroll=8)
-
-
-def wait_group(v_hbm, vbuf, sems, g):
-    for m in range(GROUP):
-        pltpu.make_async_copy(v_hbm.at[0], vbuf.at[g * GROUP + m], sems.at[g * GROUP + m]).wait()
-
-
-def forward_kernel(rows_ref, members_ref, slots_ref, v_hbm, x_ref, out_ref, vbuf, sems):
-    group_count = rows_ref.shape[0]
-    block_count = v_hbm.shape[0]
+GROUPS_PER_STEP = 8
+BLOCKS = 192
+
+
+def forward_kernel(rows_ref, members_ref, slots_ref, v_ref, x_ref, out_ref):
+    block_count = BLOCKS
+    step = pl.program_id(0)
     quarters, _, quarter, hidden = out_ref.shape
-    fetch_all(members_ref, v_hbm, vbuf, sems)
-    out_ref[...] = jnp.zeros_like(out_ref)
-
-    def body(g, carry):
-        wait_group(v_hbm, vbuf, sems, g)
+
+    @pl.when(step == 0)
+    def _():
+        out_ref[...] = jnp.zeros_like(out_ref)
+
+    def body(i, carry):
+        g = step * GROUPS_PER_STEP + i
 
         j = rows_ref[g]
         pieces = []
@@ -51,29 +39,31 @@
             piece = x_ref[slots_ref[g * GROUP + m]]
             pieces.append(jnp.where(valid, piece, jnp.zeros_like(piece)))
         sources = jnp.concatenate(pieces, axis=0)
-        weights = vbuf[pl.ds(g * GROUP, GROUP)].reshape(GROUP * quarter, vbuf.shape[-1])
+        weights = v_ref[i]
         product = lax.dot_general(
             weights, sources, (((0,), (0,)), ((), ())), preferred_element_type=jnp.float32
         )
         out_ref[:, j] += product.reshape(quarters, quarter, hidden)
         return carry
 
-    lax.fori_loop(0, group_count, body, 0, unroll=4)
-
-
-def backward_kernel(rows_ref, members_ref, slots_ref, v_hbm, a_ref, out_ref, vbuf, sems):
-    group_count = rows_ref.shape[0]
-    block_count = v_hbm.shape[0]
+    lax.fori_loop(0, GROUPS_PER_STEP, body, 0, unroll=4)
+
+
+def backward_kernel(rows_ref, members_ref, slots_ref, v_ref, a_ref, out_ref):
+    block_count = BLOCKS
+    step = pl.program_id(0)
     quarters, _, quarter, hidden = a_ref.shape
-    fetch_all(members_ref, v_hbm, vbuf, sems)
-    out_ref[...] = jnp.zeros_like(out_ref)
-
-    def body(g, carry):
-        wait_group(v_hbm, vbuf, sems, g)
+
+    @pl.when(step == 0)
+    def _():
+        out_ref[...] = jnp.zeros_like(out_ref)
+
+    def body(i, carry):
+        g = step * GROUPS_PER_STEP + i
 
         j = rows_ref[g]
         sources = a_ref[:, j].reshape(quarters * quarter, hidden)
-        weights = vbuf[pl.ds(g * GROUP, GROUP)].reshape(GROUP * quarter, vbuf.shape[-1])
+        weights = v_ref[i]
         product = jnp.dot(weights, sources, preferred_element_type=jnp.float32)
         for m in range(GROUP):
             s = slots_ref[g * GROUP + m]
@@ -84,7 +74,7 @@
 
         return carry
 
-    lax.fori_loop(0, group_count, body, 0, unroll=4)
+    lax.fori_loop(0, GROUPS_PER_STEP, body, 0, unroll=4)
 
 
 def combine_kernel(want_ref, arrived_ref, out_ref):
@@ -154,25 +144,22 @@
     )(chunks)
 
 
-def block_apply(kernel, rows, members, slots, weights, dense, out_shape):
-    block_count, quarter, width = weights.shape
+def block_apply(kernel, rows, members, slots, weights_g, dense, out_shape):
+    group_count, depth, width = weights_g.shape
     return pl.pallas_call(
         kernel,
         out_shape=jax.ShapeDtypeStruct(out_shape, jnp.float32),
         grid_spec=pltpu.PrefetchScalarGridSpec(
             num_scalar_prefetch=3,
-            grid=(1,),
+            grid=(group_count // GROUPS_PER_STEP,),
             in_specs=[
-                pl.BlockSpec(memory_space=pl.ANY),
+                pl.BlockSpec((GROUPS_PER_STEP, depth, width), lambda i, *_: (i, 0, 0)),
                 pl.BlockSpec(dense.shape, lambda i, *_: (0,) * dense.ndim),
             ],
             out_specs=pl.BlockSpec(out_shape, lambda i, *_: (0,) * len(out_shape)),
-            scratch_shapes=[
-                pltpu.VMEM((members.shape[0], quarter, width), weights.dtype),
-                pltpu.SemaphoreType.DMA((members.shape[0],)),
-            ],
         ),
-    )(rows, members, slots, weights, dense)
+        compiler_params=pltpu.CompilerParams(dimension_semantics=("arbitrary",)),
+    )(rows, members, slots, weights_g, dense)
 
 
 def combine_apply(wanted, arrived, blocks_dev):
@@ -245,6 +232,9 @@
 
     member, group_row = grouping(row_ids, blocks_dev)
     member_slot = jnp.take(placed_slots, member, axis=0, mode="clip")
+    weights_g = jnp.take(weights, member, axis=0, mode="clip").reshape(
+        member.shape[0] // GROUP, GROUP * quarter, weights.shape[2]
+    )
     wanted_flat = wanted.reshape(-1)
 
     current = teleport
@@ -256,7 +246,7 @@
             outgoing, ("x", "c"), split_axis=0, concat_axis=0, tiled=True
         )
         partial = block_apply(
-            forward_kernel, group_row, member, member_slot, weights, received,
+            forward_kernel, group_row, member, member_slot, weights_g, received,
             (quarters, blocks_dev, quarter, hidden),
         )
         summed = edge_exchange(partial, quarters, True, 1)
@@ -268,7 +258,7 @@
         rounded = adjoint.astype(jnp.bfloat16).reshape(1, blocks_dev, quarter, hidden)
         whole_rows = edge_exchange(rounded, quarters, False, 2)
         slot_sums = block_apply(
-            backward_kernel, group_row, member, member_slot, weights, whole_rows,
+            backward_kernel, group_row, member, member_slot, weights_g, whole_rows,
             (slot_total, quarter, hidden),
         )
         arrived = lax.all_to_all(

time: 348 us -> 335 us (0.963)
  Pallas kernels: 147 us -> 123 us
  local copies, waits for them, and re-layouts: 11.8 us -> 23.1 us
    pallas_call x4, Pallas kernels: 78.6 us -> 54.8 us  [block_apply(): pl.pallas_call(kernel, out_shape=jax.ShapeDtypeStruct(out_shape, jnp.floa...]
    gather x0 -> x1, local copies, waits for them, and re-layouts: none -> 11.1 us  [per_device(): jnp.take(weights, member, axis=0, mode='clip')]
    all_to_all x2, waiting for transfers between devices: 56.4 us -> 66 us  [per_device(): lax.all_to_all(slot_sums, ('x', 'c'), split_axis=0, concat_axis=0, tiled=...]
    all_gather x2, waiting for transfers between devices: 15.4 us -> 6.64 us  [per_device(): line_blocks = lax.all_gather(rounded, 'z', axis=0, tiled=True)]
  transfers between devices with their start and end apart: 7 -> 7, of which waited for: 4 -> 4; matrix products, arithmetic and copies ran while one was open for 4% -> 4% of each run, Pallas kernels for 33% -> 28%
where the time goes in v4:
time: 335 us; the launch traced here: 334 us
  Pallas kernels  123 us (37%)
  waiting for transfers between devices  102 us (30%)
  blocking collectives  35.4 us (11%)
  local copies, waits for them, and re-layouts  23.1 us (7%)
  starting transfers between devices  21.3 us (6%)
  other arithmetic  14.4 us (4%)
  between operations  13.9 us (4%)
    all_to_all x2, waiting for transfers between devices, per_device(): lax.all_to_all(slot_sums, ('x', 'c'), split_axis=0, concat_axis=0, tiled=...  66 us
    pallas_call x4, Pallas kernels, block_apply(): pl.pallas_call(kernel, out_shape=jax.ShapeDtypeStruct(out_shape, jnp.floa...  54.8 us
    pallas_call x4, Pallas kernels, edge_exchange(): pl.pallas_call(functools.partial(edge_exchange_kernel, reduce), out_shape...  54.8 us
    all_to_all x1, blocking collectives, per_device(): lax.all_to_all(outgoing, ('x', 'c'), split_axis=0, concat_axis=0, tiled=T...  35.4 us
    reduce_scatter x2, waiting for transfers between devices, per_device(): owned = lax.psum_scatter(dense, 'z', scatter_dimension=0, tiled=True)  29.5 us
    all_to_all x2, starting transfers between devices, per_device(): lax.all_to_all(slot_sums, ('x', 'c'), split_axis=0, concat_axis=0, tiled=...  16.9 us
    pallas_call x2, Pallas kernels, combine_apply(): pl.pallas_call(combine_kernel, out_shape=jax.ShapeDtypeStruct((lines, blo...  13 us
    gather x1, local copies, waits for them, and re-layouts, per_device(): jnp.take(weights, member, axis=0, mode='clip')  11.1 us
  transfers between devices with their start and end apart: 7, of which 4 were waited for; matrix products, arithmetic and copies ran while one was open for 4% of the time, Pallas kernels for 28%

profile of v4, /device:TPU:1, one launch (start us, length us, event | category | flops | bytes accessed | tf_op | source)
XLA Modules:
  0.0 334.0 jit_solution(18050390901870230090)
XLA Ops:
  7.2 0.0 copy-start
  7.2 0.8 convert_reduce_fusion
  8.0 0.9 fusion
  8.9 0.2 reduce-window.7
  9.1 0.1 convert_reduce_fusion.1
  9.2 0.6 broadcast_minimum_fusion.rows_ref
  9.8 0.8 select_reduce_fusion
  10.6 0.7 fusion.7
  11.3 1.2 scatter_custom_fusion.members_ref
  12.5 0.0 copy-start.5
  12.5 1.6 convert_element_type.73
  14.1 11.7 %shard_map.81.a_ref = bf16[4,8,64,128]{3,2,1,0:T(8,128)(2,1)} custom-call(bf16[1,8,64,128]{3,2,1,0:T(8,128)(2,1)} %bitcast.41), custom_call_target="tpu_custom_call" | custom-call | tf_op jit(solution)/shard_map/pallas_call | solution.py:133
  25.9 2.5 gather_fusion
  28.4 11.1 %gather_fusion.1 = bf16[224,64,256]{2,1,0:T(8,128)(2,1)} fusion(bf16[192,64,256]{2,1,0:T(8,128)(2,1)} %bitcast.40, s32[1024]{0:T(1024)S(1)} %pad_clamp_fusion.1), kind=kCustom, calls=%fused_computation.3 | custom fusion | bytes 14680960 | tf_op jit(solution)/shard_map/jit(_take)/gather | solution.py:235
  39.5 0.0 copy-done.5
  39.5 17.2 %shard_map.82 = f32[128,64,128]{2,1,0:T(8,128)} custom-call(s32[56]{0:T(128)} %broadcast_minimum_fusion.rows_ref, s32[224]{0:T(256)} %copy-done.5, s32[224]{0:T(256)} %gather_fusion, bf16[56,256,256]{2,1,0:T(8,128)(2,1)} %bitcast.36, bf16[4,8,64,128]{3,2,1,0:T(8,128)(2,1)} %shard_map.81.a_ref), custom_call_target="tpu_custom_call" | custom-call | tf_op jit(solution)/shard_map/pallas_call | solution.py:149
  56.7 6.6 %all-to-all-start.2 = ((f32[128,64,128]{2,1,0:T(8,128)}), f32[128,64,128]{2,1,0:T(8,128)}, u32[]{:S(2)}, u32[]{:S(2)}) async-start(f32[128,64,128]{2,1,0:T(8,128)} %shard_map.82), calls=%async_computation.2 | async-start | bytes 8388608 | tf_op jit(solution)/shard_map/all_to_all | solution.py:264
  63.3 0.0 all-gather.3.cloned.1.call-start
  63.3 0.0 copy-done.2
  63.3 0.7 convert_element_type.71
  63.9 0.0 all-gather.3.cloned.1.call-update
  64.0 0.0 reduce-scatter.3.cloned.1.call-start
  64.1 0.1 fusion.3
  64.2 0.1 broadcast_or_fusion
  64.2 0.1 reshape.247
  64.4 0.0 copy-done
  64.4 1.8 gather_fusion.2
  66.2 46.0 %all-to-all-done.2.arrived_ref = f32[128,64,128]{2,1,0:T(8,128)} async-done(((f32[128,64,128]{2,1,0:T(8,128)}), f32[128,64,128]{2,1,0:T(8,128)}, u32[]{:S(2)}, u32[]{:S(2)}) %all-to-all-start.2) | async-done | bytes 4194336 | tf_op jit(solution)/shard_map/all_to_all | solution.py:264
  112.2 6.5 %shard_map.83 = f32[8,8,64,128]{3,2,1,0:T(8,128)} custom-call(s32[128]{0:T(128)} %gather_fusion.2, f32[128,64,128]{2,1,0:T(8,128)} %all-to-all-done.2.arrived_ref), custom_call_target="tpu_custom_call" | custom-call | tf_op jit(solution)/shard_map/pallas_call | solution.py:168
  118.7 0.0 reduce-scatter.3.cloned.1.call-update
  118.7 0.1 add.205
  118.8 0.1 add.206
  118.9 0.4 copy-done.3
  119.4 0.0 all-gather.3.cloned.1.call-done
  119.4 2.2 gather_fusion.3
  121.6 1.7 broadcast_select_fusion
  123.3 4.3 %all-to-all-start = ((bf16[128,64,128]{2,1,0:T(8,128)(2,1)}), bf16[128,64,128]{2,1,0:T(8,128)(2,1)S(1)}, u32[]{:S(2)}, u32[]{:S(2)}) async-start(bf16[128,64,128]{2,1,0:T(8,128)(2,1)} %broadcast_select_fusion), calls=%async_computation | async-start | bytes 4194304 | tf_op jit(solution)/shard_map/all_to_all | solution.py:245
  127.6 29.5 %reduce-scatter.3.cloned.1.call-done = f32[1,8,64,128]{3,2,1,0:T(8,128)} async-done(((f32[8,8,64,128]{3,2,1,0:T(8,128)}), f32[1,8,64,128]{3,2,1,0:T(8,128)}) %reduce-scatter.3.cloned.1.call-update) | async-done | bytes 262160 | tf_op jit(solution)/shard_map/reduce_scatter | solution.py:268
  157.1 1.7 broadcast_multiply_fusion.1
  158.8 9.5 %shard_map.84.a_ref = bf16[4,8,64,128]{3,2,1,0:T(8,128)(2,1)} custom-call(bf16[1,8,64,128]{3,2,1,0:T(8,128)(2,1)} %get-tuple-element.6.x_ref), custom_call_target="tpu_custom_call" | custom-call | tf_op jit(solution)/shard_map/pallas_call | solution.py:133
  168.3 17.2 %shard_map.85 = f32[128,64,128]{2,1,0:T(8,128)} custom-call(s32[56]{0:T(128)} %broadcast_minimum_fusion.rows_ref, s32[224]{0:T(256)} %copy-done.5, s32[224]{0:T(256)} %gather_fusion, bf16[56,256,256]{2,1,0:T(8,128)(2,1)} %bitcast.37, bf16[4,8,64,128]{3,2,1,0:T(8,128)(2,1)} %shard_map.84.a_ref), custom_call_target="tpu_custom_call" | custom-call | tf_op jit(solution)/shard_map/pallas_call | solution.py:149
  185.5 0.0 all-to-all-done.x_ref
  185.5 1.3 copy-done.1
  186.8 10.3 %all-to-all-start.3 = ((f32[128,64,128]{2,1,0:T(8,128)}), f32[128,64,128]{2,1,0:T(8,128)}, u32[]{:S(2)}, u32[]{:S(2)}) async-start(f32[128,64,128]{2,1,0:T(8,128)} %shard_map.85), calls=%async_computation.4 | async-start | bytes 8388608 | tf_op jit(solution)/shard_map/all_to_all | solution.py:264
  197.1 0.0 all-gather.5.cloned.1.call-start
  197.1 10.2 %shard_map.77.x_ref = f32[4,8,64,128]{3,2,1,0:T(8,128)} custom-call(s32[56]{0:T(128)} %broadcast_minimum_fusion.rows_ref, s32[224]{0:T(256)} %copy-done.5, s32[224]{0:T(256)} %gather_fusion, bf16[56,256,256]{2,1,0:T(8,128)(2,1)} %bitcast.38, bf16[128,64,128]{2,1,0:T(8,128)(2,1)} %copy-done.1), custom_call_target="tpu_custom_call" | custom-call | tf_op jit(solution)/shard_map/pallas_call | solution.py:149
  207.3 16.9 %shard_map.78 = f32[8,64,128]{2,1,0:T(8,128)} custom-call(f32[4,8,64,128]{3,2,1,0:T(8,128)} %shard_map.77.x_ref), custom_call_target="tpu_custom_call" | custom-call | tf_op jit(solution)/shard_map/pallas_call | solution.py:133
  224.2 1.0 broadcast_multiply_fusion.3
  225.2 0.7 fusion.1
  225.9 0.0 all-gather.5.cloned.1.call-update
  225.9 0.0 reduce-scatter.5.cloned.1.call-start
  226.0 20.0 %all-to-all-done.3.arrived_ref = f32[128,64,128]{2,1,0:T(8,128)} async-done(((f32[128,64,128]{2,1,0:T(8,128)}), f32[128,64,128]{2,1,0:T(8,128)}, u32[]{:S(2)}, u32[]{:S(2)}) %all-to-all-start.3) | async-done | bytes 4194336 | tf_op jit(solution)/shard_map/all_to_all | solution.py:264
  246.0 6.6 %shard_map.86 = f32[8,8,64,128]{3,2,1,0:T(8,128)} custom-call(s32[128]{0:T(128)} %gather_fusion.2, f32[128,64,128]{2,1,0:T(8,128)} %all-to-all-done.3.arrived_ref), custom_call_target="tpu_custom_call" | custom-call | tf_op jit(solution)/shard_map/pallas_call | solution.py:168
  252.6 0.0 reduce-scatter.5.cloned.1.call-update
  252.6 6.6 %all-gather.5.cloned.1.call-done = bf16[64,64,128]{2,1,0:T(8,128)(2,1)} async-done(((bf16[8,64,128]{2,1,0:T(8,128)(2,1)}), bf16[64,64,128]{2,1,0:T(8,128)(2,1)}) %all-gather.5.cloned.1.call-update) | async-done | bytes 1048592 | tf_op jit(solution)/shard_map/all_gather | solution.py:243
  259.2 2.2 gather_fusion.4
  261.4 0.3 broadcast_select_fusion.1
  261.7 35.4 %all_to_all.20.x_ref = bf16[128,64,128]{2,1,0:T(8,128)(2,1)} all-to-all(bf16[128,64,128]{2,1,0:T(8,128)(2,1)S(1)} %broadcast_select_fusion.1), channel_id=1, replica_groups=mesh['z'=8,'x'=4,'c'=2,'edge'=4] {'x','c'}, dimensions={0} | all-to-all | bytes 4194304 | tf_op jit(solution)/shard_map/all_to_all | solution.py:245
  297.1 10.2 %shard_map.79.x_ref = f32[4,8,64,128]{3,2,1,0:T(8,128)} custom-call(s32[56]{0:T(128)} %broadcast_minimum_fusion.rows_ref, s32[224]{0:T(256)} %copy-done.5, s32[224]{0:T(256)} %gather_fusion, bf16[56,256,256]{2,1,0:T(8,128)(2,1)} %bitcast.39, bf16[128,64,128]{2,1,0:T(8,128)(2,1)} %all_to_all.20.x_ref), custom_call_target="tpu_custom_call" | custom-call | tf_op jit(solution)/shard_map/pallas_call | solution.py:149
  307.4 16.7 %shard_map.80 = f32[8,64,128]{2,1,0:T(8,128)} custom-call(f32[4,8,64,128]{3,2,1,0:T(8,128)} %shard_map.79.x_ref), custom_call_target="tpu_custom_call" | custom-call | tf_op jit(solution)/shard_map/pallas_call | solution.py:133
  324.0 1.0 broadcast_multiply_fusion.2
  325.0 0.7 bitcast_add_fusion.2
  325.8 1.0 broadcast_multiply_fusion
  326.7 0.7 bitcast_add_fusion
  (17 shorter events, 0.1 us)
Async XLA Ops:
  7.2 57.2 %copy-start = (s32[64,128]{1,0:T(8,128)S(1)}, s32[64,128]{1,0:T(8,128)}, u32[]{:S(2)}) copy-start(s32[64,128]{1,0:T(8,128)} %param.10) | copy-start | bytes 98308
  12.5 27.0 %copy-start.5 = (s32[224]{0:T(256)}, s32[224]{0:T(256)S(1)}, u32[]{:S(2)}) copy-start(s32[224]{0:T(256)S(1)} %scatter_custom_fusion.members_ref) | copy-start | bytes 2692
  56.7 6.6 %copy-start.2 = (f32[512,128]{1,0:T(8,128)S(1)}, f32[512,128]{1,0:T(8,128)}, u32[]{:S(2)}) copy-start(f32[512,128]{1,0:T(8,128)} %param.8) | copy-start | bytes 786436
  56.7 55.5 %all-to-all-start.2 = ((f32[128,64,128]{2,1,0:T(8,128)}), f32[128,64,128]{2,1,0:T(8,128)}, u32[]{:S(2)}, u32[]{:S(2)}) async-start(f32[128,64,128]{2,1,0:T(8,128)} %shard_map.82), calls=%async_computation.2 | async-start | bytes 8388608 | tf_op jit(solution)/shard_map/all_to_all | solution.py:264
  63.3 56.1 %all-gather.3.cloned.1.call-start = ((), (), s32[]{:S(2)}) async-start(), calls=%async_computation.6 | async-start | bytes 1179648 | tf_op jit(solution)/shard_map/all_gather | solution.py:243
  64.0 93.1 %reduce-scatter.3.cloned.1.call-start = ((), (), s32[]{:S(2)}) async-start(), calls=%async_computation.8 | async-start | bytes 2359296 | tf_op jit(solution)/shard_map/reduce_scatter | solution.py:268
  118.7 0.7 copy-start.3
  123.3 62.3 %all-to-all-start = ((bf16[128,64,128]{2,1,0:T(8,128)(2,1)}), bf16[128,64,128]{2,1,0:T(8,128)(2,1)S(1)}, u32[]{:S(2)}, u32[]{:S(2)}) async-start(bf16[128,64,128]{2,1,0:T(8,128)(2,1)} %broadcast_select_fusion), calls=%async_computation | async-start | bytes 4194304 | tf_op jit(solution)/shard_map/all_to_all | solution.py:245
  185.5 1.3 copy-start.1
  186.8 59.2 %all-to-all-start.3 = ((f32[128,64,128]{2,1,0:T(8,128)}), f32[128,64,128]{2,1,0:T(8,128)}, u32[]{:S(2)}, u32[]{:S(2)}) async-start(f32[128,64,128]{2,1,0:T(8,128)} %shard_map.85), calls=%async_computation.4 | async-start | bytes 8388608 | tf_op jit(solution)/shard_map/all_to_all | solution.py:264
  197.1 62.1 %all-gather.5.cloned.1.call-start = ((), (), s32[]{:S(2)}) async-start(), calls=%async_computation.7 | async-start | bytes 1179648 | tf_op jit(solution)/shard_map/all_gather | solution.py:243
  225.9 99.8 %reduce-scatter.5.cloned.1.call-start = ((), (), s32[]{:S(2)}) async-start(), calls=%async_computation.9 | async-start | bytes 2359296 | tf_op jit(solution)/shard_map/reduce_scatter | solution.py:268
  307.4 19.4 %copy-start.4 = (f32[512,128]{1,0:T(8,128)S(1)}, f32[512,128]{1,0:T(8,128)}, u32[]{:S(2)}) copy-start(f32[512,128]{1,0:T(8,128)} %param.9) | copy-start | bytes 786436
Sparse Core Ops, SparseCore 0:
  66.5 36.7 all-gather.2
  118.8 38.2 reduce-scatter.2
  226.0 33.1 all-gather.4
  261.6 40.7 reduce-scatter.4

commit v5 on v4

--- a/solution.py
+++ b/solution.py
@@ -67,10 +67,9 @@
         product = jnp.dot(weights, sources, preferred_element_type=jnp.float32)
         for m in range(GROUP):
             s = slots_ref[g * GROUP + m]
-
-            @pl.when(members_ref[g * GROUP + m] < block_count)
-            def _():
-                out_ref[s] += product[m * quarter:(m + 1) * quarter]
+            piece = product[m * quarter:(m + 1) * quarter]
+            valid = members_ref[g * GROUP + m] < block_count
+            out_ref[s] += jnp.where(valid, piece, jnp.zeros_like(piece))
 
         return carry
 
@@ -83,10 +82,8 @@
 
     def body(q, carry):
         j = want_ref[q]
-
-        @pl.when(j >= 0)
-        def _():
-            out_ref[q // CAP % lines, j] += arrived_ref[q]
+        piece = arrived_ref[q]
+        out_ref[q // CAP % lines, jnp.maximum(j, 0)] += jnp.where(j >= 0, piece, jnp.zeros_like(piece))
 
         return carry
 

time: 335 us -> 321 us (0.958)
  Pallas kernels: 123 us -> 108 us
    pallas_call x4, Pallas kernels: 54.8 us -> 41.8 us  [block_apply(): pl.pallas_call(kernel, out_shape=jax.ShapeDtypeStruct(out_shape, jnp.floa...]
  transfers between devices with their start and end apart: 7 -> 7, of which waited for: 4 -> 4; matrix products, arithmetic and copies ran while one was open for 4% -> 5% of each run, Pallas kernels for 28% -> 27%
where the time goes in v5:
time: 321 us; the launch traced here: 320 us
  Pallas kernels  108 us (34%)
  waiting for transfers between devices  103 us (32%)
  blocking collectives  35.4 us (11%)
  local copies, waits for them, and re-layouts  23.1 us (7%)
  starting transfers between devices  21.3 us (7%)
  other arithmetic  14.4 us (4%)
  between operations  13.9 us (4%)
    all_to_all x2, waiting for transfers between devices, per_device(): lax.all_to_all(slot_sums, ('x', 'c'), split_axis=0, concat_axis=0, tiled=...  66 us
    pallas_call x4, Pallas kernels, edge_exchange(): pl.pallas_call(functools.partial(edge_exchange_kernel, reduce), out_shape...  54.7 us
    pallas_call x4, Pallas kernels, block_apply(): pl.pallas_call(kernel, out_shape=jax.ShapeDtypeStruct(out_shape, jnp.floa...  41.8 us
    all_to_all x1, blocking collectives, per_device(): lax.all_to_all(outgoing, ('x', 'c'), split_axis=0, concat_axis=0, tiled=T...  35.4 us
    reduce_scatter x2, waiting for transfers between devices, per_device(): owned = lax.psum_scatter(dense, 'z', scatter_dimension=0, tiled=True)  29.4 us
    all_to_all x2, starting transfers between devices, per_device(): lax.all_to_all(slot_sums, ('x', 'c'), split_axis=0, concat_axis=0, tiled=...  16.8 us
    pallas_call x2, Pallas kernels, combine_apply(): pl.pallas_call(combine_kernel, out_shape=jax.ShapeDtypeStruct((lines, blo...  11.4 us
    gather x1, local copies, waits for them, and re-layouts, per_device(): jnp.take(weights, member, axis=0, mode='clip')  11.1 us
  transfers between devices with their start and end apart: 7, of which 4 were waited for; matrix products, arithmetic and copies ran while one was open for 5% of the time, Pallas kernels for 27%

profile of v5, /device:TPU:1, one launch (start us, length us, event | category | flops | bytes accessed | tf_op | source)
XLA Modules:
  0.0 319.9 jit_solution(9602150288846013511)
XLA Ops:
  7.2 0.0 copy-start
  7.2 0.8 convert_reduce_fusion
  8.0 0.9 fusion
  8.9 0.2 reduce-window.7
  9.1 0.1 convert_reduce_fusion.1
  9.2 0.6 broadcast_minimum_fusion.rows_ref
  9.8 0.8 select_reduce_fusion
  10.6 0.7 fusion.7
  11.3 1.2 scatter_custom_fusion.members_ref
  12.5 0.0 copy-start.5
  12.5 1.6 convert_element_type.73
  14.1 11.7 %shard_map.81.a_ref = bf16[4,8,64,128]{3,2,1,0:T(8,128)(2,1)} custom-call(bf16[1,8,64,128]{3,2,1,0:T(8,128)(2,1)} %bitcast.41), custom_call_target="tpu_custom_call" | custom-call | tf_op jit(solution)/shard_map/pallas_call | solution.py:130
  25.9 2.5 gather_fusion
  28.4 11.1 %gather_fusion.1 = bf16[224,64,256]{2,1,0:T(8,128)(2,1)} fusion(bf16[192,64,256]{2,1,0:T(8,128)(2,1)} %bitcast.40, s32[1024]{0:T(1024)S(1)} %pad_clamp_fusion.1), kind=kCustom, calls=%fused_computation.3 | custom fusion | bytes 14680960 | tf_op jit(solution)/shard_map/jit(_take)/gather | solution.py:232
  39.5 0.0 copy-done.5
  39.5 10.6 %shard_map.82 = f32[128,64,128]{2,1,0:T(8,128)} custom-call(s32[56]{0:T(128)} %broadcast_minimum_fusion.rows_ref, s32[224]{0:T(256)} %copy-done.5, s32[224]{0:T(256)} %gather_fusion, bf16[56,256,256]{2,1,0:T(8,128)(2,1)} %bitcast.36, bf16[4,8,64,128]{3,2,1,0:T(8,128)(2,1)} %shard_map.81.a_ref), custom_call_target="tpu_custom_call" | custom-call | tf_op jit(solution)/shard_map/pallas_call | solution.py:146
  50.1 6.6 %all-to-all-start.2 = ((f32[128,64,128]{2,1,0:T(8,128)}), f32[128,64,128]{2,1,0:T(8,128)}, u32[]{:S(2)}, u32[]{:S(2)}) async-start(f32[128,64,128]{2,1,0:T(8,128)} %shard_map.82), calls=%async_computation.2 | async-start | bytes 8388608 | tf_op jit(solution)/shard_map/all_to_all | solution.py:261
  56.7 0.0 all-gather.3.cloned.1.call-start
  56.7 0.0 copy-done.2
  56.7 0.7 convert_element_type.71
  57.4 0.0 all-gather.3.cloned.1.call-update
  57.5 0.0 reduce-scatter.3.cloned.1.call-start
  57.5 0.1 fusion.3
  57.6 0.1 broadcast_or_fusion
  57.7 0.1 reshape.247
  57.8 0.0 copy-done
  57.8 1.8 gather_fusion.2
  59.7 46.0 %all-to-all-done.2.arrived_ref = f32[128,64,128]{2,1,0:T(8,128)} async-done(((f32[128,64,128]{2,1,0:T(8,128)}), f32[128,64,128]{2,1,0:T(8,128)}, u32[]{:S(2)}, u32[]{:S(2)}) %all-to-all-start.2) | async-done | bytes 4194336 | tf_op jit(solution)/shard_map/all_to_all | solution.py:261
  105.7 5.6 %shard_map.83 = f32[8,8,64,128]{3,2,1,0:T(8,128)} custom-call(s32[128]{0:T(128)} %gather_fusion.2, f32[128,64,128]{2,1,0:T(8,128)} %all-to-all-done.2.arrived_ref), custom_call_target="tpu_custom_call" | custom-call | tf_op jit(solution)/shard_map/pallas_call | solution.py:165
  111.3 0.0 reduce-scatter.3.cloned.1.call-update
  111.3 0.1 add.205
  111.4 0.1 add.206
  111.6 0.4 copy-done.3
  112.0 0.0 all-gather.3.cloned.1.call-done
  112.0 2.2 gather_fusion.3
  114.2 1.7 broadcast_select_fusion
  115.9 4.4 %all-to-all-start = ((bf16[128,64,128]{2,1,0:T(8,128)(2,1)}), bf16[128,64,128]{2,1,0:T(8,128)(2,1)S(1)}, u32[]{:S(2)}, u32[]{:S(2)}) async-start(bf16[128,64,128]{2,1,0:T(8,128)(2,1)} %broadcast_select_fusion), calls=%async_computation | async-start | bytes 4194304 | tf_op jit(solution)/shard_map/all_to_all | solution.py:242
  120.3 29.4 %reduce-scatter.3.cloned.1.call-done = f32[1,8,64,128]{3,2,1,0:T(8,128)} async-done(((f32[8,8,64,128]{3,2,1,0:T(8,128)}), f32[1,8,64,128]{3,2,1,0:T(8,128)}) %reduce-scatter.3.cloned.1.call-update) | async-done | bytes 262160 | tf_op jit(solution)/shard_map/reduce_scatter | solution.py:265
  149.7 1.7 broadcast_multiply_fusion.1
  151.4 9.4 %shard_map.84.a_ref = bf16[4,8,64,128]{3,2,1,0:T(8,128)(2,1)} custom-call(bf16[1,8,64,128]{3,2,1,0:T(8,128)(2,1)} %get-tuple-element.6.x_ref), custom_call_target="tpu_custom_call" | custom-call | tf_op jit(solution)/shard_map/pallas_call | solution.py:130
  160.8 10.7 %shard_map.85 = f32[128,64,128]{2,1,0:T(8,128)} custom-call(s32[56]{0:T(128)} %broadcast_minimum_fusion.rows_ref, s32[224]{0:T(256)} %copy-done.5, s32[224]{0:T(256)} %gather_fusion, bf16[56,256,256]{2,1,0:T(8,128)(2,1)} %bitcast.37, bf16[4,8,64,128]{3,2,1,0:T(8,128)(2,1)} %shard_map.84.a_ref), custom_call_target="tpu_custom_call" | custom-call | tf_op jit(solution)/shard_map/pallas_call | solution.py:146
  171.5 0.0 all-to-all-done.x_ref
  171.5 1.3 copy-done.1
  172.8 10.2 %all-to-all-start.3 = ((f32[128,64,128]{2,1,0:T(8,128)}), f32[128,64,128]{2,1,0:T(8,128)}, u32[]{:S(2)}, u32[]{:S(2)}) async-start(f32[128,64,128]{2,1,0:T(8,128)} %shard_map.85), calls=%async_computation.4 | async-start | bytes 8388608 | tf_op jit(solution)/shard_map/all_to_all | solution.py:261
  183.0 0.0 all-gather.5.cloned.1.call-start
  183.0 10.2 %shard_map.77.x_ref = f32[4,8,64,128]{3,2,1,0:T(8,128)} custom-call(s32[56]{0:T(128)} %broadcast_minimum_fusion.rows_ref, s32[224]{0:T(256)} %copy-done.5, s32[224]{0:T(256)} %gather_fusion, bf16[56,256,256]{2,1,0:T(8,128)(2,1)} %bitcast.38, bf16[128,64,128]{2,1,0:T(8,128)(2,1)} %copy-done.1), custom_call_target="tpu_custom_call" | custom-call | tf_op jit(solution)/shard_map/pallas_call | solution.py:146
  193.2 16.9 %shard_map.78 = f32[8,64,128]{2,1,0:T(8,128)} custom-call(f32[4,8,64,128]{3,2,1,0:T(8,128)} %shard_map.77.x_ref), custom_call_target="tpu_custom_call" | custom-call | tf_op jit(solution)/shard_map/pallas_call | solution.py:130
  210.1 1.0 broadcast_multiply_fusion.3
  211.1 0.7 fusion.1
  211.8 0.0 all-gather.5.cloned.1.call-update
  211.8 0.0 reduce-scatter.5.cloned.1.call-start
  211.8 20.0 %all-to-all-done.3.arrived_ref = f32[128,64,128]{2,1,0:T(8,128)} async-done(((f32[128,64,128]{2,1,0:T(8,128)}), f32[128,64,128]{2,1,0:T(8,128)}, u32[]{:S(2)}, u32[]{:S(2)}) %all-to-all-start.3) | async-done | bytes 4194336 | tf_op jit(solution)/shard_map/all_to_all | solution.py:261
  231.9 5.8 %shard_map.86 = f32[8,8,64,128]{3,2,1,0:T(8,128)} custom-call(s32[128]{0:T(128)} %gather_fusion.2, f32[128,64,128]{2,1,0:T(8,128)} %all-to-all-done.3.arrived_ref), custom_call_target="tpu_custom_call" | custom-call | tf_op jit(solution)/shard_map/pallas_call | solution.py:165
  237.6 0.0 reduce-scatter.5.cloned.1.call-update
  237.7 7.4 %all-gather.5.cloned.1.call-done = bf16[64,64,128]{2,1,0:T(8,128)(2,1)} async-done(((bf16[8,64,128]{2,1,0:T(8,128)(2,1)}), bf16[64,64,128]{2,1,0:T(8,128)(2,1)}) %all-gather.5.cloned.1.call-update) | async-done | bytes 1048592 | tf_op jit(solution)/shard_map/all_gather | solution.py:240
  245.1 2.2 gather_fusion.4
  247.3 0.3 broadcast_select_fusion.1
  247.5 35.4 %all_to_all.20.x_ref = bf16[128,64,128]{2,1,0:T(8,128)(2,1)} all-to-all(bf16[128,64,128]{2,1,0:T(8,128)(2,1)S(1)} %broadcast_select_fusion.1), channel_id=1, replica_groups=mesh['z'=8,'x'=4,'c'=2,'edge'=4] {'x','c'}, dimensions={0} | all-to-all | bytes 4194304 | tf_op jit(solution)/shard_map/all_to_all | solution.py:242
  283.0 10.2 %shard_map.79.x_ref = f32[4,8,64,128]{3,2,1,0:T(8,128)} custom-call(s32[56]{0:T(128)} %broadcast_minimum_fusion.rows_ref, s32[224]{0:T(256)} %copy-done.5, s32[224]{0:T(256)} %gather_fusion, bf16[56,256,256]{2,1,0:T(8,128)(2,1)} %bitcast.39, bf16[128,64,128]{2,1,0:T(8,128)(2,1)} %all_to_all.20.x_ref), custom_call_target="tpu_custom_call" | custom-call | tf_op jit(solution)/shard_map/pallas_call | solution.py:146
  293.2 16.7 %shard_map.80 = f32[8,64,128]{2,1,0:T(8,128)} custom-call(f32[4,8,64,128]{3,2,1,0:T(8,128)} %shard_map.79.x_ref), custom_call_target="tpu_custom_call" | custom-call | tf_op jit(solution)/shard_map/pallas_call | solution.py:130
  309.9 1.0 broadcast_multiply_fusion.2
  310.9 0.7 bitcast_add_fusion.2
  311.6 1.0 broadcast_multiply_fusion
  312.6 0.7 bitcast_add_fusion
  (17 shorter events, 0.1 us)
Async XLA Ops:
  7.2 50.7 %copy-start = (s32[64,128]{1,0:T(8,128)S(1)}, s32[64,128]{1,0:T(8,128)}, u32[]{:S(2)}) copy-start(s32[64,128]{1,0:T(8,128)} %param.10) | copy-start | bytes 98308
  12.5 27.0 %copy-start.5 = (s32[224]{0:T(256)}, s32[224]{0:T(256)S(1)}, u32[]{:S(2)}) copy-start(s32[224]{0:T(256)S(1)} %scatter_custom_fusion.members_ref) | copy-start | bytes 2692
  50.1 6.6 %copy-start.2 = (f32[512,128]{1,0:T(8,128)S(1)}, f32[512,128]{1,0:T(8,128)}, u32[]{:S(2)}) copy-start(f32[512,128]{1,0:T(8,128)} %param.8) | copy-start | bytes 786436
  50.1 55.5 %all-to-all-start.2 = ((f32[128,64,128]{2,1,0:T(8,128)}), f32[128,64,128]{2,1,0:T(8,128)}, u32[]{:S(2)}, u32[]{:S(2)}) async-start(f32[128,64,128]{2,1,0:T(8,128)} %shard_map.82), calls=%async_computation.2 | async-start | bytes 8388608 | tf_op jit(solution)/shard_map/all_to_all | solution.py:261
  56.7 55.3 %all-gather.3.cloned.1.call-start = ((), (), s32[]{:S(2)}) async-start(), calls=%async_computation.6 | async-start | bytes 1179648 | tf_op jit(solution)/shard_map/all_gather | solution.py:240
  57.5 92.3 %reduce-scatter.3.cloned.1.call-start = ((), (), s32[]{:S(2)}) async-start(), calls=%async_computation.8 | async-start | bytes 2359296 | tf_op jit(solution)/shard_map/reduce_scatter | solution.py:265
  111.3 0.7 copy-start.3
  115.9 55.6 %all-to-all-start = ((bf16[128,64,128]{2,1,0:T(8,128)(2,1)}), bf16[128,64,128]{2,1,0:T(8,128)(2,1)S(1)}, u32[]{:S(2)}, u32[]{:S(2)}) async-start(bf16[128,64,128]{2,1,0:T(8,128)(2,1)} %broadcast_select_fusion), calls=%async_computation | async-start | bytes 4194304 | tf_op jit(solution)/shard_map/all_to_all | solution.py:242
  171.5 1.3 copy-start.1
  172.8 59.1 %all-to-all-start.3 = ((f32[128,64,128]{2,1,0:T(8,128)}), f32[128,64,128]{2,1,0:T(8,128)}, u32[]{:S(2)}, u32[]{:S(2)}) async-start(f32[128,64,128]{2,1,0:T(8,128)} %shard_map.85), calls=%async_computation.4 | async-start | bytes 8388608 | tf_op jit(solution)/shard_map/all_to_all | solution.py:261
  183.0 62.1 %all-gather.5.cloned.1.call-start = ((), (), s32[]{:S(2)}) async-start(), calls=%async_computation.7 | async-start | bytes 1179648 | tf_op jit(solution)/shard_map/all_gather | solution.py:240
  211.8 99.8 %reduce-scatter.5.cloned.1.call-start = ((), (), s32[]{:S(2)}) async-start(), calls=%async_computation.9 | async-start | bytes 2359296 | tf_op jit(solution)/shard_map/reduce_scatter | solution.py:265
  293.2 19.4 %copy-start.4 = (f32[512,128]{1,0:T(8,128)S(1)}, f32[512,128]{1,0:T(8,128)}, u32[]{:S(2)}) copy-start(f32[512,128]{1,0:T(8,128)} %param.9) | copy-start | bytes 786436
Sparse Core Ops, SparseCore 0:
  59.9 36.7 all-gather.2
  111.5 38.2 reduce-scatter.2
  211.9 33.1 all-gather.4
  247.5 41.1 reduce-scatter.4

commit v6 on v5

--- a/solution.py
+++ b/solution.py
@@ -16,7 +16,7 @@
 X_SIZE = 4
 CORE_SIZE = 2
 GROUP = 4
-GROUPS_PER_STEP = 8
+GROUPS_PER_STEP = 14
 BLOCKS = 192
 
 
@@ -46,7 +46,7 @@
         out_ref[:, j] += product.reshape(quarters, quarter, hidden)
         return carry
 
-    lax.fori_loop(0, GROUPS_PER_STEP, body, 0, unroll=4)
+    lax.fori_loop(0, GROUPS_PER_STEP, body, 0, unroll=7)
 
 
 def backward_kernel(rows_ref, members_ref, slots_ref, v_ref, a_ref, out_ref):
@@ -73,7 +73,7 @@
 
         return carry
 
-    lax.fori_loop(0, GROUPS_PER_STEP, body, 0, unroll=4)
+    lax.fori_loop(0, GROUPS_PER_STEP, body, 0, unroll=7)
 
 
 def combine_kernel(want_ref, arrived_ref, out_ref):

time: 321 us -> 313 us (0.975)
  Pallas kernels: 108 us -> 100 us
    pallas_call x4, Pallas kernels: 41.8 us -> 34.2 us  [block_apply(): pl.pallas_call(kernel, out_shape=jax.ShapeDtypeStruct(out_shape, jnp.floa...]
  transfers between devices with their start and end apart: 7 -> 7, of which waited for: 4 -> 4; matrix products, arithmetic and copies ran while one was open for 5% -> 5% of each run, Pallas kernels for 27% -> 26%
where the time goes in v6:
time: 313 us; the launch traced here: 312 us
  waiting for transfers between devices  103 us (33%)
  Pallas kernels  100 us (32%)
  blocking collectives  35.4 us (11%)
  local copies, waits for them, and re-layouts  23.1 us (7%)
  starting transfers between devices  21.5 us (7%)
  other arithmetic  14.4 us (5%)
  between operations  13.9 us (4%)
    all_to_all x2, waiting for transfers between devices, per_device(): lax.all_to_all(slot_sums, ('x', 'c'), split_axis=0, concat_axis=0, tiled=...  67.9 us
    pallas_call x4, Pallas kernels, edge_exchange(): pl.pallas_call(functools.partial(edge_exchange_kernel, reduce), out_shape...  54.7 us
    all_to_all x1, blocking collectives, per_device(): lax.all_to_all(outgoing, ('x', 'c'), split_axis=0, concat_axis=0, tiled=T...  35.4 us
    pallas_call x4, Pallas kernels, block_apply(): pl.pallas_call(kernel, out_shape=jax.ShapeDtypeStruct(out_shape, jnp.floa...  34.2 us
    reduce_scatter x2, waiting for transfers between devices, per_device(): owned = lax.psum_scatter(dense, 'z', scatter_dimension=0, tiled=True)  29.2 us
    all_to_all x2, starting transfers between devices, per_device(): lax.all_to_all(slot_sums, ('x', 'c'), split_axis=0, concat_axis=0, tiled=...  17 us
    pallas_call x2, Pallas kernels, combine_apply(): pl.pallas_call(combine_kernel, out_shape=jax.ShapeDtypeStruct((lines, blo...  11.4 us
    gather x1, local copies, waits for them, and re-layouts, per_device(): jnp.take(weights, member, axis=0, mode='clip')  11.1 us
  transfers between devices with their start and end apart: 7, of which 4 were waited for; matrix products, arithmetic and copies ran while one was open for 5% of the time, Pallas kernels for 26%

profile of v6, /device:TPU:1, one launch (start us, length us, event | category | flops | bytes accessed | tf_op | source)
XLA Modules:
  0.0 312.3 jit_solution(15446191404609415156)
XLA Ops:
  7.2 0.0 copy-start
  7.2 0.8 convert_reduce_fusion
  8.0 0.9 fusion
  8.9 0.2 reduce-window.7
  9.1 0.1 convert_reduce_fusion.1
  9.2 0.6 broadcast_minimum_fusion.rows_ref
  9.8 0.8 select_reduce_fusion
  10.6 0.7 fusion.7
  11.3 1.2 scatter_custom_fusion.members_ref
  12.5 0.0 copy-start.5
  12.5 1.6 convert_element_type.73
  14.1 11.7 %shard_map.81.a_ref = bf16[4,8,64,128]{3,2,1,0:T(8,128)(2,1)} custom-call(bf16[1,8,64,128]{3,2,1,0:T(8,128)(2,1)} %bitcast.41), custom_call_target="tpu_custom_call" | custom-call | tf_op jit(solution)/shard_map/pallas_call | solution.py:130
  25.9 2.5 gather_fusion
  28.4 11.1 %gather_fusion.1 = bf16[224,64,256]{2,1,0:T(8,128)(2,1)} fusion(bf16[192,64,256]{2,1,0:T(8,128)(2,1)} %bitcast.40, s32[1024]{0:T(1024)S(1)} %pad_clamp_fusion.1), kind=kCustom, calls=%fused_computation.3 | custom fusion | bytes 14680960 | tf_op jit(solution)/shard_map/jit(_take)/gather | solution.py:232
  39.5 0.0 copy-done.5
  39.5 8.8 %shard_map.82 = f32[128,64,128]{2,1,0:T(8,128)} custom-call(s32[56]{0:T(128)} %broadcast_minimum_fusion.rows_ref, s32[224]{0:T(256)} %copy-done.5, s32[224]{0:T(256)} %gather_fusion, bf16[56,256,256]{2,1,0:T(8,128)(2,1)} %bitcast.36, bf16[4,8,64,128]{3,2,1,0:T(8,128)(2,1)} %shard_map.81.a_ref), custom_call_target="tpu_custom_call" | custom-call | tf_op jit(solution)/shard_map/pallas_call | solution.py:146
  48.3 6.6 %all-to-all-start.2 = ((f32[128,64,128]{2,1,0:T(8,128)}), f32[128,64,128]{2,1,0:T(8,128)}, u32[]{:S(2)}, u32[]{:S(2)}) async-start(f32[128,64,128]{2,1,0:T(8,128)} %shard_map.82), calls=%async_computation.2 | async-start | bytes 8388608 | tf_op jit(solution)/shard_map/all_to_all | solution.py:261
  54.9 0.0 all-gather.3.cloned.1.call-start
  54.9 0.0 copy-done.2
  54.9 0.7 convert_element_type.71
  55.6 0.0 all-gather.3.cloned.1.call-update
  55.6 0.0 reduce-scatter.3.cloned.1.call-start
  55.7 0.1 fusion.3
  55.8 0.1 broadcast_or_fusion
  55.8 0.1 reshape.247
  56.0 0.0 copy-done
  56.0 1.8 gather_fusion.2
  57.8 46.0 %all-to-all-done.2.arrived_ref = f32[128,64,128]{2,1,0:T(8,128)} async-done(((f32[128,64,128]{2,1,0:T(8,128)}), f32[128,64,128]{2,1,0:T(8,128)}, u32[]{:S(2)}, u32[]{:S(2)}) %all-to-all-start.2) | async-done | bytes 4194336 | tf_op jit(solution)/shard_map/all_to_all | solution.py:261
  103.8 5.6 %shard_map.83 = f32[8,8,64,128]{3,2,1,0:T(8,128)} custom-call(s32[128]{0:T(128)} %gather_fusion.2, f32[128,64,128]{2,1,0:T(8,128)} %all-to-all-done.2.arrived_ref), custom_call_target="tpu_custom_call" | custom-call | tf_op jit(solution)/shard_map/pallas_call | solution.py:165
  109.5 0.0 reduce-scatter.3.cloned.1.call-update
  109.5 0.1 add.205
  109.6 0.1 add.206
  109.7 0.4 copy-done.3
  110.2 0.0 all-gather.3.cloned.1.call-done
  110.2 2.2 gather_fusion.3
  112.4 1.7 broadcast_select_fusion
  114.1 4.4 %all-to-all-start = ((bf16[128,64,128]{2,1,0:T(8,128)(2,1)}), bf16[128,64,128]{2,1,0:T(8,128)(2,1)S(1)}, u32[]{:S(2)}, u32[]{:S(2)}) async-start(bf16[128,64,128]{2,1,0:T(8,128)(2,1)} %broadcast_select_fusion), calls=%async_computation | async-start | bytes 4194304 | tf_op jit(solution)/shard_map/all_to_all | solution.py:242
  118.4 29.2 %reduce-scatter.3.cloned.1.call-done = f32[1,8,64,128]{3,2,1,0:T(8,128)} async-done(((f32[8,8,64,128]{3,2,1,0:T(8,128)}), f32[1,8,64,128]{3,2,1,0:T(8,128)}) %reduce-scatter.3.cloned.1.call-update) | async-done | bytes 262160 | tf_op jit(solution)/shard_map/reduce_scatter | solution.py:265
  147.6 1.7 broadcast_multiply_fusion.1
  149.3 9.4 %shard_map.84.a_ref = bf16[4,8,64,128]{3,2,1,0:T(8,128)(2,1)} custom-call(bf16[1,8,64,128]{3,2,1,0:T(8,128)(2,1)} %get-tuple-element.6.x_ref), custom_call_target="tpu_custom_call" | custom-call | tf_op jit(solution)/shard_map/pallas_call | solution.py:130
  158.7 8.8 %shard_map.85 = f32[128,64,128]{2,1,0:T(8,128)} custom-call(s32[56]{0:T(128)} %broadcast_minimum_fusion.rows_ref, s32[224]{0:T(256)} %copy-done.5, s32[224]{0:T(256)} %gather_fusion, bf16[56,256,256]{2,1,0:T(8,128)(2,1)} %bitcast.37, bf16[4,8,64,128]{3,2,1,0:T(8,128)(2,1)} %shard_map.84.a_ref), custom_call_target="tpu_custom_call" | custom-call | tf_op jit(solution)/shard_map/pallas_call | solution.py:146
  167.5 0.0 all-to-all-done.x_ref
  167.5 1.3 copy-done.1
  168.8 10.4 %all-to-all-start.3 = ((f32[128,64,128]{2,1,0:T(8,128)}), f32[128,64,128]{2,1,0:T(8,128)}, u32[]{:S(2)}, u32[]{:S(2)}) async-start(f32[128,64,128]{2,1,0:T(8,128)} %shard_map.85), calls=%async_computation.4 | async-start | bytes 8388608 | tf_op jit(solution)/shard_map/all_to_all | solution.py:261
  179.3 0.0 all-gather.5.cloned.1.call-start
  179.3 8.3 %shard_map.77.x_ref = f32[4,8,64,128]{3,2,1,0:T(8,128)} custom-call(s32[56]{0:T(128)} %broadcast_minimum_fusion.rows_ref, s32[224]{0:T(256)} %copy-done.5, s32[224]{0:T(256)} %gather_fusion, bf16[56,256,256]{2,1,0:T(8,128)(2,1)} %bitcast.38, bf16[128,64,128]{2,1,0:T(8,128)(2,1)} %copy-done.1), custom_call_target="tpu_custom_call" | custom-call | tf_op jit(solution)/shard_map/pallas_call | solution.py:146
  187.5 16.9 %shard_map.78 = f32[8,64,128]{2,1,0:T(8,128)} custom-call(f32[4,8,64,128]{3,2,1,0:T(8,128)} %shard_map.77.x_ref), custom_call_target="tpu_custom_call" | custom-call | tf_op jit(solution)/shard_map/pallas_call | solution.py:130
  204.5 1.0 broadcast_multiply_fusion.3
  205.4 0.7 fusion.1
  206.2 0.0 all-gather.5.cloned.1.call-update
  206.2 0.0 reduce-scatter.5.cloned.1.call-start
  206.2 22.0 %all-to-all-done.3.arrived_ref = f32[128,64,128]{2,1,0:T(8,128)} async-done(((f32[128,64,128]{2,1,0:T(8,128)}), f32[128,64,128]{2,1,0:T(8,128)}, u32[]{:S(2)}, u32[]{:S(2)}) %all-to-all-start.3) | async-done | bytes 4194336 | tf_op jit(solution)/shard_map/all_to_all | solution.py:261
  228.2 5.8 %shard_map.86 = f32[8,8,64,128]{3,2,1,0:T(8,128)} custom-call(s32[128]{0:T(128)} %gather_fusion.2, f32[128,64,128]{2,1,0:T(8,128)} %all-to-all-done.3.arrived_ref), custom_call_target="tpu_custom_call" | custom-call | tf_op jit(solution)/shard_map/pallas_call | solution.py:165
  233.9 0.0 reduce-scatter.5.cloned.1.call-update
  234.0 5.5 %all-gather.5.cloned.1.call-done = bf16[64,64,128]{2,1,0:T(8,128)(2,1)} async-done(((bf16[8,64,128]{2,1,0:T(8,128)(2,1)}), bf16[64,64,128]{2,1,0:T(8,128)(2,1)}) %all-gather.5.cloned.1.call-update) | async-done | bytes 1048592 | tf_op jit(solution)/shard_map/all_gather | solution.py:240
  239.5 2.2 gather_fusion.4
  241.7 0.3 broadcast_select_fusion.1
  241.9 35.4 %all_to_all.20.x_ref = bf16[128,64,128]{2,1,0:T(8,128)(2,1)} all-to-all(bf16[128,64,128]{2,1,0:T(8,128)(2,1)S(1)} %broadcast_select_fusion.1), channel_id=1, replica_groups=mesh['z'=8,'x'=4,'c'=2,'edge'=4] {'x','c'}, dimensions={0} | all-to-all | bytes 4194304 | tf_op jit(solution)/shard_map/all_to_all | solution.py:242
  277.4 8.3 %shard_map.79.x_ref = f32[4,8,64,128]{3,2,1,0:T(8,128)} custom-call(s32[56]{0:T(128)} %broadcast_minimum_fusion.rows_ref, s32[224]{0:T(256)} %copy-done.5, s32[224]{0:T(256)} %gather_fusion, bf16[56,256,256]{2,1,0:T(8,128)(2,1)} %bitcast.39, bf16[128,64,128]{2,1,0:T(8,128)(2,1)} %all_to_all.20.x_ref), custom_call_target="tpu_custom_call" | custom-call | tf_op jit(solution)/shard_map/pallas_call | solution.py:146
  285.7 16.6 %shard_map.80 = f32[8,64,128]{2,1,0:T(8,128)} custom-call(f32[4,8,64,128]{3,2,1,0:T(8,128)} %shard_map.79.x_ref), custom_call_target="tpu_custom_call" | custom-call | tf_op jit(solution)/shard_map/pallas_call | solution.py:130
  302.3 1.0 broadcast_multiply_fusion.2
  303.3 0.7 bitcast_add_fusion.2
  304.0 1.0 broadcast_multiply_fusion
  305.0 0.7 bitcast_add_fusion
  (17 shorter events, 0.1 us)
Async XLA Ops:
  7.2 48.8 %copy-start = (s32[64,128]{1,0:T(8,128)S(1)}, s32[64,128]{1,0:T(8,128)}, u32[]{:S(2)}) copy-start(s32[64,128]{1,0:T(8,128)} %param.10) | copy-start | bytes 98308
  12.5 27.0 %copy-start.5 = (s32[224]{0:T(256)}, s32[224]{0:T(256)S(1)}, u32[]{:S(2)}) copy-start(s32[224]{0:T(256)S(1)} %scatter_custom_fusion.members_ref) | copy-start | bytes 2692
  48.3 6.6 %copy-start.2 = (f32[512,128]{1,0:T(8,128)S(1)}, f32[512,128]{1,0:T(8,128)}, u32[]{:S(2)}) copy-start(f32[512,128]{1,0:T(8,128)} %param.8) | copy-start | bytes 786436
  48.3 55.6 %all-to-all-start.2 = ((f32[128,64,128]{2,1,0:T(8,128)}), f32[128,64,128]{2,1,0:T(8,128)}, u32[]{:S(2)}, u32[]{:S(2)}) async-start(f32[128,64,128]{2,1,0:T(8,128)} %shard_map.82), calls=%async_computation.2 | async-start | bytes 8388608 | tf_op jit(solution)/shard_map/all_to_all | solution.py:261
  54.9 55.3 %all-gather.3.cloned.1.call-start = ((), (), s32[]{:S(2)}) async-start(), calls=%async_computation.6 | async-start | bytes 1179648 | tf_op jit(solution)/shard_map/all_gather | solution.py:240
  55.6 92.0 %reduce-scatter.3.cloned.1.call-start = ((), (), s32[]{:S(2)}) async-start(), calls=%async_computation.8 | async-start | bytes 2359296 | tf_op jit(solution)/shard_map/reduce_scatter | solution.py:265
  109.5 0.7 copy-start.3
  114.1 53.5 %all-to-all-start = ((bf16[128,64,128]{2,1,0:T(8,128)(2,1)}), bf16[128,64,128]{2,1,0:T(8,128)(2,1)S(1)}, u32[]{:S(2)}, u32[]{:S(2)}) async-start(bf16[128,64,128]{2,1,0:T(8,128)(2,1)} %broadcast_select_fusion), calls=%async_computation | async-start | bytes 4194304 | tf_op jit(solution)/shard_map/all_to_all | solution.py:242
  167.5 1.3 copy-start.1
  168.8 59.3 %all-to-all-start.3 = ((f32[128,64,128]{2,1,0:T(8,128)}), f32[128,64,128]{2,1,0:T(8,128)}, u32[]{:S(2)}, u32[]{:S(2)}) async-start(f32[128,64,128]{2,1,0:T(8,128)} %shard_map.85), calls=%async_computation.4 | async-start | bytes 8388608 | tf_op jit(solution)/shard_map/all_to_all | solution.py:261
  179.3 60.2 %all-gather.5.cloned.1.call-start = ((), (), s32[]{:S(2)}) async-start(), calls=%async_computation.7 | async-start | bytes 1179648 | tf_op jit(solution)/shard_map/all_gather | solution.py:240
  206.2 97.9 %reduce-scatter.5.cloned.1.call-start = ((), (), s32[]{:S(2)}) async-start(), calls=%async_computation.9 | async-start | bytes 2359296 | tf_op jit(solution)/shard_map/reduce_scatter | solution.py:265
  285.7 19.3 %copy-start.4 = (f32[512,128]{1,0:T(8,128)S(1)}, f32[512,128]{1,0:T(8,128)}, u32[]{:S(2)}) copy-start(f32[512,128]{1,0:T(8,128)} %param.9) | copy-start | bytes 786436
Sparse Core Ops, SparseCore 0:
  58.1 36.7 all-gather.2
  109.6 37.9 reduce-scatter.2
  206.3 33.1 all-gather.4
  241.9 40.7 reduce-scatter.4

commit v7 on v6

--- a/solution.py
+++ b/solution.py
@@ -16,7 +16,7 @@
 X_SIZE = 4
 CORE_SIZE = 2
 GROUP = 4
-GROUPS_PER_STEP = 14
+GROUPS_PER_STEP = 28
 BLOCKS = 192
 
 

time: 313 us -> 312 us (level)
  transfers between devices with their start and end apart: 7 -> 7, of which waited for: 4 -> 4; matrix products, arithmetic and copies ran while one was open for 5% -> 5% of each run, Pallas kernels for 26% -> 25%
where the time goes in v7:
time: 312 us; the launch traced here: 311 us
  waiting for transfers between devices  103 us (33%)
  Pallas kernels  99 us (32%)
  blocking collectives  35.4 us (11%)
  local copies, waits for them, and re-layouts  23.1 us (7%)
  starting transfers between devices  21.6 us (7%)
  other arithmetic  14.4 us (5%)
  between operations  13.9 us (4%)
    all_to_all x2, waiting for transfers between devices, per_device(): lax.all_to_all(slot_sums, ('x', 'c'), split_axis=0, concat_axis=0, tiled=...  68.1 us
    pallas_call x4, Pallas kernels, edge_exchange(): pl.pallas_call(functools.partial(edge_exchange_kernel, reduce), out_shape...  54.3 us
    all_to_all x1, blocking collectives, per_device(): lax.all_to_all(outgoing, ('x', 'c'), split_axis=0, concat_axis=0, tiled=T...  35.4 us
    pallas_call x4, Pallas kernels, block_apply(): pl.pallas_call(kernel, out_shape=jax.ShapeDtypeStruct(out_shape, jnp.floa...  33.3 us
    reduce_scatter x2, waiting for transfers between devices, per_device(): owned = lax.psum_scatter(dense, 'z', scatter_dimension=0, tiled=True)  29.5 us
    all_to_all x2, starting transfers between devices, per_device(): lax.all_to_all(slot_sums, ('x', 'c'), split_axis=0, concat_axis=0, tiled=...  17.2 us
    pallas_call x2, Pallas kernels, combine_apply(): pl.pallas_call(combine_kernel, out_shape=jax.ShapeDtypeStruct((lines, blo...  11.4 us
    gather x1, local copies, waits for them, and re-layouts, per_device(): jnp.take(weights, member, axis=0, mode='clip')  11.1 us
  transfers between devices with their start and end apart: 7, of which 4 were waited for; matrix products, arithmetic and copies ran while one was open for 5% of the time, Pallas kernels for 25%

profile of v7, /device:TPU:1, one launch (start us, length us, event | category | flops | bytes accessed | tf_op | source)
XLA Modules:
  0.0 311.3 jit_solution(4584667636461663640)
XLA Ops:
  7.2 0.0 copy-start
  7.2 0.8 convert_reduce_fusion
  8.0 0.9 fusion
  8.9 0.2 reduce-window.7
  9.1 0.1 convert_reduce_fusion.1
  9.2 0.6 broadcast_minimum_fusion.rows_ref
  9.8 0.8 select_reduce_fusion
  10.6 0.7 fusion.7
  11.3 1.2 scatter_custom_fusion.members_ref
  12.5 0.0 copy-start.5
  12.5 1.6 convert_element_type.73
  14.1 11.7 %shard_map.81.a_ref = bf16[4,8,64,128]{3,2,1,0:T(8,128)(2,1)} custom-call(bf16[1,8,64,128]{3,2,1,0:T(8,128)(2,1)} %bitcast.41), custom_call_target="tpu_custom_call" | custom-call | tf_op jit(solution)/shard_map/pallas_call | solution.py:130
  25.9 2.5 gather_fusion
  28.4 11.1 %gather_fusion.1 = bf16[224,64,256]{2,1,0:T(8,128)(2,1)} fusion(bf16[192,64,256]{2,1,0:T(8,128)(2,1)} %bitcast.40, s32[1024]{0:T(1024)S(1)} %pad_clamp_fusion.1), kind=kCustom, calls=%fused_computation.3 | custom fusion | bytes 14680960 | tf_op jit(solution)/shard_map/jit(_take)/gather | solution.py:232
  39.5 0.0 copy-done.5
  39.5 8.5 %shard_map.82 = f32[128,64,128]{2,1,0:T(8,128)} custom-call(s32[56]{0:T(128)} %broadcast_minimum_fusion.rows_ref, s32[224]{0:T(256)} %copy-done.5, s32[224]{0:T(256)} %gather_fusion, bf16[56,256,256]{2,1,0:T(8,128)(2,1)} %bitcast.36, bf16[4,8,64,128]{3,2,1,0:T(8,128)(2,1)} %shard_map.81.a_ref), custom_call_target="tpu_custom_call" | custom-call | tf_op jit(solution)/shard_map/pallas_call | solution.py:146
  48.0 6.6 %all-to-all-start.2 = ((f32[128,64,128]{2,1,0:T(8,128)}), f32[128,64,128]{2,1,0:T(8,128)}, u32[]{:S(2)}, u32[]{:S(2)}) async-start(f32[128,64,128]{2,1,0:T(8,128)} %shard_map.82), calls=%async_computation.2 | async-start | bytes 8388608 | tf_op jit(solution)/shard_map/all_to_all | solution.py:261
  54.6 0.0 all-gather.3.cloned.1.call-start
  54.6 0.0 copy-done.2
  54.6 0.7 convert_element_type.71
  55.3 0.0 all-gather.3.cloned.1.call-update
  55.3 0.0 reduce-scatter.3.cloned.1.call-start
  55.4 0.1 fusion.3
  55.5 0.1 broadcast_or_fusion
  55.5 0.1 reshape.247
  55.7 0.0 copy-done
  55.7 1.8 gather_fusion.2
  57.5 46.0 %all-to-all-done.2.arrived_ref = f32[128,64,128]{2,1,0:T(8,128)} async-done(((f32[128,64,128]{2,1,0:T(8,128)}), f32[128,64,128]{2,1,0:T(8,128)}, u32[]{:S(2)}, u32[]{:S(2)}) %all-to-all-start.2) | async-done | bytes 4194336 | tf_op jit(solution)/shard_map/all_to_all | solution.py:261
  103.5 5.6 %shard_map.83 = f32[8,8,64,128]{3,2,1,0:T(8,128)} custom-call(s32[128]{0:T(128)} %gather_fusion.2, f32[128,64,128]{2,1,0:T(8,128)} %all-to-all-done.2.arrived_ref), custom_call_target="tpu_custom_call" | custom-call | tf_op jit(solution)/shard_map/pallas_call | solution.py:165
  109.2 0.0 reduce-scatter.3.cloned.1.call-update
  109.2 0.1 add.205
  109.3 0.1 add.206
  109.4 0.4 copy-done.3
  109.9 0.0 all-gather.3.cloned.1.call-done
  109.9 2.2 gather_fusion.3
  112.1 1.7 broadcast_select_fusion
  113.8 4.4 %all-to-all-start = ((bf16[128,64,128]{2,1,0:T(8,128)(2,1)}), bf16[128,64,128]{2,1,0:T(8,128)(2,1)S(1)}, u32[]{:S(2)}, u32[]{:S(2)}) async-start(bf16[128,64,128]{2,1,0:T(8,128)(2,1)} %broadcast_select_fusion), calls=%async_computation | async-start | bytes 4194304 | tf_op jit(solution)/shard_map/all_to_all | solution.py:242
  118.1 29.5 %reduce-scatter.3.cloned.1.call-done = f32[1,8,64,128]{3,2,1,0:T(8,128)} async-done(((f32[8,8,64,128]{3,2,1,0:T(8,128)}), f32[1,8,64,128]{3,2,1,0:T(8,128)}) %reduce-scatter.3.cloned.1.call-update) | async-done | bytes 262160 | tf_op jit(solution)/shard_map/reduce_scatter | solution.py:265
  147.6 1.7 broadcast_multiply_fusion.1
  149.3 9.1 %shard_map.84.a_ref = bf16[4,8,64,128]{3,2,1,0:T(8,128)(2,1)} custom-call(bf16[1,8,64,128]{3,2,1,0:T(8,128)(2,1)} %get-tuple-element.6.x_ref), custom_call_target="tpu_custom_call" | custom-call | tf_op jit(solution)/shard_map/pallas_call | solution.py:130
  158.3 8.6 %shard_map.85 = f32[128,64,128]{2,1,0:T(8,128)} custom-call(s32[56]{0:T(128)} %broadcast_minimum_fusion.rows_ref, s32[224]{0:T(256)} %copy-done.5, s32[224]{0:T(256)} %gather_fusion, bf16[56,256,256]{2,1,0:T(8,128)(2,1)} %bitcast.37, bf16[4,8,64,128]{3,2,1,0:T(8,128)(2,1)} %shard_map.84.a_ref), custom_call_target="tpu_custom_call" | custom-call | tf_op jit(solution)/shard_map/pallas_call | solution.py:146
  166.9 0.0 all-to-all-done.x_ref
  166.9 1.3 copy-done.1
  168.2 10.6 %all-to-all-start.3 = ((f32[128,64,128]{2,1,0:T(8,128)}), f32[128,64,128]{2,1,0:T(8,128)}, u32[]{:S(2)}, u32[]{:S(2)}) async-start(f32[128,64,128]{2,1,0:T(8,128)} %shard_map.85), calls=%async_computation.4 | async-start | bytes 8388608 | tf_op jit(solution)/shard_map/all_to_all | solution.py:261
  178.8 0.0 all-gather.5.cloned.1.call-start
  178.8 8.1 %shard_map.77.x_ref = f32[4,8,64,128]{3,2,1,0:T(8,128)} custom-call(s32[56]{0:T(128)} %broadcast_minimum_fusion.rows_ref, s32[224]{0:T(256)} %copy-done.5, s32[224]{0:T(256)} %gather_fusion, bf16[56,256,256]{2,1,0:T(8,128)(2,1)} %bitcast.38, bf16[128,64,128]{2,1,0:T(8,128)(2,1)} %copy-done.1), custom_call_target="tpu_custom_call" | custom-call | tf_op jit(solution)/shard_map/pallas_call | solution.py:146
  186.9 16.9 %shard_map.78 = f32[8,64,128]{2,1,0:T(8,128)} custom-call(f32[4,8,64,128]{3,2,1,0:T(8,128)} %shard_map.77.x_ref), custom_call_target="tpu_custom_call" | custom-call | tf_op jit(solution)/shard_map/pallas_call | solution.py:130
  203.8 1.0 broadcast_multiply_fusion.3
  204.8 0.7 fusion.1
  205.5 0.0 all-gather.5.cloned.1.call-update
  205.5 0.0 reduce-scatter.5.cloned.1.call-start
  205.6 22.2 %all-to-all-done.3.arrived_ref = f32[128,64,128]{2,1,0:T(8,128)} async-done(((f32[128,64,128]{2,1,0:T(8,128)}), f32[128,64,128]{2,1,0:T(8,128)}, u32[]{:S(2)}, u32[]{:S(2)}) %all-to-all-start.3) | async-done | bytes 4194336 | tf_op jit(solution)/shard_map/all_to_all | solution.py:261
  227.7 5.8 %shard_map.86 = f32[8,8,64,128]{3,2,1,0:T(8,128)} custom-call(s32[128]{0:T(128)} %gather_fusion.2, f32[128,64,128]{2,1,0:T(8,128)} %all-to-all-done.3.arrived_ref), custom_call_target="tpu_custom_call" | custom-call | tf_op jit(solution)/shard_map/pallas_call | solution.py:165
  233.5 0.0 reduce-scatter.5.cloned.1.call-update
  233.5 5.2 %all-gather.5.cloned.1.call-done = bf16[64,64,128]{2,1,0:T(8,128)(2,1)} async-done(((bf16[8,64,128]{2,1,0:T(8,128)(2,1)}), bf16[64,64,128]{2,1,0:T(8,128)(2,1)}) %all-gather.5.cloned.1.call-update) | async-done | bytes 1048592 | tf_op jit(solution)/shard_map/all_gather | solution.py:240
  238.7 2.2 gather_fusion.4
  240.9 0.3 broadcast_select_fusion.1
  241.2 35.4 %all_to_all.20.x_ref = bf16[128,64,128]{2,1,0:T(8,128)(2,1)} all-to-all(bf16[128,64,128]{2,1,0:T(8,128)(2,1)S(1)} %broadcast_select_fusion.1), channel_id=1, replica_groups=mesh['z'=8,'x'=4,'c'=2,'edge'=4] {'x','c'}, dimensions={0} | all-to-all | bytes 4194304 | tf_op jit(solution)/shard_map/all_to_all | solution.py:242
  276.6 8.1 %shard_map.79.x_ref = f32[4,8,64,128]{3,2,1,0:T(8,128)} custom-call(s32[56]{0:T(128)} %broadcast_minimum_fusion.rows_ref, s32[224]{0:T(256)} %copy-done.5, s32[224]{0:T(256)} %gather_fusion, bf16[56,256,256]{2,1,0:T(8,128)(2,1)} %bitcast.39, bf16[128,64,128]{2,1,0:T(8,128)(2,1)} %all_to_all.20.x_ref), custom_call_target="tpu_custom_call" | custom-call | tf_op jit(solution)/shard_map/pallas_call | solution.py:146
  284.6 16.6 %shard_map.80 = f32[8,64,128]{2,1,0:T(8,128)} custom-call(f32[4,8,64,128]{3,2,1,0:T(8,128)} %shard_map.79.x_ref), custom_call_target="tpu_custom_call" | custom-call | tf_op jit(solution)/shard_map/pallas_call | solution.py:130
  301.3 1.0 broadcast_multiply_fusion.2
  302.3 0.7 bitcast_add_fusion.2
  303.0 1.0 broadcast_multiply_fusion
  304.0 0.7 bitcast_add_fusion
  (17 shorter events, 0.1 us)
Async XLA Ops:
  7.2 48.5 %copy-start = (s32[64,128]{1,0:T(8,128)S(1)}, s32[64,128]{1,0:T(8,128)}, u32[]{:S(2)}) copy-start(s32[64,128]{1,0:T(8,128)} %param.10) | copy-start | bytes 98308
  12.5 27.0 %copy-start.5 = (s32[224]{0:T(256)}, s32[224]{0:T(256)S(1)}, u32[]{:S(2)}) copy-start(s32[224]{0:T(256)S(1)} %scatter_custom_fusion.members_ref) | copy-start | bytes 2692
  48.0 6.6 %copy-start.2 = (f32[512,128]{1,0:T(8,128)S(1)}, f32[512,128]{1,0:T(8,128)}, u32[]{:S(2)}) copy-start(f32[512,128]{1,0:T(8,128)} %param.8) | copy-start | bytes 786436
  48.0 55.5 %all-to-all-start.2 = ((f32[128,64,128]{2,1,0:T(8,128)}), f32[128,64,128]{2,1,0:T(8,128)}, u32[]{:S(2)}, u32[]{:S(2)}) async-start(f32[128,64,128]{2,1,0:T(8,128)} %shard_map.82), calls=%async_computation.2 | async-start | bytes 8388608 | tf_op jit(solution)/shard_map/all_to_all | solution.py:261
  54.6 55.3 %all-gather.3.cloned.1.call-start = ((), (), s32[]{:S(2)}) async-start(), calls=%async_computation.6 | async-start | bytes 1179648 | tf_op jit(solution)/shard_map/all_gather | solution.py:240
  55.3 92.3 %reduce-scatter.3.cloned.1.call-start = ((), (), s32[]{:S(2)}) async-start(), calls=%async_computation.8 | async-start | bytes 2359296 | tf_op jit(solution)/shard_map/reduce_scatter | solution.py:265
  109.2 0.7 copy-start.3
  113.8 53.2 %all-to-all-start = ((bf16[128,64,128]{2,1,0:T(8,128)(2,1)}), bf16[128,64,128]{2,1,0:T(8,128)(2,1)S(1)}, u32[]{:S(2)}, u32[]{:S(2)}) async-start(bf16[128,64,128]{2,1,0:T(8,128)(2,1)} %broadcast_select_fusion), calls=%async_computation | async-start | bytes 4194304 | tf_op jit(solution)/shard_map/all_to_all | solution.py:242
  166.9 1.3 copy-start.1
  168.2 59.5 %all-to-all-start.3 = ((f32[128,64,128]{2,1,0:T(8,128)}), f32[128,64,128]{2,1,0:T(8,128)}, u32[]{:S(2)}, u32[]{:S(2)}) async-start(f32[128,64,128]{2,1,0:T(8,128)} %shard_map.85), calls=%async_computation.4 | async-start | bytes 8388608 | tf_op jit(solution)/shard_map/all_to_all | solution.py:261
  178.8 59.9 %all-gather.5.cloned.1.call-start = ((), (), s32[]{:S(2)}) async-start(), calls=%async_computation.7 | async-start | bytes 1179648 | tf_op jit(solution)/shard_map/all_gather | solution.py:240
  205.5 97.5 %reduce-scatter.5.cloned.1.call-start = ((), (), s32[]{:S(2)}) async-start(), calls=%async_computation.9 | async-start | bytes 2359296 | tf_op jit(solution)/shard_map/reduce_scatter | solution.py:265
  284.6 19.3 %copy-start.4 = (f32[512,128]{1,0:T(8,128)S(1)}, f32[512,128]{1,0:T(8,128)}, u32[]{:S(2)}) copy-start(f32[512,128]{1,0:T(8,128)} %param.9) | copy-start | bytes 786436
Sparse Core Ops, SparseCore 0:
  57.8 36.7 all-gather.2
  109.3 38.2 reduce-scatter.2
  205.7 32.9 all-gather.4
  241.1 41.1 reduce-scatter.4

commit v8 on v7

--- a/solution.py
+++ b/solution.py
@@ -90,7 +90,7 @@
     lax.fori_loop(0, arrived_ref.shape[0], body, 0, unroll=8)
 
 
-def edge_exchange_kernel(reduce, x_ref, out_ref, held, send_sem, recv_sem):
+def edge_exchange_kernel(reduce, x_ref, base_ref, out_ref, held, send_sem, recv_sem):
     count = held.shape[0]
     me = lax.axis_index("edge")
     barrier = pltpu.get_barrier_semaphore()
@@ -119,18 +119,18 @@
         total = held[0]
         for q in range(1, count):
             total = total + held[q]
-        out_ref[...] = total
+        out_ref[...] = 0.9 * total + 0.1 * base_ref[...]
     else:
         out_ref[...] = held[...]
 
 
-def edge_exchange(chunks, count, reduce, collective_id):
+def edge_exchange(chunks, count, reduce, collective_id, base):
     piece = chunks.shape[1:]
     out_shape = piece if reduce else (count,) + piece
     return pl.pallas_call(
         functools.partial(edge_exchange_kernel, reduce),
         out_shape=jax.ShapeDtypeStruct(out_shape, chunks.dtype),
-        in_specs=[pl.BlockSpec(memory_space=pltpu.VMEM)],
+        in_specs=[pl.BlockSpec(memory_space=pltpu.VMEM)] * 2,
         out_specs=pl.BlockSpec(memory_space=pltpu.VMEM),
         scratch_shapes=[
             pltpu.VMEM((count,) + piece, chunks.dtype),
@@ -138,7 +138,7 @@
             pltpu.SemaphoreType.DMA((count,)),
         ],
         compiler_params=pltpu.CompilerParams(collective_id=collective_id, has_side_effects=True),
-    )(chunks)
+    )(chunks, base)
 
 
 def block_apply(kernel, rows, members, slots, weights_g, dense, out_shape):
@@ -246,14 +246,15 @@
             forward_kernel, group_row, member, member_slot, weights_g, received,
             (quarters, blocks_dev, quarter, hidden),
         )
-        summed = edge_exchange(partial, quarters, True, 1)
-        current = 0.9 * summed.reshape(row_count, hidden) + 0.1 * teleport
+        current = edge_exchange(
+            partial, quarters, True, 1, teleport.reshape(blocks_dev, quarter, hidden)
+        ).reshape(row_count, hidden)
 
     adjoint = cotangent
     gradient = 0.1 * cotangent
     for step_index in range(STEPS):
         rounded = adjoint.astype(jnp.bfloat16).reshape(1, blocks_dev, quarter, hidden)
-        whole_rows = edge_exchange(rounded, quarters, False, 2)
+        whole_rows = edge_exchange(rounded, quarters, False, 2, rounded)
         slot_sums = block_apply(
             backward_kernel, group_row, member, member_slot, weights_g, whole_rows,
             (slot_total, quarter, hidden),

time: 312 us -> 313 us (level)
  transfers between devices with their start and end apart: 7 -> 7, of which waited for: 4 -> 4; matrix products, arithmetic and copies ran while one was open for 5% -> 4% of each run, Pallas kernels for 25% -> 25%
where the time goes in v8:
time: 313 us; the launch traced here: 312 us
  waiting for transfers between devices  103 us (33%)
  Pallas kernels  99.7 us (32%)
  blocking collectives  35.4 us (11%)
  local copies, waits for them, and re-layouts  24.8 us (8%)
  starting transfers between devices  21.1 us (7%)
  between operations  13.9 us (4%)
  other arithmetic  12.6 us (4%)
    all_to_all x2, waiting for transfers between devices, per_device(): lax.all_to_all(slot_sums, ('x', 'c'), split_axis=0, concat_axis=0, tiled=...  68.1 us
    pallas_call x4, Pallas kernels, edge_exchange(): pl.pallas_call(functools.partial(edge_exchange_kernel, reduce), out_shape...  55 us
    all_to_all x1, blocking collectives, per_device(): lax.all_to_all(outgoing, ('x', 'c'), split_axis=0, concat_axis=0, tiled=T...  35.4 us
    pallas_call x4, Pallas kernels, block_apply(): pl.pallas_call(kernel, out_shape=jax.ShapeDtypeStruct(out_shape, jnp.floa...  33.3 us
    reduce_scatter x2, waiting for transfers between devices, per_device(): owned = lax.psum_scatter(dense, 'z', scatter_dimension=0, tiled=True)  29.5 us
    all_to_all x2, starting transfers between devices, per_device(): lax.all_to_all(slot_sums, ('x', 'c'), split_axis=0, concat_axis=0, tiled=...  16.7 us
    pallas_call x2, Pallas kernels, combine_apply(): pl.pallas_call(combine_kernel, out_shape=jax.ShapeDtypeStruct((lines, blo...  11.4 us
    gather x1, local copies, waits for them, and re-layouts, per_device(): jnp.take(weights, member, axis=0, mode='clip')  11.1 us
  transfers between devices with their start and end apart: 7, of which 4 were waited for; matrix products, arithmetic and copies ran while one was open for 4% of the time, Pallas kernels for 25%

profile of v8, /device:TPU:1, one launch (start us, length us, event | category | flops | bytes accessed | tf_op | source)
XLA Modules:
  0.0 311.5 jit_solution(9547553739905287594)
XLA Ops:
  7.2 0.0 copy-start
  7.2 0.8 convert_reduce_fusion
  8.0 0.9 fusion
  8.9 0.2 reduce-window.7
  9.1 0.1 convert_reduce_fusion.1
  9.2 0.6 broadcast_minimum_fusion.rows_ref
  9.8 0.8 select_reduce_fusion
  10.6 0.7 fusion.6
  11.3 1.2 scatter_custom_fusion.members_ref
  12.5 0.0 copy-start.5
  12.5 1.6 convert_element_type.74
  14.1 11.8 %shard_map.81.a_ref = bf16[4,8,64,128]{3,2,1,0:T(8,128)(2,1)} custom-call(bf16[1,8,64,128]{3,2,1,0:T(8,128)(2,1)} %bitcast.38, bf16[1,8,64,128]{3,2,1,0:T(8,128)(2,1)} %bitcast.39), custom_call_target="tpu_custom_call" | custom-call | tf_op jit(solution)/shard_map/pallas_call | solution.py:130
  25.9 2.5 gather_fusion
  28.4 11.1 %gather_fusion.1 = bf16[224,64,256]{2,1,0:T(8,128)(2,1)} fusion(bf16[192,64,256]{2,1,0:T(8,128)(2,1)} %bitcast.35, s32[1024]{0:T(1024)S(1)} %pad_clamp_fusion.1), kind=kCustom, calls=%fused_computation.3 | custom fusion | bytes 14680960 | tf_op jit(solution)/shard_map/jit(_take)/gather | solution.py:232
  39.6 0.0 copy-done.5
  39.6 8.5 %shard_map.82 = f32[128,64,128]{2,1,0:T(8,128)} custom-call(s32[56]{0:T(128)} %broadcast_minimum_fusion.rows_ref, s32[224]{0:T(256)} %copy-done.5, s32[224]{0:T(256)} %gather_fusion, bf16[56,256,256]{2,1,0:T(8,128)(2,1)} %bitcast.31, bf16[4,8,64,128]{3,2,1,0:T(8,128)(2,1)} %shard_map.81.a_ref), custom_call_target="tpu_custom_call" | custom-call | tf_op jit(solution)/shard_map/pallas_call | solution.py:146
  48.1 6.6 %all-to-all-start.2 = ((f32[128,64,128]{2,1,0:T(8,128)}), f32[128,64,128]{2,1,0:T(8,128)}, u32[]{:S(2)}, u32[]{:S(2)}) async-start(f32[128,64,128]{2,1,0:T(8,128)} %shard_map.82), calls=%async_computation.2 | async-start | bytes 8388608 | tf_op jit(solution)/shard_map/all_to_all | solution.py:262
  54.7 0.0 all-gather.3.cloned.1.call-start
  54.7 0.0 copy-done.2
  54.7 0.7 convert_element_type.72
  55.4 0.0 all-gather.3.cloned.1.call-update
  55.4 0.0 reduce-scatter.3.cloned.1.call-start
  55.5 0.1 fusion.2
  55.6 0.1 broadcast_or_fusion
  55.6 0.1 reshape.248
  55.8 0.0 copy-done
  55.8 1.8 gather_fusion.2
  57.6 46.0 %all-to-all-done.2.arrived_ref = f32[128,64,128]{2,1,0:T(8,128)} async-done(((f32[128,64,128]{2,1,0:T(8,128)}), f32[128,64,128]{2,1,0:T(8,128)}, u32[]{:S(2)}, u32[]{:S(2)}) %all-to-all-start.2) | async-done | bytes 4194336 | tf_op jit(solution)/shard_map/all_to_all | solution.py:262
  103.6 5.6 %shard_map.83 = f32[8,8,64,128]{3,2,1,0:T(8,128)} custom-call(s32[128]{0:T(128)} %gather_fusion.2, f32[128,64,128]{2,1,0:T(8,128)} %all-to-all-done.2.arrived_ref), custom_call_target="tpu_custom_call" | custom-call | tf_op jit(solution)/shard_map/pallas_call | solution.py:165
  109.3 0.0 reduce-scatter.3.cloned.1.call-update
  109.3 0.1 add.199
  109.4 0.1 add.200
  109.5 0.4 copy-done.3
  110.0 0.0 all-gather.3.cloned.1.call-done
  110.0 2.2 gather_fusion.3
  112.2 1.7 broadcast_select_fusion
  113.9 4.4 %all-to-all-start = ((bf16[128,64,128]{2,1,0:T(8,128)(2,1)}), bf16[128,64,128]{2,1,0:T(8,128)(2,1)S(1)}, u32[]{:S(2)}, u32[]{:S(2)}) async-start(bf16[128,64,128]{2,1,0:T(8,128)(2,1)} %broadcast_select_fusion), calls=%async_computation | async-start | bytes 4194304 | tf_op jit(solution)/shard_map/all_to_all | solution.py:242
  118.2 29.4 %reduce-scatter.3.cloned.1.call-done = f32[1,8,64,128]{3,2,1,0:T(8,128)} async-done(((f32[8,8,64,128]{3,2,1,0:T(8,128)}), f32[1,8,64,128]{3,2,1,0:T(8,128)}) %reduce-scatter.3.cloned.1.call-update) | async-done | bytes 262160 | tf_op jit(solution)/shard_map/reduce_scatter | solution.py:266
  147.7 1.7 broadcast_multiply_fusion.1
  149.3 9.6 %shard_map.84.a_ref = bf16[4,8,64,128]{3,2,1,0:T(8,128)(2,1)} custom-call(bf16[1,8,64,128]{3,2,1,0:T(8,128)(2,1)} %get-tuple-element.6.x_ref.base_ref, bf16[1,8,64,128]{3,2,1,0:T(8,128)(2,1)} %get-tuple-element.6.x_ref.base_ref), custom_call_target="tpu_custom_call" | custom-call | tf_op jit(solution)/shard_map/pallas_call | solution.py:130
  158.9 8.6 %shard_map.85 = f32[128,64,128]{2,1,0:T(8,128)} custom-call(s32[56]{0:T(128)} %broadcast_minimum_fusion.rows_ref, s32[224]{0:T(256)} %copy-done.5, s32[224]{0:T(256)} %gather_fusion, bf16[56,256,256]{2,1,0:T(8,128)(2,1)} %bitcast.32, bf16[4,8,64,128]{3,2,1,0:T(8,128)(2,1)} %shard_map.84.a_ref), custom_call_target="tpu_custom_call" | custom-call | tf_op jit(solution)/shard_map/pallas_call | solution.py:146
  167.5 0.0 all-to-all-done.x_ref
  167.5 1.3 copy-done.1
  168.8 10.0 %all-to-all-start.3 = ((f32[128,64,128]{2,1,0:T(8,128)}), f32[128,64,128]{2,1,0:T(8,128)}, u32[]{:S(2)}, u32[]{:S(2)}) async-start(f32[128,64,128]{2,1,0:T(8,128)} %shard_map.85), calls=%async_computation.4 | async-start | bytes 8388608 | tf_op jit(solution)/shard_map/all_to_all | solution.py:262
  178.8 0.0 all-gather.5.cloned.1.call-start
  178.8 8.1 %shard_map.77.x_ref = f32[4,8,64,128]{3,2,1,0:T(8,128)} custom-call(s32[56]{0:T(128)} %broadcast_minimum_fusion.rows_ref, s32[224]{0:T(256)} %copy-done.5, s32[224]{0:T(256)} %gather_fusion, bf16[56,256,256]{2,1,0:T(8,128)(2,1)} %bitcast.33, bf16[128,64,128]{2,1,0:T(8,128)(2,1)} %copy-done.1), custom_call_target="tpu_custom_call" | custom-call | tf_op jit(solution)/shard_map/pallas_call | solution.py:146
  186.9 17.0 %shard_map.78 = f32[8,64,128]{2,1,0:T(8,128)} custom-call(f32[4,8,64,128]{3,2,1,0:T(8,128)} %shard_map.77.x_ref, f32[8,64,128]{2,1,0:T(8,128)} %bitcast.36), custom_call_target="tpu_custom_call" | custom-call | tf_op jit(solution)/shard_map/pallas_call | solution.py:130
  203.9 1.6 convert_element_type.73
  205.5 0.0 all-gather.5.cloned.1.call-update
  205.6 0.0 reduce-scatter.5.cloned.1.call-start
  205.6 22.2 %all-to-all-done.3.arrived_ref = f32[128,64,128]{2,1,0:T(8,128)} async-done(((f32[128,64,128]{2,1,0:T(8,128)}), f32[128,64,128]{2,1,0:T(8,128)}, u32[]{:S(2)}, u32[]{:S(2)}) %all-to-all-start.3) | async-done | bytes 4194336 | tf_op jit(solution)/shard_map/all_to_all | solution.py:262
  227.8 5.8 %shard_map.86 = f32[8,8,64,128]{3,2,1,0:T(8,128)} custom-call(s32[128]{0:T(128)} %gather_fusion.2, f32[128,64,128]{2,1,0:T(8,128)} %all-to-all-done.3.arrived_ref), custom_call_target="tpu_custom_call" | custom-call | tf_op jit(solution)/shard_map/pallas_call | solution.py:165
  233.5 0.0 reduce-scatter.5.cloned.1.call-update
  233.6 5.4 %all-gather.5.cloned.1.call-done = bf16[64,64,128]{2,1,0:T(8,128)(2,1)} async-done(((bf16[8,64,128]{2,1,0:T(8,128)(2,1)}), bf16[64,64,128]{2,1,0:T(8,128)(2,1)}) %all-gather.5.cloned.1.call-update) | async-done | bytes 1048592 | tf_op jit(solution)/shard_map/all_gather | solution.py:240
  238.9 2.2 gather_fusion.4
  241.1 0.3 broadcast_select_fusion.1
  241.4 35.4 %all_to_all.20.x_ref = bf16[128,64,128]{2,1,0:T(8,128)(2,1)} all-to-all(bf16[128,64,128]{2,1,0:T(8,128)(2,1)S(1)} %broadcast_select_fusion.1), channel_id=1, replica_groups=mesh['z'=8,'x'=4,'c'=2,'edge'=4] {'x','c'}, dimensions={0} | all-to-all | bytes 4194304 | tf_op jit(solution)/shard_map/all_to_all | solution.py:242
  276.8 8.1 %shard_map.79.x_ref = f32[4,8,64,128]{3,2,1,0:T(8,128)} custom-call(s32[56]{0:T(128)} %broadcast_minimum_fusion.rows_ref, s32[224]{0:T(256)} %copy-done.5, s32[224]{0:T(256)} %gather_fusion, bf16[56,256,256]{2,1,0:T(8,128)(2,1)} %bitcast.34, bf16[128,64,128]{2,1,0:T(8,128)(2,1)} %all_to_all.20.x_ref), custom_call_target="tpu_custom_call" | custom-call | tf_op jit(solution)/shard_map/pallas_call | solution.py:146
  284.9 16.7 %shard_map.80 = f32[8,64,128]{2,1,0:T(8,128)} custom-call(f32[4,8,64,128]{3,2,1,0:T(8,128)} %shard_map.79.x_ref, f32[8,64,128]{2,1,0:T(8,128)} %bitcast.37), custom_call_target="tpu_custom_call" | custom-call | tf_op jit(solution)/shard_map/pallas_call | solution.py:130
  301.5 0.0 reduce-scatter.5.cloned.1.call-done
  301.6 1.0 broadcast_multiply_fusion
  302.6 0.0 copy-done.4
  302.6 0.7 bitcast_add_fusion
  303.3 1.7 copy.9
  (15 shorter events, 0.1 us)
Async XLA Ops:
  7.2 48.6 %copy-start = (s32[64,128]{1,0:T(8,128)S(1)}, s32[64,128]{1,0:T(8,128)}, u32[]{:S(2)}) copy-start(s32[64,128]{1,0:T(8,128)} %param.10) | copy-start | bytes 98308
  12.5 27.1 %copy-start.5 = (s32[224]{0:T(256)}, s32[224]{0:T(256)S(1)}, u32[]{:S(2)}) copy-start(s32[224]{0:T(256)S(1)} %scatter_custom_fusion.members_ref) | copy-start | bytes 2692
  48.1 6.6 %copy-start.2 = (f32[512,128]{1,0:T(8,128)S(1)}, f32[512,128]{1,0:T(8,128)}, u32[]{:S(2)}) copy-start(f32[512,128]{1,0:T(8,128)} %param.8) | copy-start | bytes 786436
  48.1 55.5 %all-to-all-start.2 = ((f32[128,64,128]{2,1,0:T(8,128)}), f32[128,64,128]{2,1,0:T(8,128)}, u32[]{:S(2)}, u32[]{:S(2)}) async-start(f32[128,64,128]{2,1,0:T(8,128)} %shard_map.82), calls=%async_computation.2 | async-start | bytes 8388608 | tf_op jit(solution)/shard_map/all_to_all | solution.py:262
  54.7 55.3 %all-gather.3.cloned.1.call-start = ((), (), s32[]{:S(2)}) async-start(), calls=%async_computation.6 | async-start | bytes 1179648 | tf_op jit(solution)/shard_map/all_gather | solution.py:240
  55.4 92.3 %reduce-scatter.3.cloned.1.call-start = ((), (), s32[]{:S(2)}) async-start(), calls=%async_computation.8 | async-start | bytes 2359296 | tf_op jit(solution)/shard_map/reduce_scatter | solution.py:266
  109.3 0.7 copy-start.3
  113.9 53.6 %all-to-all-start = ((bf16[128,64,128]{2,1,0:T(8,128)(2,1)}), bf16[128,64,128]{2,1,0:T(8,128)(2,1)S(1)}, u32[]{:S(2)}, u32[]{:S(2)}) async-start(bf16[128,64,128]{2,1,0:T(8,128)(2,1)} %broadcast_select_fusion), calls=%async_computation | async-start | bytes 4194304 | tf_op jit(solution)/shard_map/all_to_all | solution.py:242
  167.5 1.3 copy-start.1
  168.8 59.0 %all-to-all-start.3 = ((f32[128,64,128]{2,1,0:T(8,128)}), f32[128,64,128]{2,1,0:T(8,128)}, u32[]{:S(2)}, u32[]{:S(2)}) async-start(f32[128,64,128]{2,1,0:T(8,128)} %shard_map.85), calls=%async_computation.4 | async-start | bytes 8388608 | tf_op jit(solution)/shard_map/all_to_all | solution.py:262
  178.8 60.1 %all-gather.5.cloned.1.call-start = ((), (), s32[]{:S(2)}) async-start(), calls=%async_computation.7 | async-start | bytes 1179648 | tf_op jit(solution)/shard_map/all_gather | solution.py:240
  205.6 96.0 %reduce-scatter.5.cloned.1.call-start = ((), (), s32[]{:S(2)}) async-start(), calls=%async_computation.9 | async-start | bytes 2359296 | tf_op jit(solution)/shard_map/reduce_scatter | solution.py:266
  284.9 17.7 %copy-start.4 = (f32[512,128]{1,0:T(8,128)S(1)}, f32[512,128]{1,0:T(8,128)}, u32[]{:S(2)}) copy-start(f32[512,128]{1,0:T(8,128)} %param.9) | copy-start | bytes 786436
Sparse Core Ops, SparseCore 0:
  57.9 36.7 all-gather.2
  109.4 38.2 reduce-scatter.2
  205.7 33.1 all-gather.4
  241.3 40.7 reduce-scatter.4

commit v9 on v7

--- a/solution.py
+++ b/solution.py
@@ -87,7 +87,7 @@
 
         return carry
 
-    lax.fori_loop(0, arrived_ref.shape[0], body, 0, unroll=8)
+    lax.fori_loop(0, arrived_ref.shape[0], body, 0, unroll=16)
 
 
 def edge_exchange_kernel(reduce, x_ref, out_ref, held, send_sem, recv_sem):

time: 312 us -> 312 us (level)
  no operation moved by 1% of the time
where the time goes in v9:
time: 312 us; the launch traced here: 311 us
  waiting for transfers between devices  103 us (33%)
  Pallas kernels  99.4 us (32%)
  blocking collectives  35.4 us (11%)
  local copies, waits for them, and re-layouts  23.1 us (7%)
  starting transfers between devices  21.4 us (7%)
  other arithmetic  14.4 us (5%)
  between operations  13.9 us (4%)
    all_to_all x2, waiting for transfers between devices, per_device(): lax.all_to_all(slot_sums, ('x', 'c'), split_axis=0, concat_axis=0, tiled=...  68.1 us
    pallas_call x4, Pallas kernels, edge_exchange(): pl.pallas_call(functools.partial(edge_exchange_kernel, reduce), out_shape...  54.9 us
    all_to_all x1, blocking collectives, per_device(): lax.all_to_all(outgoing, ('x', 'c'), split_axis=0, concat_axis=0, tiled=T...  35.4 us
    pallas_call x4, Pallas kernels, block_apply(): pl.pallas_call(kernel, out_shape=jax.ShapeDtypeStruct(out_shape, jnp.floa...  33.3 us
    reduce_scatter x2, waiting for transfers between devices, per_device(): owned = lax.psum_scatter(dense, 'z', scatter_dimension=0, tiled=True)  29.1 us
    all_to_all x2, starting transfers between devices, per_device(): lax.all_to_all(slot_sums, ('x', 'c'), split_axis=0, concat_axis=0, tiled=...  16.9 us
    pallas_call x2, Pallas kernels, combine_apply(): pl.pallas_call(combine_kernel, out_shape=jax.ShapeDtypeStruct((lines, blo...  11.3 us
    gather x1, local copies, waits for them, and re-layouts, per_device(): jnp.take(weights, member, axis=0, mode='clip')  11.1 us
  transfers between devices with their start and end apart: 7, of which 4 were waited for; matrix products, arithmetic and copies ran while one was open for 5% of the time, Pallas kernels for 25%

profile of v9, /device:TPU:1, one launch (start us, length us, event | category | flops | bytes accessed | tf_op | source)
XLA Modules:
  0.0 311.3 jit_solution(8319706591017943115)
XLA Ops:
  7.2 0.0 copy-start
  7.2 0.8 convert_reduce_fusion
  8.0 0.9 fusion
  8.9 0.2 reduce-window.7
  9.1 0.1 convert_reduce_fusion.1
  9.2 0.6 broadcast_minimum_fusion.rows_ref
  9.8 0.8 select_reduce_fusion
  10.6 0.7 fusion.7
  11.3 1.2 scatter_custom_fusion.members_ref
  12.5 0.0 copy-start.5
  12.5 1.6 convert_element_type.73
  14.1 11.7 %shard_map.81.a_ref = bf16[4,8,64,128]{3,2,1,0:T(8,128)(2,1)} custom-call(bf16[1,8,64,128]{3,2,1,0:T(8,128)(2,1)} %bitcast.41), custom_call_target="tpu_custom_call" | custom-call | tf_op jit(solution)/shard_map/pallas_call | solution.py:130
  25.9 2.5 gather_fusion
  28.4 11.1 %gather_fusion.1 = bf16[224,64,256]{2,1,0:T(8,128)(2,1)} fusion(bf16[192,64,256]{2,1,0:T(8,128)(2,1)} %bitcast.40, s32[1024]{0:T(1024)S(1)} %pad_clamp_fusion.1), kind=kCustom, calls=%fused_computation.3 | custom fusion | bytes 14680960 | tf_op jit(solution)/shard_map/jit(_take)/gather | solution.py:232
  39.5 0.0 copy-done.5
  39.5 8.5 %shard_map.82 = f32[128,64,128]{2,1,0:T(8,128)} custom-call(s32[56]{0:T(128)} %broadcast_minimum_fusion.rows_ref, s32[224]{0:T(256)} %copy-done.5, s32[224]{0:T(256)} %gather_fusion, bf16[56,256,256]{2,1,0:T(8,128)(2,1)} %bitcast.36, bf16[4,8,64,128]{3,2,1,0:T(8,128)(2,1)} %shard_map.81.a_ref), custom_call_target="tpu_custom_call" | custom-call | tf_op jit(solution)/shard_map/pallas_call | solution.py:146
  48.0 6.6 %all-to-all-start.2 = ((f32[128,64,128]{2,1,0:T(8,128)}), f32[128,64,128]{2,1,0:T(8,128)}, u32[]{:S(2)}, u32[]{:S(2)}) async-start(f32[128,64,128]{2,1,0:T(8,128)} %shard_map.82), calls=%async_computation.2 | async-start | bytes 8388608 | tf_op jit(solution)/shard_map/all_to_all | solution.py:261
  54.6 0.0 all-gather.3.cloned.1.call-start
  54.6 0.0 copy-done.2
  54.6 0.7 convert_element_type.71
  55.3 0.0 all-gather.3.cloned.1.call-update
  55.3 0.0 reduce-scatter.3.cloned.1.call-start
  55.4 0.1 fusion.3
  55.5 0.1 broadcast_or_fusion
  55.6 0.1 reshape.247
  55.7 0.0 copy-done
  55.7 1.8 gather_fusion.2
  57.6 46.0 %all-to-all-done.2.arrived_ref = f32[128,64,128]{2,1,0:T(8,128)} async-done(((f32[128,64,128]{2,1,0:T(8,128)}), f32[128,64,128]{2,1,0:T(8,128)}, u32[]{:S(2)}, u32[]{:S(2)}) %all-to-all-start.2) | async-done | bytes 4194336 | tf_op jit(solution)/shard_map/all_to_all | solution.py:261
  103.6 5.6 %shard_map.83 = f32[8,8,64,128]{3,2,1,0:T(8,128)} custom-call(s32[128]{0:T(128)} %gather_fusion.2, f32[128,64,128]{2,1,0:T(8,128)} %all-to-all-done.2.arrived_ref), custom_call_target="tpu_custom_call" | custom-call | tf_op jit(solution)/shard_map/pallas_call | solution.py:165
  109.1 0.0 reduce-scatter.3.cloned.1.call-update
  109.2 0.1 add.205
  109.3 0.1 add.206
  109.4 0.4 copy-done.3
  109.8 0.0 all-gather.3.cloned.1.call-done
  109.9 2.2 gather_fusion.3
  112.1 1.7 broadcast_select_fusion
  113.7 4.4 %all-to-all-start = ((bf16[128,64,128]{2,1,0:T(8,128)(2,1)}), bf16[128,64,128]{2,1,0:T(8,128)(2,1)S(1)}, u32[]{:S(2)}, u32[]{:S(2)}) async-start(bf16[128,64,128]{2,1,0:T(8,128)(2,1)} %broadcast_select_fusion), calls=%async_computation | async-start | bytes 4194304 | tf_op jit(solution)/shard_map/all_to_all | solution.py:242
  118.1 29.1 %reduce-scatter.3.cloned.1.call-done = f32[1,8,64,128]{3,2,1,0:T(8,128)} async-done(((f32[8,8,64,128]{3,2,1,0:T(8,128)}), f32[1,8,64,128]{3,2,1,0:T(8,128)}) %reduce-scatter.3.cloned.1.call-update) | async-done | bytes 262160 | tf_op jit(solution)/shard_map/reduce_scatter | solution.py:265
  147.2 1.7 broadcast_multiply_fusion.1
  148.9 9.6 %shard_map.84.a_ref = bf16[4,8,64,128]{3,2,1,0:T(8,128)(2,1)} custom-call(bf16[1,8,64,128]{3,2,1,0:T(8,128)(2,1)} %get-tuple-element.6.x_ref), custom_call_target="tpu_custom_call" | custom-call | tf_op jit(solution)/shard_map/pallas_call | solution.py:130
  158.5 8.6 %shard_map.85 = f32[128,64,128]{2,1,0:T(8,128)} custom-call(s32[56]{0:T(128)} %broadcast_minimum_fusion.rows_ref, s32[224]{0:T(256)} %copy-done.5, s32[224]{0:T(256)} %gather_fusion, bf16[56,256,256]{2,1,0:T(8,128)(2,1)} %bitcast.37, bf16[4,8,64,128]{3,2,1,0:T(8,128)(2,1)} %shard_map.84.a_ref), custom_call_target="tpu_custom_call" | custom-call | tf_op jit(solution)/shard_map/pallas_call | solution.py:146
  167.0 0.0 all-to-all-done.x_ref
  167.1 1.3 copy-done.1
  168.3 10.3 %all-to-all-start.3 = ((f32[128,64,128]{2,1,0:T(8,128)}), f32[128,64,128]{2,1,0:T(8,128)}, u32[]{:S(2)}, u32[]{:S(2)}) async-start(f32[128,64,128]{2,1,0:T(8,128)} %shard_map.85), calls=%async_computation.4 | async-start | bytes 8388608 | tf_op jit(solution)/shard_map/all_to_all | solution.py:261
  178.6 0.0 all-gather.5.cloned.1.call-start
  178.7 8.1 %shard_map.77.x_ref = f32[4,8,64,128]{3,2,1,0:T(8,128)} custom-call(s32[56]{0:T(128)} %broadcast_minimum_fusion.rows_ref, s32[224]{0:T(256)} %copy-done.5, s32[224]{0:T(256)} %gather_fusion, bf16[56,256,256]{2,1,0:T(8,128)(2,1)} %bitcast.38, bf16[128,64,128]{2,1,0:T(8,128)(2,1)} %copy-done.1), custom_call_target="tpu_custom_call" | custom-call | tf_op jit(solution)/shard_map/pallas_call | solution.py:146
  186.7 16.9 %shard_map.78 = f32[8,64,128]{2,1,0:T(8,128)} custom-call(f32[4,8,64,128]{3,2,1,0:T(8,128)} %shard_map.77.x_ref), custom_call_target="tpu_custom_call" | custom-call | tf_op jit(solution)/shard_map/pallas_call | solution.py:130
  203.7 1.0 broadcast_multiply_fusion.3
  204.6 0.7 fusion.1
  205.3 0.0 all-gather.5.cloned.1.call-update
  205.4 0.0 reduce-scatter.5.cloned.1.call-start
  205.4 22.2 %all-to-all-done.3.arrived_ref = f32[128,64,128]{2,1,0:T(8,128)} async-done(((f32[128,64,128]{2,1,0:T(8,128)}), f32[128,64,128]{2,1,0:T(8,128)}, u32[]{:S(2)}, u32[]{:S(2)}) %all-to-all-start.3) | async-done | bytes 4194336 | tf_op jit(solution)/shard_map/all_to_all | solution.py:261
  227.6 5.7 %shard_map.86 = f32[8,8,64,128]{3,2,1,0:T(8,128)} custom-call(s32[128]{0:T(128)} %gather_fusion.2, f32[128,64,128]{2,1,0:T(8,128)} %all-to-all-done.3.arrived_ref), custom_call_target="tpu_custom_call" | custom-call | tf_op jit(solution)/shard_map/pallas_call | solution.py:165
  233.3 0.0 reduce-scatter.5.cloned.1.call-update
  233.3 5.4 %all-gather.5.cloned.1.call-done = bf16[64,64,128]{2,1,0:T(8,128)(2,1)} async-done(((bf16[8,64,128]{2,1,0:T(8,128)(2,1)}), bf16[64,64,128]{2,1,0:T(8,128)(2,1)}) %all-gather.5.cloned.1.call-update) | async-done | bytes 1048592 | tf_op jit(solution)/shard_map/all_gather | solution.py:240
  238.7 2.2 gather_fusion.4
  240.9 0.3 broadcast_select_fusion.1
  241.2 35.4 %all_to_all.20.x_ref = bf16[128,64,128]{2,1,0:T(8,128)(2,1)} all-to-all(bf16[128,64,128]{2,1,0:T(8,128)(2,1)S(1)} %broadcast_select_fusion.1), channel_id=1, replica_groups=mesh['z'=8,'x'=4,'c'=2,'edge'=4] {'x','c'}, dimensions={0} | all-to-all | bytes 4194304 | tf_op jit(solution)/shard_map/all_to_all | solution.py:242
  276.6 8.1 %shard_map.79.x_ref = f32[4,8,64,128]{3,2,1,0:T(8,128)} custom-call(s32[56]{0:T(128)} %broadcast_minimum_fusion.rows_ref, s32[224]{0:T(256)} %copy-done.5, s32[224]{0:T(256)} %gather_fusion, bf16[56,256,256]{2,1,0:T(8,128)(2,1)} %bitcast.39, bf16[128,64,128]{2,1,0:T(8,128)(2,1)} %all_to_all.20.x_ref), custom_call_target="tpu_custom_call" | custom-call | tf_op jit(solution)/shard_map/pallas_call | solution.py:146
  284.7 16.6 %shard_map.80 = f32[8,64,128]{2,1,0:T(8,128)} custom-call(f32[4,8,64,128]{3,2,1,0:T(8,128)} %shard_map.79.x_ref), custom_call_target="tpu_custom_call" | custom-call | tf_op jit(solution)/shard_map/pallas_call | solution.py:130
  301.3 1.0 broadcast_multiply_fusion.2
  302.3 0.7 bitcast_add_fusion.2
  303.0 1.0 broadcast_multiply_fusion
  304.0 0.7 bitcast_add_fusion
  (17 shorter events, 0.1 us)
Async XLA Ops:
  7.2 48.6 %copy-start = (s32[64,128]{1,0:T(8,128)S(1)}, s32[64,128]{1,0:T(8,128)}, u32[]{:S(2)}) copy-start(s32[64,128]{1,0:T(8,128)} %param.10) | copy-start | bytes 98308
  12.5 27.0 %copy-start.5 = (s32[224]{0:T(256)}, s32[224]{0:T(256)S(1)}, u32[]{:S(2)}) copy-start(s32[224]{0:T(256)S(1)} %scatter_custom_fusion.members_ref) | copy-start | bytes 2692
  48.0 6.6 %copy-start.2 = (f32[512,128]{1,0:T(8,128)S(1)}, f32[512,128]{1,0:T(8,128)}, u32[]{:S(2)}) copy-start(f32[512,128]{1,0:T(8,128)} %param.8) | copy-start | bytes 786436
  48.0 55.6 %all-to-all-start.2 = ((f32[128,64,128]{2,1,0:T(8,128)}), f32[128,64,128]{2,1,0:T(8,128)}, u32[]{:S(2)}, u32[]{:S(2)}) async-start(f32[128,64,128]{2,1,0:T(8,128)} %shard_map.82), calls=%async_computation.2 | async-start | bytes 8388608 | tf_op jit(solution)/shard_map/all_to_all | solution.py:261
  54.6 55.2 %all-gather.3.cloned.1.call-start = ((), (), s32[]{:S(2)}) async-start(), calls=%async_computation.6 | async-start | bytes 1179648 | tf_op jit(solution)/shard_map/all_gather | solution.py:240
  55.3 91.9 %reduce-scatter.3.cloned.1.call-start = ((), (), s32[]{:S(2)}) async-start(), calls=%async_computation.8 | async-start | bytes 2359296 | tf_op jit(solution)/shard_map/reduce_scatter | solution.py:265
  109.1 0.7 copy-start.3
  113.7 53.3 %all-to-all-start = ((bf16[128,64,128]{2,1,0:T(8,128)(2,1)}), bf16[128,64,128]{2,1,0:T(8,128)(2,1)S(1)}, u32[]{:S(2)}, u32[]{:S(2)}) async-start(bf16[128,64,128]{2,1,0:T(8,128)(2,1)} %broadcast_select_fusion), calls=%async_computation | async-start | bytes 4194304 | tf_op jit(solution)/shard_map/all_to_all | solution.py:242
  167.0 1.3 copy-start.1
  168.3 59.2 %all-to-all-start.3 = ((f32[128,64,128]{2,1,0:T(8,128)}), f32[128,64,128]{2,1,0:T(8,128)}, u32[]{:S(2)}, u32[]{:S(2)}) async-start(f32[128,64,128]{2,1,0:T(8,128)} %shard_map.85), calls=%async_computation.4 | async-start | bytes 8388608 | tf_op jit(solution)/shard_map/all_to_all | solution.py:261
  178.6 60.1 %all-gather.5.cloned.1.call-start = ((), (), s32[]{:S(2)}) async-start(), calls=%async_computation.7 | async-start | bytes 1179648 | tf_op jit(solution)/shard_map/all_gather | solution.py:240
  205.4 97.7 %reduce-scatter.5.cloned.1.call-start = ((), (), s32[]{:S(2)}) async-start(), calls=%async_computation.9 | async-start | bytes 2359296 | tf_op jit(solution)/shard_map/reduce_scatter | solution.py:265
  284.7 19.3 %copy-start.4 = (f32[512,128]{1,0:T(8,128)S(1)}, f32[512,128]{1,0:T(8,128)}, u32[]{:S(2)}) copy-start(f32[512,128]{1,0:T(8,128)} %param.9) | copy-start | bytes 786436
Sparse Core Ops, SparseCore 0:
  57.8 36.7 all-gather.2
  109.3 37.8 reduce-scatter.2
  205.5 33.1 all-gather.4
  241.1 40.7 reduce-scatter.4
